TPU v7x, 32 devices: a whole 2x2x4 slice. The times are simulated.
32 devices in a mesh: seq: 8 (over z, y), head: 4 (over x, core).
Axes of the slice: x: 2, y: 2, z: 4, core: 2. Of those that a mesh axis runs over, the one named last changes fastest.
Arguments:
- tokens: bfloat16 [2048, 1024], P('seq'), may hold values from -6 to 6
- w_qkv: bfloat16 [1024, 3, 1024], P('seq', None, 'head'), may hold values from -0.1875 to 0.1875
- w_out: bfloat16 [1024, 1024], P('head', 'seq'), may hold values from -1 to 1
- ln1_gain: bfloat16 [1024], P('seq'), may hold values from 0.5 to 1.5
- ln1_bias: bfloat16 [1024], P('seq'), may hold values from -1.796875 to 1.796875
- ln2_gain: bfloat16 [1024], P('seq'), may hold values from 0.5 to 1.5
- ln2_bias: bfloat16 [1024], P('seq'), may hold values from -1.796875 to 1.796875
- w_up: bfloat16 [1024, 4096], P('seq', 'head'), may hold values from -0.1875 to 0.1875
- up_bias: bfloat16 [4096], P('head'), may hold values from -1.796875 to 1.796875
- w_down: bfloat16 [4096, 1024], P('head', 'seq'), may hold values from -0.09375 to 0.09375
- down_bias: bfloat16 [1024], P('seq'), may hold values from -1.796875 to 1.796875
- seq_units: int32 [4], replicated, may hold values from 1 to 4, 8 in all
- seq_pad: int32 [4], replicated, may hold values from 0 to 127
- rand_picks: int32 [32, 16, 3], P('seq', 'head'), may hold values from 0 to 65535
- cotangent: bfloat16 [2048, 1024], P('seq'), may hold values from -6 to 6
Outputs:
- output: bfloat16 [2048, 1024], P('seq')
- x_grad: float32 [2048, 1024], P('seq')
- w_qkv_grad: float32 [1024, 3, 1024], P('seq', None, 'head')
- w_out_grad: float32 [1024, 1024], P('head', 'seq')
- ln1_gain_grad: float32 [1024], P('seq')
- ln1_bias_grad: float32 [1024], P('seq')
- ln2_gain_grad: float32 [1024], P('seq')
- ln2_bias_grad: float32 [1024], P('seq')
- w_up_grad: float32 [1024, 4096], P('seq', 'head')
- up_bias_grad: float32 [4096], P('head')
- w_down_grad: float32 [4096, 1024], P('head', 'seq')
- down_bias_grad: float32 [1024], P('seq')
Inputs may be any that keep to these rules, and one draw needn't show every extreme that they name: `seq_units`: each sequence covers whole units; the values add up to the number of units in the stream, and some sequence covers 4 units.
All inputs are finite; a program needn't handle non-finite values.
Results may differ from a plain program's by a relative error of at most 0.012.
Values may be sent and summed in bfloat16 or wider, within the bound.
A program may use at most 128 MiB of HBM per device.

v0:
```python
import jax
import jax.numpy as jnp
from jax import lax
from jax.sharding import PartitionSpec as P

HEAD_DIM = 64
BLK = 64
SPAN = 4
BLK_DEV = 4


EPSILON = 1e-05
NEGATIVE = -1e30


def passed_along(value, axis, steps):
    count = lax.axis_size(axis)
    leading, last = (max(0, -steps), min(count, count - steps))
    return lax.ppermute(value, axis, [(source, source + steps) for source in range(leading, last)])


def layer_norm(features, norm_gain, norm_shift):
    average = jnp.mean(features, axis=-1, keepdims=True)
    centred = features - average
    spread = jnp.mean(centred * centred, axis=-1, keepdims=True)
    return centred * lax.rsqrt(spread + EPSILON) * norm_gain + norm_shift


def gelu_tanh(values):
    return jax.nn.gelu(values, approximate=True)


def gather_rows(w_qkv, w_up, ln1_gain, ln1_bias, ln2_gain, ln2_bias, down_bias):
    return (
        lax.all_gather(w_qkv, "seq", axis=0, tiled=True),
        lax.all_gather(w_up, "seq", axis=0, tiled=True),
        lax.all_gather(ln1_gain, "seq", axis=0, tiled=True),
        lax.all_gather(ln1_bias, "seq", axis=0, tiled=True),
        lax.all_gather(ln2_gain, "seq", axis=0, tiled=True),
        lax.all_gather(ln2_bias, "seq", axis=0, tiled=True),
        lax.all_gather(down_bias, "seq", axis=0, tiled=True),
    )


def gather_columns(w_out, w_down):
    return (
        lax.all_gather(w_out, "seq", axis=1, tiled=True),
        lax.all_gather(w_down, "seq", axis=1, tiled=True),
    )


def sequence_layout(seq_units, seq_pad, tok_dev):
    device = lax.axis_index("seq")
    seq_count = seq_units.shape[0]
    starts = jnp.cumsum(seq_units) - seq_units
    member = jnp.sum((starts <= device).astype(jnp.int32)) - 1
    pick_one = (jnp.arange(seq_count, dtype=jnp.int32) == member).astype(jnp.int32)
    leader = jnp.sum(pick_one * starts)
    span_dev = jnp.sum(pick_one * seq_units)
    padding = jnp.sum(pick_one * seq_pad)
    position = device - leader
    offsets = jnp.arange(2 * SPAN - 1, dtype=jnp.int32) - (SPAN - 1)
    relative = position + offsets
    inside = (relative >= 0) & (relative < span_dev)
    places = relative[:, None] * tok_dev + jnp.arange(tok_dev, dtype=jnp.int32)[None, :]
    usable = inside[:, None] & (places < span_dev * tok_dev - padding)
    return (position, span_dev, usable.reshape((2 * SPAN - 1) * BLK_DEV, BLK))


def key_blocks(position, span_dev, picked_raw, local_heads):
    root_block = (SPAN - 1 - position) * BLK_DEV
    query_blocks = position * BLK_DEV + jnp.arange(BLK_DEV, dtype=jnp.int32)
    window = query_blocks[:, None] + jnp.arange(3, dtype=jnp.int32)[None, :] - 1 + root_block
    anchors = jnp.stack([root_block, root_block + span_dev * BLK_DEV - 1])
    chosen = picked_raw % (span_dev * BLK_DEV) + root_block
    window = jnp.broadcast_to(window[:, None, :], (BLK_DEV, local_heads, 3))
    anchors = jnp.broadcast_to(anchors[None, None, :], (BLK_DEV, local_heads, 2))
    return jnp.concatenate([window, anchors, chosen], axis=-1)


def project_inputs(inputs, qkv_full, gain_one, shift_one):
    normed = layer_norm(inputs, gain_one.astype(jnp.float32), shift_one.astype(jnp.float32)).astype(
        jnp.bfloat16
    )
    triple = jnp.einsum("td,dcf->tcf", normed, qkv_full, preferred_element_type=jnp.float32).astype(
        jnp.bfloat16
    )
    return (normed, triple)


def near_blocks(triple, local_heads):
    key_part = triple[:, 1].reshape(BLK_DEV, BLK, local_heads, HEAD_DIM)
    value_part = triple[:, 2].reshape(BLK_DEV, BLK, local_heads, HEAD_DIM)
    own_tiles = jnp.transpose(jnp.concatenate([key_part, value_part], axis=-1), (0, 2, 1, 3))
    pieces = []
    for offset in range(1 - SPAN, SPAN):
        if offset == 0:
            pieces.append(own_tiles)
        else:
            pieces.append(passed_along(own_tiles, "seq", -offset))
    return jnp.concatenate(pieces, axis=0)


def log_total(logits, over_axes):
    row_max = jnp.max(logits, axis=over_axes, keepdims=True)
    return row_max + jnp.log(jnp.sum(jnp.exp(logits - row_max), axis=over_axes, keepdims=True))


def sparse_logits(queries, picked, picked_usable, scaling):
    logits = (
        jnp.einsum(
            "bqhd,bhrkd->bhqrk", queries, picked[..., :HEAD_DIM], preferred_element_type=jnp.float32
        )
        * scaling
    )
    return jnp.where(picked_usable[:, :, None], logits, NEGATIVE)


def global_logits(edge_queries, seq_tiles, seq_usable, scaling):
    logits = (
        jnp.einsum(
            "qhd,nhkd->hqnk",
            edge_queries,
            seq_tiles[..., :HEAD_DIM],
            preferred_element_type=jnp.float32,
        )
        * scaling
    )
    return jnp.where(seq_usable[None, None], logits, NEGATIVE)


def sequence_tiles(nearby, usable, position):
    root_block = (SPAN - 1 - position) * BLK_DEV
    seq_tiles = lax.dynamic_slice_in_dim(nearby, root_block, SPAN * BLK_DEV, 0)
    seq_usable = lax.dynamic_slice_in_dim(usable, root_block, SPAN * BLK_DEV, 0)
    return (root_block, seq_tiles, seq_usable)


def edge_rows(queries):
    return jnp.concatenate([queries[0], queries[BLK_DEV - 1]], axis=0)


def attend_forward(queries, nearby, usable, indices, position, span_dev, scaling):
    local_heads = nearby.shape[1]
    tok_dev = BLK_DEV * BLK
    head_ids = jnp.arange(local_heads, dtype=jnp.int32)[None, :, None]
    picked = nearby[indices, head_ids]
    logits = sparse_logits(queries, picked, usable[indices], scaling)
    sparse_total = log_total(logits, (3, 4))
    chances = jnp.exp(logits - sparse_total).astype(jnp.bfloat16)
    sparse_out = jnp.einsum(
        "bhqrk,bhrkd->bqhd", chances, picked[..., HEAD_DIM:], preferred_element_type=jnp.float32
    )
    root_block, seq_tiles, seq_usable = sequence_tiles(nearby, usable, position)
    lead_logits = global_logits(edge_rows(queries), seq_tiles, seq_usable, scaling)
    lead_total = log_total(lead_logits, (2, 3))
    lead_chances = jnp.exp(lead_logits - lead_total).astype(jnp.bfloat16)
    lead_out = jnp.einsum(
        "hqnk,nhkd->qhd",
        lead_chances,
        seq_tiles[..., HEAD_DIM:],
        preferred_element_type=jnp.float32,
    )
    merged = sparse_out.reshape(tok_dev, local_heads, HEAD_DIM)
    first_rows = jnp.where(position == 0, lead_out[:BLK], merged[:BLK])
    last_rows = jnp.where(position == span_dev - 1, lead_out[BLK:], merged[tok_dev - BLK :])
    return (
        jnp.concatenate([first_rows, merged[BLK : tok_dev - BLK], last_rows], axis=0),
        sparse_total,
        lead_total,
    )


def attend_backward(
    queries,
    nearby,
    usable,
    indices,
    position,
    span_dev,
    scaling,
    sparse_total,
    lead_total,
    grad_out,
):
    local_heads = nearby.shape[1]
    tok_dev = BLK_DEV * BLK
    head_ids = jnp.arange(local_heads, dtype=jnp.int32)[None, :, None]
    is_first = position == 0
    is_last = position == span_dev - 1
    row_ids = jnp.arange(tok_dev, dtype=jnp.int32)
    keep_rows = jnp.logical_not(is_first & (row_ids < BLK) | is_last & (row_ids >= tok_dev - BLK))
    zeros_low = jnp.zeros_like(grad_out)
    sparse_grad = jnp.where(keep_rows[:, None, None], grad_out, zeros_low).reshape(
        BLK_DEV, BLK, local_heads, HEAD_DIM
    )
    lead_grad = jnp.concatenate(
        [
            jnp.where(is_first, grad_out[:BLK], zeros_low[:BLK]),
            jnp.where(is_last, grad_out[tok_dev - BLK :], zeros_low[:BLK]),
        ],
        axis=0,
    )
    picked = nearby[indices, head_ids]
    logits = sparse_logits(queries, picked, usable[indices], scaling)
    chances = jnp.exp(logits - sparse_total)
    grad_prob = jnp.einsum(
        "bqhd,bhrkd->bhqrk", sparse_grad, picked[..., HEAD_DIM:], preferred_element_type=jnp.float32
    )
    inner_sum = jnp.sum(chances * grad_prob, axis=(3, 4), keepdims=True)
    grad_logit = (chances * (grad_prob - inner_sum)).astype(jnp.bfloat16)
    grad_queries = scaling * jnp.einsum(
        "bhqrk,bhrkd->bqhd", grad_logit, picked[..., :HEAD_DIM], preferred_element_type=jnp.float32
    )
    grad_keys = scaling * jnp.einsum(
        "bhqrk,bqhd->bhrkd", grad_logit, queries, preferred_element_type=jnp.float32
    )
    grad_values = jnp.einsum(
        "bhqrk,bqhd->bhrkd",
        chances.astype(jnp.bfloat16),
        sparse_grad,
        preferred_element_type=jnp.float32,
    )
    grad_near = (
        jnp.zeros(nearby.shape, jnp.float32)
        .at[indices, head_ids]
        .add(jnp.concatenate([grad_keys, grad_values], axis=-1))
    )
    root_block, seq_tiles, seq_usable = sequence_tiles(nearby, usable, position)
    edge_queries = edge_rows(queries)
    lead_logits = global_logits(edge_queries, seq_tiles, seq_usable, scaling)
    lead_chances = jnp.exp(lead_logits - lead_total)
    lead_prob = jnp.einsum(
        "qhd,nhkd->hqnk", lead_grad, seq_tiles[..., HEAD_DIM:], preferred_element_type=jnp.float32
    )
    lead_inner = jnp.sum(lead_chances * lead_prob, axis=(2, 3), keepdims=True)
    lead_logit = (lead_chances * (lead_prob - lead_inner)).astype(jnp.bfloat16)
    lead_queries = scaling * jnp.einsum(
        "hqnk,nhkd->qhd", lead_logit, seq_tiles[..., :HEAD_DIM], preferred_element_type=jnp.float32
    )
    lead_keys = scaling * jnp.einsum(
        "hqnk,qhd->nhkd", lead_logit, edge_queries, preferred_element_type=jnp.float32
    )
    lead_values = jnp.einsum(
        "hqnk,qhd->nhkd",
        lead_chances.astype(jnp.bfloat16),
        lead_grad,
        preferred_element_type=jnp.float32,
    )
    segment = lax.dynamic_slice_in_dim(grad_near, root_block, SPAN * BLK_DEV, 0)
    segment = segment + jnp.concatenate([lead_keys, lead_values], axis=-1)
    grad_near = lax.dynamic_update_slice_in_dim(grad_near, segment, root_block, 0)
    grad_queries = grad_queries.reshape(tok_dev, local_heads, HEAD_DIM)
    grad_queries = jnp.concatenate(
        [
            grad_queries[:BLK] + lead_queries[:BLK],
            grad_queries[BLK : tok_dev - BLK],
            grad_queries[tok_dev - BLK :] + lead_queries[BLK:],
        ],
        axis=0,
    )
    return (grad_queries, grad_near)


def return_blocks(grad_near):
    blocks = grad_near.reshape((2 * SPAN - 1, BLK_DEV) + grad_near.shape[1:])
    owned_grad = blocks[SPAN - 1]
    for offset in range(1 - SPAN, SPAN):
        if offset != 0:
            owned_grad = owned_grad + passed_along(blocks[offset + SPAN - 1], "seq", offset)
    return owned_grad


def local(
    tokens,
    w_qkv,
    w_out,
    ln1_gain,
    ln1_bias,
    ln2_gain,
    ln2_bias,
    w_up,
    up_bias,
    w_down,
    down_bias,
    seq_units,
    seq_pad,
    rand_picks,
    cotangent,
):
    tok_dev = tokens.shape[0]
    local_heads = w_qkv.shape[2] // HEAD_DIM
    scaling = HEAD_DIM ** (-0.5)
    rows_full = gather_rows(w_qkv, w_up, ln1_gain, ln1_bias, ln2_gain, ln2_bias, down_bias)
    cols_full = gather_columns(w_out, w_down)
    qkv_full, up_full, gain_one, shift_one, gain_two, shift_two, down_shift = rows_full
    out_full, down_full = cols_full
    position, span_dev, usable = sequence_layout(seq_units, seq_pad, tok_dev)
    indices = key_blocks(position, span_dev, rand_picks, local_heads)
    inputs = tokens.astype(jnp.float32)
    normed, triple = project_inputs(inputs, qkv_full, gain_one, shift_one)
    nearby = near_blocks(triple, local_heads)
    queries = triple[:, 0].reshape(BLK_DEV, BLK, local_heads, HEAD_DIM)
    attended, sparse_total, lead_total = attend_forward(
        queries, nearby, usable, indices, position, span_dev, scaling
    )
    attended = attended.astype(jnp.bfloat16).reshape(tok_dev, local_heads * HEAD_DIM)
    branch = lax.psum(jnp.dot(attended, out_full, preferred_element_type=jnp.float32), "head")
    middle = inputs + branch
    gain_two_f = gain_two.astype(jnp.float32)
    shift_two_f = shift_two.astype(jnp.float32)
    normed_two = layer_norm(middle, gain_two_f, shift_two_f).astype(jnp.bfloat16)
    pre_act = jnp.dot(normed_two, up_full, preferred_element_type=jnp.float32) + up_bias.astype(
        jnp.float32
    )
    hidden = gelu_tanh(pre_act).astype(jnp.bfloat16)
    ffn_part = lax.psum(
        jnp.dot(hidden, down_full, preferred_element_type=jnp.float32).astype(jnp.bfloat16), "head"
    ).astype(jnp.float32)
    output = (middle + ffn_part + down_shift.astype(jnp.float32)).astype(jnp.bfloat16)
    rows_back = gather_rows(w_qkv, w_up, ln1_gain, ln1_bias, ln2_gain, ln2_bias, down_bias)
    cols_back = gather_columns(w_out, w_down)
    (
        qkv_back,
        up_back,
        gain_one_back,
        shift_one_back,
        gain_two_back,
        shift_two_back,
        unused_shift,
    ) = rows_back
    out_back, down_back = cols_back
    grad_output = cotangent.astype(jnp.float32)
    normed_two = layer_norm(
        middle, gain_two_back.astype(jnp.float32), shift_two_back.astype(jnp.float32)
    ).astype(jnp.bfloat16)
    pre_act = jnp.dot(normed_two, up_back, preferred_element_type=jnp.float32) + up_bias.astype(
        jnp.float32
    )
    hidden_pair = jax.vjp(gelu_tanh, pre_act)
    hidden = hidden_pair[0].astype(jnp.bfloat16)
    grad_down_bias = jnp.sum(grad_output, axis=0)
    grad_w_down = jnp.einsum("tf,td->fd", hidden, cotangent, preferred_element_type=jnp.float32)
    grad_hidden = jnp.einsum("td,fd->tf", cotangent, down_back, preferred_element_type=jnp.float32)
    grad_pre = hidden_pair[1](grad_hidden)[0].astype(jnp.bfloat16)
    grad_up_bias = jnp.sum(grad_pre.astype(jnp.float32), axis=0)
    grad_w_up = jnp.einsum("td,tf->df", normed_two, grad_pre, preferred_element_type=jnp.float32)
    grad_normed_two = lax.psum(
        jnp.einsum("tf,df->td", grad_pre, up_back, preferred_element_type=jnp.float32), "head"
    )
    norm_two_pair = jax.vjp(
        layer_norm, middle, gain_two_back.astype(jnp.float32), shift_two_back.astype(jnp.float32)
    )
    grad_mid_norm, grad_gain_two, grad_shift_two = norm_two_pair[1](grad_normed_two)
    grad_middle = grad_output + grad_mid_norm
    grad_branch = grad_middle.astype(jnp.bfloat16)
    grad_w_out = jnp.einsum("tf,td->fd", attended, grad_branch, preferred_element_type=jnp.float32)
    grad_attended = jnp.einsum(
        "td,fd->tf", grad_branch, out_back, preferred_element_type=jnp.float32
    ).astype(jnp.bfloat16)
    grad_attended = grad_attended.reshape(tok_dev, local_heads, HEAD_DIM)
    normed, triple = project_inputs(inputs, qkv_back, gain_one_back, shift_one_back)
    nearby = near_blocks(triple, local_heads)
    queries = triple[:, 0].reshape(BLK_DEV, BLK, local_heads, HEAD_DIM)
    grad_queries, grad_near = attend_backward(
        queries,
        nearby,
        usable,
        indices,
        position,
        span_dev,
        scaling,
        sparse_total,
        lead_total,
        grad_attended,
    )
    owned_grad = jnp.transpose(return_blocks(grad_near).astype(jnp.bfloat16), (0, 2, 1, 3))
    grad_keys = owned_grad[..., :HEAD_DIM].reshape(tok_dev, local_heads * HEAD_DIM)
    grad_values = owned_grad[..., HEAD_DIM:].reshape(tok_dev, local_heads * HEAD_DIM)
    grad_triple = jnp.stack(
        [
            grad_queries.astype(jnp.bfloat16).reshape(tok_dev, local_heads * HEAD_DIM),
            grad_keys,
            grad_values,
        ],
        axis=1,
    )
    grad_w_qkv = jnp.einsum("td,tcf->dcf", normed, grad_triple, preferred_element_type=jnp.float32)
    grad_normed = lax.psum(
        jnp.einsum("tcf,dcf->td", grad_triple, qkv_back, preferred_element_type=jnp.float32), "head"
    )
    norm_one_pair = jax.vjp(
        layer_norm, inputs, gain_one_back.astype(jnp.float32), shift_one_back.astype(jnp.float32)
    )
    grad_in_norm, grad_gain_one, grad_shift_one = norm_one_pair[1](grad_normed)
    x_grad = grad_middle + grad_in_norm
    row_grads = (
        lax.psum_scatter(grad_w_qkv, "seq", scatter_dimension=0, tiled=True),
        lax.psum_scatter(grad_w_up, "seq", scatter_dimension=0, tiled=True),
        lax.psum_scatter(grad_gain_one, "seq", scatter_dimension=0, tiled=True),
        lax.psum_scatter(grad_shift_one, "seq", scatter_dimension=0, tiled=True),
        lax.psum_scatter(grad_gain_two, "seq", scatter_dimension=0, tiled=True),
        lax.psum_scatter(grad_shift_two, "seq", scatter_dimension=0, tiled=True),
        lax.psum_scatter(grad_down_bias, "seq", scatter_dimension=0, tiled=True),
    )
    col_grads = (
        lax.psum_scatter(grad_w_out, "seq", scatter_dimension=1, tiled=True),
        lax.psum_scatter(grad_w_down, "seq", scatter_dimension=1, tiled=True),
    )
    up_bias_grad = lax.psum(grad_up_bias, "seq")
    return (
        output,
        x_grad,
        row_grads[0],
        col_grads[0],
        row_grads[2],
        row_grads[3],
        row_grads[4],
        row_grads[5],
        row_grads[1],
        up_bias_grad,
        col_grads[1],
        row_grads[6],
    )


def solution(mesh):
    in_specs = (
        P("seq", None),
        P("seq", None, "head"),
        P("head", "seq"),
        P("seq"),
        P("seq"),
        P("seq"),
        P("seq"),
        P("seq", "head"),
        P("head"),
        P("head", "seq"),
        P("seq"),
        P(),
        P(),
        P("seq", "head", None),
        P("seq", None),
    )
    out_specs = (
        P("seq", None),
        P("seq", None),
        P("seq", None, "head"),
        P("head", "seq"),
        P("seq"),
        P("seq"),
        P("seq"),
        P("seq"),
        P("seq", "head"),
        P("head"),
        P("head", "seq"),
        P("seq"),
    )
    return jax.shard_map(local, mesh=mesh, in_specs=in_specs, out_specs=out_specs, check_vma=False)
```

profile of v0, /device:TPU:0, one launch (start us, length us, event | category | flops | bytes accessed | tf_op | source)
XLA Modules:
  0.0 856.5 jit_solution(14368563780889970232)
XLA Ops:
  13.4 22.3 %all-gather = bf16[8,1,128]{2,1,0:T(2,128)(2,1)S(1)} all-gather(bf16[1,1,128]{2,1,0:T(2,128)(2,1)} %bitcast.210), channel_id=1, replica_groups=mesh['seq'=8,'head'=4] {'seq'}, dimensions={0}, use_global_device_ids=true | all-gather | bytes 2304 | tf_op jit(solution)/shard_map/all_gather | solution.py:37
  35.7 16.5 %all-gather.1 = bf16[8,1,128]{2,1,0:T(2,128)(2,1)S(1)} all-gather(bf16[1,1,128]{2,1,0:T(2,128)(2,1)} %bitcast.211), channel_id=1, replica_groups=mesh['seq'=8,'head'=4] {'seq'}, dimensions={0}, use_global_device_ids=true | all-gather | bytes 2304 | tf_op jit(solution)/shard_map/all_gather | solution.py:38
  59.1 28.9 %all_gather.38 = bf16[256,1024]{1,0:T(8,128)(2,1)} all-gather(bf16[256,128]{1,0:T(8,128)(2,1)} %param.17), channel_id=1, replica_groups=mesh['seq'=8,'head'=4] {'seq'}, dimensions={1}, use_global_device_ids=true | all-gather | bytes 589824 | tf_op jit(solution)/shard_map/all_gather | solution.py:47
  88.1 2.1 convolution_convert_fusion.1
  90.8 3.9 collective-permute-start
  96.3 3.3 collective-permute-start.1
  99.5 5.4 collective-permute-start.2
  109.5 3.7 collective-permute-done.3
  113.3 2.2 collective-permute-done.4
  115.5 3.9 collective-permute-done.5
  121.0 4.1 gather_fusion
  125.1 3.3 fusion
  128.5 1.7 exponential_reduce_fusion
  131.6 4.3 fusion.15
  137.6 2.3 fusion.76
  141.4 20.3 %all-gather.2 = bf16[8,1,128]{2,1,0:T(2,128)(2,1)S(1)} all-gather(bf16[1,1,128]{2,1,0:T(2,128)(2,1)S(1)} %bitcast.212), channel_id=1, replica_groups=mesh['seq'=8,'head'=4] {'seq'}, dimensions={0}, use_global_device_ids=true | all-gather | bytes 2304 | tf_op jit(solution)/shard_map/all_gather | solution.py:39
  161.7 16.2 %all-gather.3 = bf16[8,1,128]{2,1,0:T(2,128)(2,1)S(1)} all-gather(bf16[1,1,128]{2,1,0:T(2,128)(2,1)S(1)} %bitcast.213), channel_id=1, replica_groups=mesh['seq'=8,'head'=4] {'seq'}, dimensions={0}, use_global_device_ids=true | all-gather | bytes 2304 | tf_op jit(solution)/shard_map/all_gather | solution.py:40
  177.9 1.5 fusion.114
  179.7 51.0 %all-gather.13.cloned.1.call-done = bf16[1024,1024]{1,0:T(8,128)(2,1)} async-done(((bf16[1024,128]{1,0:T(8,128)(2,1)}), bf16[1024,1024]{1,0:T(8,128)(2,1)}) %all-gather.13.cloned.1.call-update) | async-done | bytes 2097168 | tf_op jit(solution)/shard_map/all_gather | solution.py:48
  230.8 3.5 fusion.120
  234.3 46.2 %all-gather.11.cloned.1.call-done = bf16[1024,1024]{1,0:T(8,128)(2,1)} async-done(((bf16[128,1024]{1,0:T(8,128)(2,1)}), bf16[1024,1024]{1,0:T(8,128)(2,1)}) %all-gather.11.cloned.1.call-update) | async-done | bytes 2097168 | tf_op jit(solution)/shard_map/all_gather | solution.py:36
  280.5 5.0 convert_reduce_fusion.2
  286.3 1.7 fusion.121
  288.1 18.1 %all-gather.4 = bf16[8,1,128]{2,1,0:T(2,128)(2,1)S(1)} all-gather(bf16[1,1,128]{2,1,0:T(2,128)(2,1)S(1)} %bitcast.214), channel_id=1, replica_groups=mesh['seq'=8,'head'=4] {'seq'}, dimensions={0}, use_global_device_ids=true | all-gather | bytes 2304 | tf_op jit(solution)/shard_map/all_gather | solution.py:41
  307.0 3.5 convolution_convert_fusion
  310.6 12.2 %all-reduce.15.cloned.1.call-done = f32[256,1024]{1,0:T(8,128)} async-done(((f32[256,1024]{1,0:T(8,128)}), f32[256,1024]{1,0:T(8,128)}) %all-reduce.15.cloned.1.call-update) | async-done | bytes 1048592 | tf_op jit(solution)/shard_map/psum | solution.py:348
  322.9 2.2 multiply_reduce_fusion.2
  325.0 34.2 %all-reduce.13.cloned.1.call-done = bf16[256,1024]{1,0:T(8,128)(2,1)} async-done(((bf16[256,1024]{1,0:T(8,128)(2,1)}), bf16[256,1024]{1,0:T(8,128)(2,1)}) %all-reduce.13.cloned.1.call-update) | async-done | bytes 524304 | tf_op jit(solution)/shard_map/psum | solution.py:317
  359.2 2.6 fusion.113
  364.9 6.0 multiply_reduce_fusion
  371.0 3.6 fusion.57
  374.8 1.9 multiply_reduce_fusion.1
  378.2 1.5 multiply_bitcast_fusion
  379.6 1.9 fusion.84
  381.5 1.6 copy-done.2
  383.1 1.9 multiply_convert_fusion
  385.7 1.5 copy-done.10
  387.2 3.1 pad_maximum_fusion
  390.3 2.3 broadcast_in_dim.66
  392.6 21.4 %scatter_fusion = f32[28,4,64,128]{3,2,1,0:T(8,128)} fusion(f32[28,4,64,128]{3,2,1,0:T(8,128)} %broadcast_in_dim.66, s32[128]{0:T(128)S(1)} %reshape.390, f32[128,64,128]{2,1,0:T(8,128)} %bitcast.160), kind=kCustom, calls=%fused_computation.2 | custom fusion | flops 1048576 | bytes 12583936 | tf_op jit(solution)/shard_map/scatter-add | solution.py:227
  413.9 1.9 constant_dynamic-slice_fusion
  416.6 2.8 copy_dynamic-update-slice_fusion
  419.4 1.5 fusion.115
  422.2 3.4 collective-permute-start.10
  425.6 4.9 collective-permute-start.11
  434.4 3.5 collective-permute-done.10
  438.8 4.4 collective-permute-start.9
  445.2 9.3 %collective-permute-done.11 = f32[4,4,64,128]{3,2,1,0:T(8,128)} collective-permute-done((f32[4,4,64,128]{3,2,1,0:T(8,128)}, f32[4,4,64,128]{3,2,1,0:T(8,128)}, u32[]{:S(2)}, u32[]{:S(2)}) %collective-permute-start.11) | collective-permute-done | bytes 524320 | tf_op jit(solution)/shard_map/ppermute | solution.py:19
  454.5 5.4 collective-permute-done.7
  459.9 11.6 %collective-permute-done.9 = f32[4,4,64,128]{3,2,1,0:T(8,128)} collective-permute-done((f32[4,4,64,128]{3,2,1,0:T(8,128)}, f32[4,4,64,128]{3,2,1,0:T(8,128)}, u32[]{:S(2)}, u32[]{:S(2)}) %collective-permute-start.9) | collective-permute-done | bytes 524320 | tf_op jit(solution)/shard_map/ppermute | solution.py:19
  471.5 2.2 fusion.56
  474.7 3.0 convolution_bitcast_fusion
  479.3 2.4 fusion.62
  482.8 2.8 fusion.110
  487.0 2.9 fusion.108
  491.8 26.9 %all-reduce.17.cloned.1.call-done = f32[256,1024]{1,0:T(8,128)} async-done(((f32[256,1024]{1,0:T(8,128)}), f32[256,1024]{1,0:T(8,128)}) %all-reduce.17.cloned.1.call-update) | async-done | bytes 1048592 | tf_op jit(solution)/shard_map/psum | solution.py:389
  518.7 1.6 fusion.111
  520.4 1.8 fusion.33
  522.2 1.5 convert_reduce_fusion.1
  523.7 37.8 %all-reduce.5 = (f32[1024]{0:T(1024)S(1)}, f32[1024]{0:T(1024)S(1)}, f32[1024]{0:T(1024)S(1)}, f32[1024]{0:T(1024)S(1)}, f32[1024]{0:T(1024)}, /*index=5*/f32[1024]{0:T(1024)S(1)}) all-reduce(f32[1024]{0:T(1024)S(1)} %get-tuple-element.14, f32[1024]{0:T(1024)S(1)} %get-tuple-element.17, ...), channel_id=4, replica_groups=mesh['seq'=8,'head'=4] {'seq'}, use_global_device_ids=true, to_apply=%region_27.28.clone | all-reduce | flops 6144 | bytes 49152
  564.5 23.0 %reduce-scatter.7.cloned.1.call-done = f32[256,128]{1,0:T(8,128)} async-done(((f32[256,1024]{1,0:T(8,128)}), f32[256,128]{1,0:T(8,128)}) %reduce-scatter.7.cloned.1.call-update) | async-done | bytes 131088 | tf_op jit(solution)/shard_map/reduce_scatter | solution.py:407
  587.4 78.3 %reduce-scatter.5.cloned.1.call-done = f32[128,3,256]{2,0,1:T(8,128)} async-done(((f32[1024,3,256]{2,0,1:T(8,128)}), f32[128,3,256]{2,0,1:T(8,128)}) %reduce-scatter.5.cloned.1.call-update) | async-done | bytes 393232 | tf_op jit(solution)/shard_map/reduce_scatter | solution.py:398
  665.7 91.3 %reduce-scatter.9.cloned.1.call-done = f32[128,1024]{1,0:T(8,128)} async-done(((f32[1024,1024]{1,0:T(8,128)}), f32[128,1024]{1,0:T(8,128)}) %reduce-scatter.9.cloned.1.call-update) | async-done | bytes 524304 | tf_op jit(solution)/shard_map/reduce_scatter | solution.py:399
  757.1 92.9 %reduce-scatter.11.cloned.1.call-done = f32[1024,128]{1,0:T(8,128)} async-done(((f32[1024,1024]{1,0:T(8,128)}), f32[1024,128]{1,0:T(8,128)}) %reduce-scatter.11.cloned.1.call-update) | async-done | bytes 524304 | tf_op jit(solution)/shard_map/reduce_scatter | solution.py:408
  (292 shorter events, 46.6 us)
Async XLA Ops:
  7.2 80.9 %copy-start.5 = (bf16[256,1024]{1,0:T(8,128)(2,1)S(1)}, bf16[256,1024]{1,0:T(8,128)(2,1)}, u32[]{:S(2)}) copy-start(bf16[256,1024]{1,0:T(8,128)(2,1)} %param.15) | copy-start | bytes 1572868
  7.2 80.9 %all-gather.9.cloned.1.call-start = ((), (), s32[]{:S(2)}) async-start(), calls=%async_computation.4 | async-start | bytes 1769472 | tf_op jit(solution)/shard_map/all_gather | solution.py:35
  7.9 170.0 %all-reduce.11.cloned.1.call-start = ((), (), s32[]{:S(2)}) async-start(), calls=%async_computation.5 | async-start | bytes 2097152 | tf_op jit(solution)/shard_map/psum | solution.py:308
  52.3 37.9 %copy-start.56 = (f32[8,1,128]{2,1,0:T(1,128)}, f32[8,1,128]{2,1,0:T(1,128)S(1)}, u32[]{:S(2)}) copy-start(f32[8,1,128]{2,1,0:T(1,128)S(1)} %convert_element_type.125) | copy-start | bytes 12292
  57.2 33.0 %copy-start.50 = (f32[256]{0:T(256)}, f32[256]{0:T(256)S(1)}, u32[]{:S(2)}) copy-start(f32[256]{0:T(256)S(1)} %broadcast_multiply_fusion.1) | copy-start | bytes 3076
  59.1 31.1 %copy-start.62 = (f32[256]{0:T(256)}, f32[256]{0:T(256)S(1)}, u32[]{:S(2)}) copy-start(f32[256]{0:T(256)S(1)} %fusion.92) | copy-start | bytes 3076
  90.8 17.2 %collective-permute-start = (bf16[4,4,64,128]{3,2,0,1:T(8,128)(2,1)S(1)}, bf16[4,4,64,128]{3,2,0,1:T(8,128)(2,1)S(1)}, u32[]{:S(2)}, u32[]{:S(2)}) collective-permute-start(bf16[4,4,64,128]{3,2,0,1:T(8,128)(2,1)S(1)} %maximum_bitcast_fusion), channel_id=1, source_target_pairs={{0,12},{4,16},{8,20},{12,24},{16,28},{1,13},{5,17},{9,21},{13,25},... | collective-permute-start | bytes 786440 | tf_op jit(solution)/shard_map/ppermute | solution.py:19
  96.3 33.9 %copy-start.40 = (pred[128,64]{1,0:T(8,128)(4,1)}, pred[128,64]{1,0:T(8,128)(4,1)S(1)}, u32[]{:S(2)}) copy-start(pred[128,64]{1,0:T(8,128)(4,1)S(1)} %gather_fusion.1) | copy-start | bytes 24580
  96.3 13.1 %collective-permute-start.1 = (bf16[4,4,64,128]{3,2,0,1:T(8,128)(2,1)S(1)}, bf16[4,4,64,128]{3,2,0,1:T(8,128)(2,1)S(1)}, u32[]{:S(2)}, u32[]{:S(2)}) collective-permute-start(bf16[4,4,64,128]{3,2,0,1:T(8,128)(2,1)S(1)} %maximum_bitcast_fusion), channel_id=1, source_target_pairs={{0,8},{4,12},{8,16},{12,20},{16,24},{20,28},{1,9},{5,13},{9,17},{1... | collective-permute-start | bytes 786440 | tf_op jit(solution)/shard_map/ppermute | solution.py:19
  99.5 9.8 %collective-permute-start.2 = (bf16[4,4,64,128]{3,2,0,1:T(8,128)(2,1)S(1)}, bf16[4,4,64,128]{3,2,0,1:T(8,128)(2,1)S(1)}, u32[]{:S(2)}, u32[]{:S(2)}) collective-permute-start(bf16[4,4,64,128]{3,2,0,1:T(8,128)(2,1)S(1)} %maximum_bitcast_fusion), channel_id=1, source_target_pairs={{0,4},{4,8},{8,12},{12,16},{16,20},{20,24},{24,28},{1,5},{5,9},{9,... | collective-permute-start | bytes 786440 | tf_op jit(solution)/shard_map/ppermute | solution.py:19
  104.9 8.3 collective-permute-start.3
  106.2 9.2 %collective-permute-start.4 = (bf16[4,4,64,128]{3,2,0,1:T(8,128)(2,1)S(1)}, bf16[4,4,64,128]{3,2,0,1:T(8,128)(2,1)S(1)}, u32[]{:S(2)}, u32[]{:S(2)}) collective-permute-start(bf16[4,4,64,128]{3,2,0,1:T(8,128)(2,1)S(1)} %maximum_bitcast_fusion), channel_id=1, source_target_pairs={{8,0},{12,4},{16,8},{20,12},{24,16},{28,20},{9,1},{13,5},{17,9},{2... | collective-permute-start | bytes 786440 | tf_op jit(solution)/shard_map/ppermute | solution.py:19
  107.7 12.3 %copy-start.32 = (bf16[64,1,256]{0,2,1:T(8,128)(2,1)}, bf16[64,1,256]{0,2,1:T(8,128)(2,1)S(1)}, u32[]{:S(2)}) copy-start(bf16[64,1,256]{0,2,1:T(8,128)(2,1)S(1)} %copy.124) | copy-start | bytes 98308
  107.8 12.2 %copy-start.34 = (bf16[64,1,256]{0,2,1:T(8,128)(2,1)}, bf16[64,1,256]{0,2,1:T(8,128)(2,1)S(1)}, u32[]{:S(2)}) copy-start(bf16[64,1,256]{0,2,1:T(8,128)(2,1)S(1)} %copy.125) | copy-start | bytes 98308
  108.0 17.2 %copy-start.29 = (bf16[4,64,4,64]{3,2,1,0:T(4,128)(2,1)}, bf16[4,64,4,64]{3,2,1,0:T(4,128)(2,1)S(1)}, u32[]{:S(2)}) copy-start(bf16[4,64,4,64]{3,2,1,0:T(4,128)(2,1)S(1)} %reshape_squeeze.14) | copy-start | bytes 393220
  108.0 11.4 %collective-permute-start.5 = (bf16[4,4,64,128]{3,2,0,1:T(8,128)(2,1)S(1)}, bf16[4,4,64,128]{3,2,0,1:T(8,128)(2,1)S(1)}, u32[]{:S(2)}, u32[]{:S(2)}) collective-permute-start(bf16[4,4,64,128]{3,2,0,1:T(8,128)(2,1)S(1)} %maximum_bitcast_fusion), channel_id=1, source_target_pairs={{12,0},{16,4},{20,8},{24,12},{28,16},{13,1},{17,5},{21,9},{25,13},... | collective-permute-start | bytes 786440 | tf_op jit(solution)/shard_map/ppermute | solution.py:19
  120.7 4.5 copy-start.52
  121.0 14.9 %copy-start.16 = (bf16[4,128,16,64]{1,3,2,0:T(8,128)(2,1)}, bf16[4,128,16,64]{1,3,2,0:T(8,128)(2,1)S(1)}, u32[]{:S(2)}) copy-start(bf16[4,128,16,64]{1,3,2,0:T(8,128)(2,1)S(1)} %fusion.10) | copy-start | bytes 3145732
  131.6 4.3 copy-start.8
  137.0 4.4 copy-start.73
  137.0 24.7 %copy-start.74 = (bf16[128]{0:T(256)(128)(2,1)S(1)}, bf16[128]{0:T(256)(128)(2,1)}, u32[]{:S(2)}) copy-start(bf16[128]{0:T(256)(128)(2,1)} %param.21) | copy-start | bytes 772
  137.0 40.8 %copy-start.72 = (bf16[1024]{0:T(1024)(128)(2,1)S(1)}, bf16[1024]{0:T(1024)(128)(2,1)}, u32[]{:S(2)}) copy-start(bf16[1024]{0:T(1024)(128)(2,1)} %param.23) | copy-start | bytes 6148
  137.2 40.6 %copy-start.42 = (bf16[64,256]{1,0:T(8,128)(2,1)}, bf16[64,256]{1,0:T(8,128)(2,1)S(1)}, u32[]{:S(2)}) copy-start(bf16[64,256]{1,0:T(8,128)(2,1)S(1)} %copy.90) | copy-start | bytes 98308
  137.3 40.5 %copy-start.44 = (bf16[64,256]{1,0:T(8,128)(2,1)}, bf16[64,256]{1,0:T(8,128)(2,1)S(1)}, u32[]{:S(2)}) copy-start(bf16[64,256]{1,0:T(8,128)(2,1)S(1)} %copy.91) | copy-start | bytes 98308
  137.6 40.2 %copy-start.36 = (bf16[128,256]{1,0:T(8,128)(2,1)}, bf16[128,256]{1,0:T(8,128)(2,1)S(1)}, u32[]{:S(2)}) copy-start(bf16[128,256]{1,0:T(8,128)(2,1)S(1)} %concatenate.85) | copy-start | bytes 196612
  140.0 90.8 %all-gather.13.cloned.1.call-start = ((), (), s32[]{:S(2)}) async-start(), calls=%async_computation.7 | async-start | bytes 2359296 | tf_op jit(solution)/shard_map/all_gather | solution.py:48
  140.7 139.7 %all-gather.11.cloned.1.call-start = ((), (), s32[]{:S(2)}) async-start(), calls=%async_computation.6 | async-start | bytes 2359296 | tf_op jit(solution)/shard_map/all_gather | solution.py:36
  141.3 181.5 %all-reduce.15.cloned.1.call-start = ((), (), s32[]{:S(2)}) async-start(), calls=%async_computation.9 | async-start | bytes 2097152 | tf_op jit(solution)/shard_map/psum | solution.py:348
  161.7 197.6 %copy-start.48 = (f32[8,1,128]{2,1,0:T(1,128)}, f32[8,1,128]{2,1,0:T(1,128)S(1)}, u32[]{:S(2)}) copy-start(f32[8,1,128]{2,1,0:T(1,128)S(1)} %convert_element_type.126) | copy-start | bytes 12292
  177.8 102.6 %copy-start.60 = (f32[8,1,128]{2,1,0:T(1,128)}, f32[8,1,128]{2,1,0:T(1,128)S(1)}, u32[]{:S(2)}) copy-start(f32[8,1,128]{2,1,0:T(1,128)S(1)} %convert_element_type.127) | copy-start | bytes 12292
  179.5 179.7 %copy-start.54 = (f32[256]{0:T(256)}, f32[256]{0:T(256)S(1)}, u32[]{:S(2)}) copy-start(f32[256]{0:T(256)S(1)} %broadcast_multiply_fusion) | copy-start | bytes 3076
  179.7 179.5 %copy-start.64 = (f32[256]{0:T(256)}, f32[256]{0:T(256)S(1)}, u32[]{:S(2)}) copy-start(f32[256]{0:T(256)S(1)} %fusion.93) | copy-start | bytes 3076
  280.5 5.9 copy-start.26
  288.1 71.1 %all-reduce.13.cloned.1.call-start = ((), (), s32[]{:S(2)}) async-start(), calls=%async_computation.8 | async-start | bytes 1048576 | tf_op jit(solution)/shard_map/psum | solution.py:317
  310.6 208.1 %all-reduce.17.cloned.1.call-start = ((), (), s32[]{:S(2)}) async-start(), calls=%async_computation.10 | async-start | bytes 2097152 | tf_op jit(solution)/shard_map/psum | solution.py:389
  359.2 3.6 copy-start.21
  364.9 6.0 copy-start.1
  364.9 6.0 copy-start.41
  364.9 6.0 copy-start.71
  370.9 3.6 copy-start.47
  371.0 3.7 copy-start.46
  371.0 3.8 copy-start.53
  377.6 3.8 copy-start.11
  378.1 4.9 copy-start.2
  419.4 23.8 %copy-start.20 = (bf16[128,64,128]{2,1,0:T(8,128)(2,1)S(1)}, bf16[128,64,128]{2,1,0:T(8,128)(2,1)}, u32[]{:S(2)}) copy-start(bf16[128,64,128]{2,1,0:T(8,128)(2,1)} %gather_fusion) | copy-start | bytes 6291460
  422.2 15.8 %collective-permute-start.10 = (f32[4,4,64,128]{3,2,1,0:T(8,128)S(1)}, f32[4,4,64,128]{3,2,1,0:T(8,128)S(1)}, u32[]{:S(2)}, u32[]{:S(2)}) collective-permute-start(f32[4,4,64,128]{3,2,1,0:T(8,128)S(1)} %get-tuple-element.35), channel_id=1, source_target_pairs={{0,8},{4,12},{8,16},{12,20},{16,24},{20,28},{1,9},{5,13},{9,17},{1... | collective-permute-start | bytes 1572872 | tf_op jit(solution)/shard_map/ppermute | solution.py:19
  425.6 28.8 %collective-permute-start.11 = (f32[4,4,64,128]{3,2,1,0:T(8,128)}, f32[4,4,64,128]{3,2,1,0:T(8,128)}, u32[]{:S(2)}, u32[]{:S(2)}) collective-permute-start(f32[4,4,64,128]{3,2,1,0:T(8,128)} %get-tuple-element.34), channel_id=1, source_target_pairs={{0,12},{4,16},{8,20},{12,24},{16,28},{1,13},{5,17},{9,21},{13,25},... | collective-permute-start | bytes 1572872 | tf_op jit(solution)/shard_map/ppermute | solution.py:19
  430.5 24.0 %collective-permute-start.6 = (f32[4,4,64,128]{3,2,1,0:T(8,128)}, f32[4,4,64,128]{3,2,1,0:T(8,128)}, u32[]{:S(2)}, u32[]{:S(2)}) collective-permute-start(f32[4,4,64,128]{3,2,1,0:T(8,128)} %get-tuple-element.33), channel_id=1, source_target_pairs={{12,0},{16,4},{20,8},{24,12},{28,16},{13,1},{17,5},{21,9},{25,13},... | collective-permute-start | bytes 1572872 | tf_op jit(solution)/shard_map/ppermute | solution.py:19
  431.8 28.1 %collective-permute-start.7 = (f32[4,4,64,128]{3,2,1,0:T(8,128)}, f32[4,4,64,128]{3,2,1,0:T(8,128)}, u32[]{:S(2)}, u32[]{:S(2)}) collective-permute-start(f32[4,4,64,128]{3,2,1,0:T(8,128)} %get-tuple-element.38), channel_id=1, source_target_pairs={{8,0},{12,4},{16,8},{20,12},{24,16},{28,20},{9,1},{13,5},{17,9},{2... | collective-permute-start | bytes 1572872 | tf_op jit(solution)/shard_map/ppermute | solution.py:19
  433.1 26.8 %collective-permute-start.8 = (f32[4,4,64,128]{3,2,1,0:T(8,128)}, f32[4,4,64,128]{3,2,1,0:T(8,128)}, u32[]{:S(2)}, u32[]{:S(2)}) collective-permute-start(f32[4,4,64,128]{3,2,1,0:T(8,128)} %get-tuple-element.37), channel_id=1, source_target_pairs={{4,0},{8,4},{12,8},{16,12},{20,16},{24,20},{28,24},{5,1},{9,5},{13... | collective-permute-start | bytes 1572872 | tf_op jit(solution)/shard_map/ppermute | solution.py:19
  438.8 5.3 copy-start.9
  438.8 5.3 copy-start.13
  438.8 32.7 %collective-permute-start.9 = (f32[4,4,64,128]{3,2,1,0:T(8,128)}, f32[4,4,64,128]{3,2,1,0:T(8,128)}, u32[]{:S(2)}, u32[]{:S(2)}) collective-permute-start(f32[4,4,64,128]{3,2,1,0:T(8,128)} %get-tuple-element.36), channel_id=1, source_target_pairs={{0,4},{4,8},{8,12},{12,16},{16,20},{20,24},{24,28},{1,5},{5,9},{9,... | collective-permute-start | bytes 1572872 | tf_op jit(solution)/shard_map/ppermute | solution.py:19
  444.0 27.5 %copy-start.39 = (f32[4,4,64,128]{3,2,1,0:T(8,128)S(1)}, f32[4,4,64,128]{3,2,1,0:T(8,128)}, u32[]{:S(2)}) copy-start(f32[4,4,64,128]{3,2,1,0:T(8,128)} %copy-done.38) | copy-start | bytes 1572868
  474.7 3.2 copy-start.25
  474.7 3.2 copy-start.37
  477.8 109.6 %reduce-scatter.7.cloned.1.call-start = ((), (), s32[]{:S(2)}) async-start(), calls=%async_computation.12 | async-start | bytes 1179648 | tf_op jit(solution)/shard_map/reduce_scatter | solution.py:407
  479.2 186.5 %reduce-scatter.5.cloned.1.call-start = ((), (), s32[]{:S(2)}) async-start(), calls=%async_computation.11 | async-start | bytes 3538944 | tf_op jit(solution)/shard_map/reduce_scatter | solution.py:398
  481.8 275.3 %reduce-scatter.9.cloned.1.call-start = ((), (), s32[]{:S(2)}) async-start(), calls=%async_computation.13 | async-start | bytes 4718592 | tf_op jit(solution)/shard_map/reduce_scatter | solution.py:399
  485.7 364.3 %reduce-scatter.11.cloned.1.call-start = ((), (), s32[]{:S(2)}) async-start(), calls=%async_computation.14 | async-start | bytes 4718592 | tf_op jit(solution)/shard_map/reduce_scatter | solution.py:408
  489.9 30.4 %copy-start.67 = (f32[256]{0:T(256)S(1)}, f32[256]{0:T(256)}, u32[]{:S(2)}) copy-start(f32[256]{0:T(256)} %copy-done.66) | copy-start | bytes 3076
  490.0 32.2 %copy-start.15 = (f32[256,1024]{1,0:T(8,128)S(1)}, f32[256,1024]{1,0:T(8,128)}, u32[]{:S(2)}) copy-start(f32[256,1024]{1,0:T(8,128)} %copy-done.14) | copy-start | bytes 3145732
  490.0 32.2 %copy-start.69 = (f32[256]{0:T(256)S(1)}, f32[256]{0:T(256)}, u32[]{:S(2)}) copy-start(f32[256]{0:T(256)} %copy-done.68) | copy-start | bytes 3076
  518.7 3.5 copy-start.18
  (36 other events, 56.4 us)
Sparse Core Ops, SparseCore 0:
  10.2 46.6 all-gather.8
  140.1 36.8 all-reduce.10
  179.3 51.4 all-gather.12
  233.0 47.4 all-gather.10
  288.2 34.5 all-reduce.14
  325.6 33.5 all-reduce.12
  477.9 40.7 all-reduce.16
  523.1 64.3 reduce-scatter.6
  591.6 74.0 reduce-scatter.4
  669.8 87.2 reduce-scatter.8
  761.7 88.2 reduce-scatter.10
where the time goes:
time: 858 us; the launch traced here: 856 us
  waiting for transfers between devices  498 us (58%)
  blocking collectives  160 us (19%)
  other arithmetic  56.7 us (7%)
  matrix products  56.1 us (7%)
  starting transfers between devices  33.5 us (4%)
  local copies, waits for them, and re-layouts  32.7 us (4%)
  between operations  19.7 us (2%)
    reduce_scatter x1, waiting for transfers between devices, local(): lax.psum_scatter(grad_w_down, 'seq', scatter_dimension=1, tiled=True)  92.9 us
    reduce_scatter x1, waiting for transfers between devices, local(): lax.psum_scatter(grad_w_up, 'seq', scatter_dimension=0, tiled=True)  91.3 us
    reduce_scatter x1, waiting for transfers between devices, local(): lax.psum_scatter(grad_w_qkv, 'seq', scatter_dimension=0, tiled=True)  78.3 us
    all_gather x1, waiting for transfers between devices, gather_columns(): lax.all_gather(w_down, 'seq', axis=1, tiled=True)  51 us
    all_gather x1, waiting for transfers between devices, gather_rows(): lax.all_gather(w_up, 'seq', axis=0, tiled=True)  46.2 us
    ppermute x12, waiting for transfers between devices, passed_along(): lax.ppermute(value, axis, [(source, source + steps) for source in range(l...  39.7 us
    unnamed x1, blocking collectives  37.8 us
    psum x1, waiting for transfers between devices, local(): lax.psum(jnp.dot(hidden, down_full, preferred_element_type=jnp.float32).a...  34.2 us
  transfers between devices with their start and end apart: 23, of which 16 were waited for; matrix products, arithmetic and copies ran while one was open for 5% of the time, Pallas kernels for 0%

commit v1 on v0

v1 whole, which is shorter than its diff:
```python
import jax
import jax.numpy as jnp
from jax import lax
from jax.sharding import PartitionSpec as P

HEAD_DIM = 64
BLK = 64
SPAN = 4
BLK_DEV = 4
EPSILON = 1e-05
NEGATIVE = -1e30
F32 = jnp.float32
BF16 = jnp.bfloat16


def shifted(value, axis, steps):
    count = lax.axis_size(axis)
    first, last = max(0, -steps), min(count, count - steps)
    return lax.ppermute(value, axis, [(i, i + steps) for i in range(first, last)])


def norm_parts(features):
    average = jnp.mean(features, axis=-1, keepdims=True)
    centred = features - average
    spread = jnp.mean(centred * centred, axis=-1, keepdims=True)
    inverse = lax.rsqrt(spread + EPSILON)
    return centred * inverse, inverse


def norm_backward(xhat, inverse, scaled):
    first = jnp.mean(scaled, axis=-1, keepdims=True)
    second = jnp.mean(scaled * xhat, axis=-1, keepdims=True)
    return inverse * (scaled - first - xhat * second)


def dot(a, b, dims):
    return lax.dot_general(a, b, (dims, ((), ())), preferred_element_type=F32)


def sequence_place(seq_units, seq_pad):
    device = lax.axis_index("seq")
    start, leader, span, pad = 0, 0, 0, 0
    for k in range(seq_units.shape[0]):
        units = seq_units[k]
        inside = (device >= start) & (device < start + units)
        leader = jnp.where(inside, start, leader)
        span = jnp.where(inside, units, span)
        pad = jnp.where(inside, seq_pad[k], pad)
        start = start + units
    return device - leader, span, pad


def key_counts(position, span, picks):
    blocks = lax.broadcasted_iota(jnp.int32, (1, 1, SPAN * BLK_DEV), 2)
    query = position * BLK_DEV + lax.broadcasted_iota(jnp.int32, (BLK_DEV, 1, 1), 0)
    total = span * BLK_DEV
    count = jnp.zeros((BLK_DEV, picks.shape[1], SPAN * BLK_DEV), F32)
    for wanted in (query - 1, query, query + 1, 0, total - 1):
        count = count + (blocks == wanted).astype(F32)
    chosen = picks % total
    for r in range(picks.shape[2]):
        count = count + (blocks == chosen[:, :, r : r + 1]).astype(F32)
    return jnp.where((query == 0) | (query == total - 1), 1.0, count)


def local_general(
    tokens, w_qkv, w_out, ln1_gain, ln1_bias, ln2_gain, ln2_bias, w_up, up_bias, w_down, down_bias,
    seq_units, seq_pad, rand_picks, cotangent,
):
    tok, width = tokens.shape
    heads = w_qkv.shape[2] // HEAD_DIM
    rows = lambda v: lax.all_gather(v, "seq", axis=0, tiled=True)
    cols = lambda v: lax.all_gather(v, "seq", axis=1, tiled=True)
    vectors = jnp.stack([ln1_gain, ln1_bias, ln2_gain, ln2_bias, down_bias], axis=0)
    gain_one, shift_one, gain_two, shift_two, down_shift = [
        v[None].astype(F32) for v in cols(vectors)
    ]
    qkv = rows(w_qkv)
    out_w, up_w, down_w = cols(w_out), rows(w_up), cols(w_down)
    position, span, pad = sequence_place(seq_units, seq_pad)
    root = SPAN - 1 - position
    inputs = tokens.astype(F32)
    xhat_one, inv_one = norm_parts(inputs)
    normed = (xhat_one * gain_one + shift_one).astype(BF16)
    triple = jnp.einsum("td,dcf->tcf", normed, qkv, preferred_element_type=F32).astype(BF16)
    own = jnp.stack([triple[:, 1], triple[:, 2]], axis=0)
    pieces = [own if o == 0 else shifted(own, "seq", -o) for o in range(1 - SPAN, SPAN)]
    nearby = jnp.stack(pieces, axis=0)
    window = lax.dynamic_slice_in_dim(nearby, root, SPAN, 0)
    split = lambda v: v.reshape(v.shape[0], heads, HEAD_DIM)
    keys = split(window[:, 0].reshape(SPAN * tok, -1))
    values = split(window[:, 1].reshape(SPAN * tok, -1))
    queries = split(triple[:, 0])
    scaling = HEAD_DIM ** (-0.5)
    live = jnp.arange(SPAN * tok, dtype=jnp.int32) < span * tok - pad
    count = jnp.repeat(key_counts(position, span, rand_picks), BLK, axis=2)
    count = jnp.where(live[None, None], count, 0.0)
    count = jnp.transpose(jnp.repeat(count, BLK, axis=0), (1, 0, 2))
    logits = jnp.einsum("qhd,khd->hqk", queries, keys, preferred_element_type=F32) * scaling
    logits = jnp.where(count > 0, logits, NEGATIVE)
    grown = jnp.exp(logits - jnp.max(logits, axis=-1, keepdims=True)) * count
    chances = grown / jnp.sum(grown, axis=-1, keepdims=True)
    chances_low = chances.astype(BF16)
    attended = jnp.einsum("hqk,khd->qhd", chances_low, values, preferred_element_type=F32)
    attended = attended.astype(BF16).reshape(tok, heads * HEAD_DIM)
    middle = inputs + lax.psum(dot(attended, out_w, ((1,), (0,))), "head")
    xhat_two, inv_two = norm_parts(middle)
    normed_two = (xhat_two * gain_two + shift_two).astype(BF16)
    pre_act = dot(normed_two, up_w, ((1,), (0,))) + up_bias.astype(F32)[None]
    hidden, pull = jax.vjp(lambda v: jax.nn.gelu(v, approximate=True), pre_act)
    hidden = hidden.astype(BF16)
    ffn = lax.psum(dot(hidden, down_w, ((1,), (0,))).astype(BF16), "head").astype(F32)
    output = (middle + ffn + down_shift).astype(BF16)
    grad_out = cotangent.astype(F32)
    grad_w_down = dot(hidden, cotangent, ((0,), (0,)))
    grad_pre = pull(dot(cotangent, down_w, ((1,), (1,))))[0].astype(BF16)
    grad_w_up = dot(normed_two, grad_pre, ((0,), (0,)))
    grad_up_bias = lax.psum(jnp.sum(grad_pre.astype(F32), axis=0), "seq")
    grad_two = lax.psum(dot(grad_pre, up_w, ((1,), (1,))), "head")
    grad_middle = grad_out + norm_backward(xhat_two, inv_two, grad_two * gain_two)
    grad_branch = grad_middle.astype(BF16)
    grad_w_out = dot(attended, grad_branch, ((0,), (0,)))
    grad_att = split(dot(grad_branch, out_w, ((1,), (1,))).astype(BF16))
    grad_prob = jnp.einsum("qhd,khd->hqk", grad_att, values, preferred_element_type=F32)
    inner = jnp.sum(chances * grad_prob, axis=-1, keepdims=True)
    grad_logit = (chances * (grad_prob - inner)).astype(BF16)
    dq = scaling * jnp.einsum("hqk,khd->qhd", grad_logit, keys, preferred_element_type=F32)
    dk = scaling * jnp.einsum("hqk,qhd->khd", grad_logit, queries, preferred_element_type=F32)
    dv = jnp.einsum("hqk,qhd->khd", chances_low, grad_att, preferred_element_type=F32)
    part = jnp.stack([dk.reshape(SPAN, tok, -1), dv.reshape(SPAN, tok, -1)], axis=1)
    near = jnp.zeros((2 * SPAN - 1,) + part.shape[1:], F32)
    near = lax.dynamic_update_slice_in_dim(near, part, root, 0)
    owned = near[SPAN - 1]
    for offset in range(1 - SPAN, SPAN):
        if offset:
            owned = owned + shifted(near[offset + SPAN - 1], "seq", offset)
    owned = owned.astype(BF16)
    grad_triple = jnp.stack([dq.reshape(tok, -1).astype(BF16), owned[0], owned[1]], axis=1)
    grad_w_qkv = jnp.einsum("td,tcf->dcf", normed, grad_triple, preferred_element_type=F32)
    grad_one = lax.psum(
        jnp.einsum("tcf,dcf->td", grad_triple, qkv, preferred_element_type=F32), "head"
    )
    x_grad = grad_middle + norm_backward(xhat_one, inv_one, grad_one * gain_one)
    sums = jnp.stack(
        [
            jnp.sum(grad_one * xhat_one, axis=0), jnp.sum(grad_one, axis=0),
            jnp.sum(grad_two * xhat_two, axis=0), jnp.sum(grad_two, axis=0),
            jnp.sum(grad_out, axis=0),
        ],
        axis=0,
    )
    scatter = lambda v, d: lax.psum_scatter(v, "seq", scatter_dimension=d, tiled=True)
    sums = scatter(sums, 1)
    return (
        output, x_grad, scatter(grad_w_qkv, 0), scatter(grad_w_out, 1), sums[0], sums[1], sums[2],
        sums[3], scatter(grad_w_up, 0), grad_up_bias, scatter(grad_w_down, 1), sums[4],
    )


IN_SPECS = (
    P("seq", None), P("seq", None, "head"), P("head", "seq"), P("seq"), P("seq"), P("seq"),
    P("seq"), P("seq", "head"), P("head"), P("head", "seq"), P("seq"), P(), P(),
    P("seq", "head", None), P("seq", None),
)
OUT_SPECS = (
    P("seq", None), P("seq", None), P("seq", None, "head"), P("head", "seq"), P("seq"), P("seq"),
    P("seq"), P("seq"), P("seq", "head"), P("head"), P("head", "seq"), P("seq"),
)


def solution(mesh):
    return jax.shard_map(
        local_general, mesh=mesh, in_specs=IN_SPECS, out_specs=OUT_SPECS, check_vma=False
    )
```

time: 858 us -> 853 us (level)
  waiting for transfers between devices: 498 us -> 636 us
  blocking collectives: 160 us -> 77.8 us
  other arithmetic: 56.7 us -> 18.9 us
  matrix products: 56.1 us -> 35.6 us
    psum x4, waiting for transfers between devices: 73.3 us -> 146 us  [the longest x1 41.7 us: local_general(): lax.psum(jnp.einsum('tcf,dcf->td', grad_triple, qkv, preferred_element_ty...]
    all_gather x6 -> x2, blocking collectives: 122 us -> 55.7 us  [local_general(): cols = lambda v: lax.all_gather(v, 'seq', axis=1, tiled=True)]
    reduce_scatter x4 -> x5, waiting for transfers between devices: 285 us -> 348 us  [local_general(): lax.psum_scatter(v, 'seq', scatter_dimension=d, tiled=True)]
    unnamed x1 -> x0, blocking collectives: 37.8 us -> none
    psum x0 -> x1, blocking collectives: none -> 22.1 us  [local_general(): grad_up_bias = lax.psum(jnp.sum(grad_pre.astype(F32), axis=0), 'seq')]
    scatter-add x1 -> x0, other arithmetic: 21.4 us -> none  [attend_backward(): grad_near = jnp.zeros(nearby.shape, jnp.float32).at[indices, head_ids].ad...]
    dot_general x22 -> x18, matrix products: 53.7 us -> 35.6 us  [the longest x9 20.3 us: dot(): return lax.dot_general(a, b, (dims, ((), ())), preferred_element_type=F32)]
    another operation x7 -> x10, local copies, waits for them, and re-layouts: 0.99 us -> 12.6 us  [the longest x4 10.5 us: local_general(): jnp.stack([dk.reshape(SPAN, tok, -1), dv.reshape(SPAN, tok, -1)], axis=1)]
  transfers between devices with their start and end apart: 23 -> 24, of which waited for: 16 -> 17; matrix products, arithmetic and copies ran while one was open for 5% -> 4% of each run, Pallas kernels for 0% -> 0%
where the time goes in v1:
time: 853 us; the launch traced here: 851 us
  waiting for transfers between devices  636 us (75%)
  blocking collectives  77.8 us (9%)
  matrix products  35.6 us (4%)
  starting transfers between devices  29.3 us (3%)
  local copies, waits for them, and re-layouts  29.2 us (3%)
  between operations  24.6 us (3%)
  other arithmetic  18.9 us (2%)
    reduce_scatter x5, waiting for transfers between devices, local_general(): lax.psum_scatter(v, 'seq', scatter_dimension=d, tiled=True)  348 us
    all_gather x2, blocking collectives, local_general(): cols = lambda v: lax.all_gather(v, 'seq', axis=1, tiled=True)  55.7 us
    all_gather x1, waiting for transfers between devices, local_general(): cols = lambda v: lax.all_gather(v, 'seq', axis=1, tiled=True)  52.1 us
    all_gather x2, waiting for transfers between devices, local_general(): rows = lambda v: lax.all_gather(v, 'seq', axis=0, tiled=True)  46.4 us
    ppermute x12, waiting for transfers between devices, shifted(): lax.ppermute(value, axis, [(i, i + steps) for i in range(first, last)])  42.2 us
    psum x1, waiting for transfers between devices, local_general(): lax.psum(jnp.einsum('tcf,dcf->td', grad_triple, qkv, preferred_element_ty...  41.7 us
    psum x1, waiting for transfers between devices, local_general(): middle = inputs + lax.psum(dot(attended, out_w, ((1,), (0,))), 'head')  38.9 us
    psum x1, waiting for transfers between devices, local_general(): lax.psum(dot(hidden, down_w, ((1,), (0,))).astype(BF16), 'head').astype(F32)  34.6 us
  transfers between devices with their start and end apart: 24, of which 17 were waited for; matrix products, arithmetic and copies ran while one was open for 4% of the time, Pallas kernels for 0%

profile of v1, /device:TPU:0, one launch (start us, length us, event | category | flops | bytes accessed | tf_op | source)
XLA Modules:
  0.0 851.5 jit_solution(9352380124314227854)
XLA Ops:
  7.2 1.8 copy.36
  9.1 1.4 fusion.48
  18.8 1.4 fusion.47
  23.5 27.9 %all_gather.15 = bf16[5,1024]{1,0:T(8,128)(2,1)S(1)} all-gather(bf16[5,128]{1,0:T(8,128)(2,1)S(1)} %stack.75), channel_id=1, replica_groups=mesh['seq'=8,'head'=4] {'seq'}, dimensions={1}, use_global_device_ids=true | all-gather | bytes 11520 | tf_op jit(solution)/shard_map/all_gather | solution.py:73
  52.7 1.3 fusion.16
  54.2 27.8 %all_gather.17 = bf16[256,1024]{1,0:T(8,128)(2,1)S(1)} all-gather(bf16[256,128]{1,0:T(8,128)(2,1)} %param.17), channel_id=1, replica_groups=mesh['seq'=8,'head'=4] {'seq'}, dimensions={1}, use_global_device_ids=true | all-gather | bytes 589824 | tf_op jit(solution)/shard_map/all_gather | solution.py:73
  82.0 2.1 convolution_convert_fusion.1
  84.2 1.6 collective-permute-start
  86.1 5.1 collective-permute-start.1
  91.3 1.5 collective-permute-start.2
  92.7 1.3 collective-permute-start.3
  94.0 1.3 collective-permute-start.4
  95.3 1.3 collective-permute-start.5
  96.8 4.2 collective-permute-done.3
  101.0 6.9 collective-permute-done.4
  109.7 2.9 fusion.49
  113.3 3.2 convolution_convert_fusion.3
  116.6 1.3 fusion.50
  119.3 38.9 %all-reduce.5.cloned.1.call-done = f32[256,1024]{1,0:T(8,128)} async-done(((f32[256,1024]{1,0:T(8,128)}), f32[256,1024]{1,0:T(8,128)}) %all-reduce.5.cloned.1.call-update) | async-done | bytes 1048592 | tf_op jit(solution)/shard_map/psum | solution.py:106
  158.2 1.4 fusion.45
  159.9 52.1 %all-gather.8.cloned.1.call-done = bf16[1024,1024]{1,0:T(8,128)(2,1)} async-done(((bf16[1024,128]{1,0:T(8,128)(2,1)}), bf16[1024,1024]{1,0:T(8,128)(2,1)}) %all-gather.8.cloned.1.call-update) | async-done | bytes 2097168 | tf_op jit(solution)/shard_map/all_gather | solution.py:73
  211.9 3.3 fusion.51
  215.2 46.4 %all-gather.6.cloned.1.call-done = bf16[1024,1024]{1,0:T(8,128)(2,1)} async-done(((bf16[128,1024]{1,0:T(8,128)(2,1)}), bf16[1024,1024]{1,0:T(8,128)(2,1)}) %all-gather.6.cloned.1.call-update) | async-done | bytes 2097168 | tf_op jit(solution)/shard_map/all_gather | solution.py:72
  261.6 3.5 convert_reduce_fusion.2
  266.0 1.7 fusion.52
  267.8 3.2 convolution_convert_fusion
  271.2 31.2 %all-reduce.9.cloned.1.call-done = f32[256,1024]{1,0:T(8,128)} async-done(((f32[256,1024]{1,0:T(8,128)}), f32[256,1024]{1,0:T(8,128)}) %all-reduce.9.cloned.1.call-update) | async-done | bytes 1048592 | tf_op jit(solution)/shard_map/psum | solution.py:119
  302.4 1.7 multiply_reduce_fusion.1
  304.2 34.6 %all-reduce.7.cloned.1.call-done = bf16[256,1024]{1,0:T(8,128)(2,1)} async-done(((bf16[256,1024]{1,0:T(8,128)(2,1)}), bf16[256,1024]{1,0:T(8,128)(2,1)}) %all-reduce.7.cloned.1.call-update) | async-done | bytes 524304 | tf_op jit(solution)/shard_map/psum | solution.py:112
  338.8 2.9 convert_add_fusion.1
  343.2 1.7 convolution_bitcast_fusion.1
  345.6 1.3 copy-done.1
  346.9 1.4 fusion.1
  348.4 2.7 stack_reshape.6
  351.1 2.6 copy.42
  353.6 2.7 stack_reshape.7
  356.3 2.5 copy.43
  360.6 1.5 slice_bitcast_fusion.5
  362.1 1.5 copy-done.4
  363.6 4.2 collective-permute-start.10
  367.8 4.3 collective-permute-start.11
  373.3 1.3 collective-permute-start.7
  374.6 1.3 collective-permute-start.8
  375.9 3.4 collective-permute-done.10
  379.3 4.2 collective-permute-start.9
  384.4 11.5 %collective-permute-done.11 = f32[2,256,256]{2,1,0:T(8,128)} collective-permute-done((f32[2,256,256]{2,1,0:T(8,128)}, f32[2,256,256]{2,1,0:T(8,128)}, u32[]{:S(2)}, u32[]{:S(2)}) %collective-permute-start.11) | collective-permute-done | bytes 524320 | tf_op jit(solution)/shard_map/ppermute | solution.py:19
  395.9 5.4 collective-permute-done.7
  401.3 10.7 %collective-permute-done.9 = f32[2,256,256]{2,1,0:T(8,128)} collective-permute-done((f32[2,256,256]{2,1,0:T(8,128)}, f32[2,256,256]{2,1,0:T(8,128)}, u32[]{:S(2)}, u32[]{:S(2)}) %collective-permute-start.9) | collective-permute-done | bytes 524320 | tf_op jit(solution)/shard_map/ppermute | solution.py:19
  412.0 2.2 fusion.33
  414.3 1.6 convolution_bitcast_fusion
  415.9 41.7 %all-reduce.11.cloned.1.call-done = f32[256,1024]{1,0:T(8,128)} async-done(((f32[256,1024]{1,0:T(8,128)}), f32[256,1024]{1,0:T(8,128)}) %all-reduce.11.cloned.1.call-update) | async-done | bytes 1048592 | tf_op jit(solution)/shard_map/psum | solution.py:140
  457.6 1.8 fusion.15
  460.1 1.3 fusion.34
  461.4 2.5 fusion.37
  465.0 2.8 fusion.43
  469.2 2.9 fusion.42
  472.1 22.1 %psum.39 = f32[1024]{0:T(1024)} all-reduce(f32[1024]{0:T(1024)S(1)} %get-tuple-element.20), channel_id=1, replica_groups=mesh['seq'=8,'head'=4] {'seq'}, use_global_device_ids=true, to_apply=%region_25.26 | all-reduce | flops 1024 | bytes 8192 | tf_op jit(solution)/shard_map/psum | solution.py:118
  494.2 1.3 fusion.14
  495.5 19.4 %reduce-scatter.10.cloned.1.call-done = f32[5,128]{1,0:T(8,128)} async-done(((f32[5,1024]{1,0:T(8,128)}), f32[5,128]{1,0:T(8,128)}) %reduce-scatter.10.cloned.1.call-update) | async-done | bytes 2576 | tf_op jit(solution)/shard_map/reduce_scatter | solution.py:152
  514.9 1.4 slice_bitcast_fusion.14
  516.3 65.9 %reduce-scatter.8.cloned.1.call-done = f32[256,128]{1,0:T(8,128)} async-done(((f32[256,1024]{1,0:T(8,128)}), f32[256,128]{1,0:T(8,128)}) %reduce-scatter.8.cloned.1.call-update) | async-done | bytes 131088 | tf_op jit(solution)/shard_map/reduce_scatter | solution.py:152
  582.2 78.2 %reduce-scatter.6.cloned.1.call-done = f32[128,3,256]{2,0,1:T(8,128)} async-done(((f32[1024,3,256]{2,0,1:T(8,128)}), f32[128,3,256]{2,0,1:T(8,128)}) %reduce-scatter.6.cloned.1.call-update) | async-done | bytes 393232 | tf_op jit(solution)/shard_map/reduce_scatter | solution.py:152
  660.4 91.4 %reduce-scatter.12.cloned.1.call-done = f32[128,1024]{1,0:T(8,128)} async-done(((f32[1024,1024]{1,0:T(8,128)}), f32[128,1024]{1,0:T(8,128)}) %reduce-scatter.12.cloned.1.call-update) | async-done | bytes 524304 | tf_op jit(solution)/shard_map/reduce_scatter | solution.py:152
  751.8 92.8 %reduce-scatter.14.cloned.1.call-done = f32[1024,128]{1,0:T(8,128)} async-done(((f32[1024,1024]{1,0:T(8,128)}), f32[1024,128]{1,0:T(8,128)}) %reduce-scatter.14.cloned.1.call-update) | async-done | bytes 524304 | tf_op jit(solution)/shard_map/reduce_scatter | solution.py:152
  (124 shorter events, 18.3 us)
Async XLA Ops:
  7.2 74.8 %copy-start = (bf16[256,1024]{1,0:T(8,128)(2,1)S(1)}, bf16[256,1024]{1,0:T(8,128)(2,1)}, u32[]{:S(2)}) copy-start(bf16[256,1024]{1,0:T(8,128)(2,1)} %param.15) | copy-start | bytes 1572868
  7.2 74.8 %all-gather.4.cloned.1.call-start = ((), (), s32[]{:S(2)}) async-start(), calls=%async_computation.5 | async-start | bytes 1769472 | tf_op jit(solution)/shard_map/all_gather | solution.py:72
  9.0 149.2 %all-reduce.5.cloned.1.call-start = ((), (), s32[]{:S(2)}) async-start(), calls=%async_computation.6 | async-start | bytes 2097152 | tf_op jit(solution)/shard_map/psum | solution.py:106
  84.2 11.1 %collective-permute-start = (bf16[2,256,256]{1,2,0:T(8,128)(2,1)S(1)}, bf16[2,256,256]{1,2,0:T(8,128)(2,1)S(1)}, u32[]{:S(2)}, u32[]{:S(2)}) collective-permute-start(bf16[2,256,256]{1,2,0:T(8,128)(2,1)S(1)} %pad_maximum_fusion.1), channel_id=1, source_target_pairs={{0,12},{4,16},{8,20},{12,24},{16,28},{1,13},{5,17},{9,21},{13,25},... | collective-permute-start | bytes 786440 | tf_op jit(solution)/shard_map/ppermute | solution.py:19
  86.1 10.6 %collective-permute-start.1 = (bf16[2,256,256]{1,2,0:T(8,128)(2,1)S(1)}, bf16[2,256,256]{1,2,0:T(8,128)(2,1)S(1)}, u32[]{:S(2)}, u32[]{:S(2)}) collective-permute-start(bf16[2,256,256]{1,2,0:T(8,128)(2,1)S(1)} %pad_maximum_fusion.1), channel_id=1, source_target_pairs={{0,8},{4,12},{8,16},{12,20},{16,24},{20,28},{1,9},{5,13},{9,17},{1... | collective-permute-start | bytes 786440 | tf_op jit(solution)/shard_map/ppermute | solution.py:19
  91.3 5.4 collective-permute-start.2
  92.7 8.3 collective-permute-start.3
  94.0 13.9 %collective-permute-start.4 = (bf16[2,256,256]{1,2,0:T(8,128)(2,1)S(1)}, bf16[2,256,256]{1,2,0:T(8,128)(2,1)S(1)}, u32[]{:S(2)}, u32[]{:S(2)}) collective-permute-start(bf16[2,256,256]{1,2,0:T(8,128)(2,1)S(1)} %pad_maximum_fusion.1), channel_id=1, source_target_pairs={{8,0},{12,4},{16,8},{20,12},{24,16},{28,20},{9,1},{13,5},{17,9},{2... | collective-permute-start | bytes 786440 | tf_op jit(solution)/shard_map/ppermute | solution.py:19
  95.3 12.6 %collective-permute-start.5 = (bf16[2,256,256]{1,2,0:T(8,128)(2,1)S(1)}, bf16[2,256,256]{1,2,0:T(8,128)(2,1)S(1)}, u32[]{:S(2)}, u32[]{:S(2)}) collective-permute-start(bf16[2,256,256]{1,2,0:T(8,128)(2,1)S(1)} %pad_maximum_fusion.1), channel_id=1, source_target_pairs={{12,0},{16,4},{20,8},{24,12},{28,16},{13,1},{17,5},{21,9},{25,13},... | collective-permute-start | bytes 786440 | tf_op jit(solution)/shard_map/ppermute | solution.py:19
  108.9 0.8 copy-start.5
  113.3 3.2 copy-start.18
  116.6 2.7 copy-start.20
  117.9 94.0 %copy-start.7 = (bf16[256,1024]{1,0:T(8,128)(2,1)S(1)}, bf16[256,1024]{1,0:T(8,128)(2,1)}, u32[]{:S(2)}) copy-start(bf16[256,1024]{1,0:T(8,128)(2,1)} %param.29) | copy-start | bytes 1572868
  117.9 94.0 %all-gather.8.cloned.1.call-start = ((), (), s32[]{:S(2)}) async-start(), calls=%async_computation.8 | async-start | bytes 2359296 | tf_op jit(solution)/shard_map/all_gather | solution.py:73
  118.6 143.0 %all-gather.6.cloned.1.call-start = ((), (), s32[]{:S(2)}) async-start(), calls=%async_computation.7 | async-start | bytes 2359296 | tf_op jit(solution)/shard_map/all_gather | solution.py:72
  119.2 183.2 %all-reduce.9.cloned.1.call-start = ((), (), s32[]{:S(2)}) async-start(), calls=%async_computation.10 | async-start | bytes 2097152 | tf_op jit(solution)/shard_map/psum | solution.py:119
  261.6 4.3 copy-start.12
  265.1 0.8 copy-start.13
  265.2 2.6 copy-start.16
  267.7 71.1 %all-reduce.7.cloned.1.call-start = ((), (), s32[]{:S(2)}) async-start(), calls=%async_computation.9 | async-start | bytes 1048576 | tf_op jit(solution)/shard_map/psum | solution.py:112
  271.0 186.6 %all-reduce.11.cloned.1.call-start = ((), (), s32[]{:S(2)}) async-start(), calls=%async_computation.11 | async-start | bytes 2097152 | tf_op jit(solution)/shard_map/psum | solution.py:140
  338.8 3.3 copy-start.3
  338.8 3.3 copy-start.19
  345.6 1.3 copy-start.1
  358.9 1.2 copy-start.10
  358.9 1.5 copy-start.11
  360.6 3.0 copy-start.4
  360.6 22.9 %copy-start.2 = (bf16[4,256,1024]{2,1,0:T(8,128)(2,1)S(1)}, bf16[4,256,1024]{2,1,0:T(8,128)(2,1)}, u32[]{:S(2)}) copy-start(bf16[4,256,1024]{2,1,0:T(8,128)(2,1)} %copy-done.1) | copy-start | bytes 6291460
  360.6 22.9 %copy-start.6 = (bf16[1024,4,64]{0,2,1:T(8,128)(2,1)S(1)}, bf16[1024,4,64]{0,2,1:T(8,128)(2,1)}, u32[]{:S(2)}) copy-start(bf16[1024,4,64]{0,2,1:T(8,128)(2,1)} %copy-done.5) | copy-start | bytes 1572868
  363.6 15.7 %collective-permute-start.10 = (f32[2,256,256]{2,1,0:T(8,128)S(1)}, f32[2,256,256]{2,1,0:T(8,128)}, u32[]{:S(2)}, u32[]{:S(2)}) collective-permute-start(f32[2,256,256]{2,1,0:T(8,128)S(1)} %get-tuple-element.26), channel_id=1, source_target_pairs={{0,8},{4,12},{8,16},{12,20},{16,24},{20,28},{1,9},{5,13},{9,17},{1... | collective-permute-start | bytes 1572872 | tf_op jit(solution)/shard_map/ppermute | solution.py:19
  367.8 28.1 %collective-permute-start.11 = (f32[2,256,256]{2,1,0:T(8,128)}, f32[2,256,256]{2,1,0:T(8,128)}, u32[]{:S(2)}, u32[]{:S(2)}) collective-permute-start(f32[2,256,256]{2,1,0:T(8,128)} %get-tuple-element.25), channel_id=1, source_target_pairs={{0,12},{4,16},{8,20},{12,24},{16,28},{1,13},{5,17},{9,21},{13,25},... | collective-permute-start | bytes 1572872 | tf_op jit(solution)/shard_map/ppermute | solution.py:19
  372.1 23.9 %collective-permute-start.6 = (f32[2,256,256]{2,1,0:T(8,128)}, f32[2,256,256]{2,1,0:T(8,128)}, u32[]{:S(2)}, u32[]{:S(2)}) collective-permute-start(f32[2,256,256]{2,1,0:T(8,128)} %get-tuple-element.24), channel_id=1, source_target_pairs={{12,0},{16,4},{20,8},{24,12},{28,16},{13,1},{17,5},{21,9},{25,13},... | collective-permute-start | bytes 1572872 | tf_op jit(solution)/shard_map/ppermute | solution.py:19
  373.3 28.0 %collective-permute-start.7 = (f32[2,256,256]{2,1,0:T(8,128)}, f32[2,256,256]{2,1,0:T(8,128)}, u32[]{:S(2)}, u32[]{:S(2)}) collective-permute-start(f32[2,256,256]{2,1,0:T(8,128)} %get-tuple-element.29), channel_id=1, source_target_pairs={{8,0},{12,4},{16,8},{20,12},{24,16},{28,20},{9,1},{13,5},{17,9},{2... | collective-permute-start | bytes 1572872 | tf_op jit(solution)/shard_map/ppermute | solution.py:19
  374.6 26.7 %collective-permute-start.8 = (f32[2,256,256]{2,1,0:T(8,128)}, f32[2,256,256]{2,1,0:T(8,128)}, u32[]{:S(2)}, u32[]{:S(2)}) collective-permute-start(f32[2,256,256]{2,1,0:T(8,128)} %get-tuple-element.28), channel_id=1, source_target_pairs={{4,0},{8,4},{12,8},{16,12},{20,16},{24,20},{28,24},{5,1},{9,5},{13... | collective-permute-start | bytes 1572872 | tf_op jit(solution)/shard_map/ppermute | solution.py:19
  379.3 32.7 %collective-permute-start.9 = (f32[2,256,256]{2,1,0:T(8,128)}, f32[2,256,256]{2,1,0:T(8,128)}, u32[]{:S(2)}, u32[]{:S(2)}) collective-permute-start(f32[2,256,256]{2,1,0:T(8,128)} %get-tuple-element.27), channel_id=1, source_target_pairs={{0,4},{4,8},{8,12},{12,16},{16,20},{20,24},{24,28},{1,5},{5,9},{9,... | collective-permute-start | bytes 1572872 | tf_op jit(solution)/shard_map/ppermute | solution.py:19
  384.4 29.9 %copy-start.15 = (bf16[1024,3,256]{0,2,1:T(8,128)(2,1)S(1)}, bf16[1024,3,256]{0,2,1:T(8,128)(2,1)}, u32[]{:S(2)}) copy-start(bf16[1024,3,256]{0,2,1:T(8,128)(2,1)} %all-gather.4.cloned.1.call-done) | copy-start | bytes 4718596
  415.9 99.1 %reduce-scatter.10.cloned.1.call-start = ((), (), s32[]{:S(2)}) async-start(), calls=%async_computation.14 | async-start | bytes 36864 | tf_op jit(solution)/shard_map/reduce_scatter | solution.py:152
  460.0 122.2 %reduce-scatter.8.cloned.1.call-start = ((), (), s32[]{:S(2)}) async-start(), calls=%async_computation.13 | async-start | bytes 1179648 | tf_op jit(solution)/shard_map/reduce_scatter | solution.py:152
  461.4 199.0 %reduce-scatter.6.cloned.1.call-start = ((), (), s32[]{:S(2)}) async-start(), calls=%async_computation.12 | async-start | bytes 3538944 | tf_op jit(solution)/shard_map/reduce_scatter | solution.py:152
  463.9 1.0 copy-start.14
  464.0 287.9 %reduce-scatter.12.cloned.1.call-start = ((), (), s32[]{:S(2)}) async-start(), calls=%async_computation.15 | async-start | bytes 4718592 | tf_op jit(solution)/shard_map/reduce_scatter | solution.py:152
  467.8 1.0 copy-start.8
  467.8 1.4 copy-start.17
  467.8 376.8 %reduce-scatter.14.cloned.1.call-start = ((), (), s32[]{:S(2)}) async-start(), calls=%async_computation.16 | async-start | bytes 4718592 | tf_op jit(solution)/shard_map/reduce_scatter | solution.py:152
  472.1 22.1 %copy-start.9 = (f32[256,1024]{1,0:T(8,128)S(1)}, f32[256,1024]{1,0:T(8,128)}, u32[]{:S(2)}) copy-start(f32[256,1024]{1,0:T(8,128)} %all-reduce.11.cloned.1.call-done) | copy-start | bytes 3145732
Sparse Core Ops, SparseCore 0:
  10.6 48.0 all-gather.3
  118.0 40.1 all-reduce.4
  160.5 51.4 all-gather.7
  214.1 47.4 all-gather.5
  267.8 34.5 all-reduce.8
  305.2 33.5 all-reduce.6
  416.0 41.5 all-reduce.10
  461.0 53.8 reduce-scatter.9
  519.3 62.8 reduce-scatter.7
  586.3 74.0 reduce-scatter.5
  664.6 87.1 reduce-scatter.11
  756.3 88.2 reduce-scatter.13

commit v2 on v1

--- a/solution.py
+++ b/solution.py
@@ -1,6 +1,8 @@
 import jax
 import jax.numpy as jnp
 from jax import lax
+from jax.experimental import pallas as pl
+from jax.experimental.pallas import tpu as pltpu
 from jax.sharding import PartitionSpec as P
 
 HEAD_DIM = 64
@@ -157,6 +159,630 @@
     )
 
 
+MESH = pl.DeviceIdType.MESH
+SEQ = 8
+HEAD = 4
+LINE = 4
+VMEM_BYTES = 60 * 1024 * 1024
+
+
+def al(value, multiple):
+    return pl.multiple_of(value, multiple)
+
+
+def fused_kernel(
+    units, pads, picks, tok, cot, wq, wo, wu, wd, vec, upb,
+    out_o, xg_o, gq_o, go_o, gu_o, gd_o, small_o, upbg_o,
+    wq_all, wo_all, wu_all, wd_all, gains, normed, qs, kv_all, kwin, vwin, lg, prob, prob_low, ds,
+    att, att_low, n2, hid, dgelu, gp, gb, xgb, mid_own, gm_own, gatt, dq, dk, dv, dkv_pad, dkv_send,
+    dkv_recv, gt, part_send, part_recv, sum_f, cnt,
+    sq, so, su, sd, aq, ao, au, ad, bq, bo, bu, bd, rq, ro, ru, rd,
+    sm_send, sm_recv, sm_own, sm_two, up_send, up_recv,
+    g_ss, g_rs, v_ss, v_rs, kv_ss, kv_rs, dkv_ss, dkv_rs, rs_ss, rs_rs, ag_ss, ag_rs,
+    ra_ss, ra_rs, rb_ss, rb_rs, sm_ss, sm_rs, sm2_ss, sm2_rs, up_ss, up_rs,
+):
+    s = lax.axis_index("seq")
+    h = lax.axis_index("head")
+    z, y = lax.div(s, 2), lax.rem(s, 2)
+    mate = z * 2 + 1 - y
+    tokens = tok.shape[0]
+    quarter = tokens // HEAD
+    head_w = qs.shape[1]
+    width = tok.shape[1]
+
+    def copy(src, dst, ss, rs, **where):
+        return pltpu.make_async_remote_copy(
+            src_ref=src, dst_ref=dst, send_sem=ss, recv_sem=rs, device_id=where,
+            device_id_type=MESH,
+        )
+
+    barrier = pltpu.get_barrier_semaphore()
+    for d in range(1, SEQ):
+        pl.semaphore_signal(
+            barrier, inc=1, device_id={"seq": lax.rem(s + d, SEQ)}, device_id_type=MESH
+        )
+    for d in range(1, HEAD):
+        pl.semaphore_signal(
+            barrier, inc=1, device_id={"head": lax.rem(h + d, HEAD)}, device_id_type=MESH
+        )
+    for k in range(2 * SPAN - 1):
+        other = s + k - (SPAN - 1)
+
+        @pl.when((other < 0) | (other >= SEQ))
+        def _():
+            kv_all[k] = jnp.zeros(kv_all.shape[1:], BF16)
+            dkv_recv[k] = jnp.zeros(dkv_recv.shape[1:], BF16)
+
+    pl.semaphore_wait(barrier, SEQ - 1 + HEAD - 1)
+
+    shard = [wq, wo, wu, wd]
+    d_rows = wq.shape[0]
+    slot = [
+        lambda o: wq_all.at[pl.ds(al(o * d_rows, d_rows), d_rows), :],
+        lambda o: wo_all.at[:, pl.ds(al(o * d_rows, d_rows), d_rows)],
+        lambda o: wu_all.at[pl.ds(al(o * d_rows, d_rows), d_rows), :],
+        lambda o: wd_all.at[:, pl.ds(al(o * d_rows, d_rows), d_rows)],
+    ]
+
+    def own_shard(w):
+        here = slot[w](s)
+        here[...] = shard[w][...]
+
+    def line_copy(w, d):
+        to = lax.rem(z + d, LINE) * 2 + y
+        return copy(shard[w], slot[w](s), g_ss.at[w, d - 1], g_rs.at[w, s], seq=to)
+
+    def mate_copy(w):
+        return copy(shard[w], slot[w](s), g_ss.at[w, 3], g_rs.at[w, s], seq=mate)
+
+    def forward_copy(w, d):
+        o = lax.rem(z + LINE - d, LINE) * 2 + y
+        return copy(slot[w](o), slot[w](o), g_ss.at[w, 3 + d], g_rs.at[w, o], seq=mate)
+
+    def gather_start(w):
+        mate_copy(w).start()
+        for d in range(1, LINE):
+            line_copy(w, d).start()
+
+    def gather_forward(w):
+        for d in range(1, LINE):
+            o = lax.rem(z + LINE - d, LINE) * 2 + y
+            copy(shard[w], slot[w](o), g_ss.at[w, d - 1], g_rs.at[w, o], seq=mate).wait_recv()
+            forward_copy(w, d).start()
+
+    def gather_finish(w):
+        for d in range(LINE):
+            o = lax.rem(z + d, LINE) * 2 + 1 - y
+            copy(shard[w], slot[w](o), g_ss.at[w, 3], g_rs.at[w, o], seq=mate).wait_recv()
+
+    def gather_drain(w):
+        for d in range(1, LINE):
+            line_copy(w, d).wait_send()
+            forward_copy(w, d).wait_send()
+        mate_copy(w).wait_send()
+
+    def vec_copy(d):
+        to = lax.rem(s + d, SEQ)
+        return copy(
+            vec, gains.at[:, pl.ds(al(s * d_rows, d_rows), d_rows)], v_ss.at[d - 1], v_rs.at[s],
+            seq=to,
+        )
+
+    for d in range(1, SEQ):
+        vec_copy(d).start()
+    gather_start(0)
+    gather_start(1)
+    for w in range(4):
+        own_shard(w)
+    gains[:, pl.ds(al(s * d_rows, d_rows), d_rows)] = vec[...]
+
+    start, leader, span, pad = 0, 0, 0, 0
+    for k in range(units.shape[0]):
+        here = units[k]
+        inside = (s >= start) & (s < start + here)
+        leader = jnp.where(inside, start, leader)
+        span = jnp.where(inside, here, span)
+        pad = jnp.where(inside, pads[k], pad)
+        start = start + here
+    position = s - leader
+    root = jnp.clip(SPAN - 1 - position, 0, SPAN - 1)
+    total = span * BLK_DEV
+    live = span * tokens - pad
+
+    for d in range(1, SEQ):
+        o = lax.rem(s + d, SEQ)
+        copy(
+            vec, gains.at[:, pl.ds(al(o * d_rows, d_rows), d_rows)], v_ss.at[0], v_rs.at[o],
+            seq=mate,
+        ).wait_recv()
+    for c in range(HEAD):
+        r = pl.ds(c * quarter, quarter)
+        xhat, _ = norm_parts(tok[r, :].astype(F32))
+        normed[r, :] = (xhat * gains[0:1, :] + gains[1:2, :]).astype(BF16)
+    gather_forward(0)
+    gather_finish(0)
+    gather_start(2)
+    gather_start(3)
+    scaling = HEAD_DIM ** (-0.5)
+    for c in range(3):
+        r = pl.ds(c * head_w, head_w)
+        part = dot(normed[...], wq_all[:, r], ((1,), (0,)))
+        if c == 0:
+            qs[...] = (part.astype(BF16).astype(F32) * scaling).astype(BF16)
+        else:
+            kv_all[SPAN - 1, :, pl.ds((c - 1) * head_w, head_w)] = part.astype(BF16)
+
+    def near(k, then):
+        other = s + k - (SPAN - 1)
+        if k != SPAN - 1:
+            pl.when((other >= 0) & (other < SEQ))(lambda: then(other))
+
+    def kv_copy(k, other):
+        back = 2 * (SPAN - 1) - k
+        return copy(
+            kv_all.at[SPAN - 1], kv_all.at[back], kv_ss.at[k], kv_rs.at[back], seq=other
+        )
+
+    def kv_arrival(k, other):
+        return copy(kv_all.at[SPAN - 1], kv_all.at[k], kv_ss.at[k], kv_rs.at[k], seq=other)
+
+    for k in range(2 * SPAN - 1):
+        near(k, lambda other, k=k: kv_copy(k, other).start())
+
+    columns = lax.broadcasted_iota(jnp.int32, (1, SPAN * tokens), 1)
+    usable = columns < live
+    blocks = lax.div(columns, BLK)
+    for hh in range(HEAD):
+        for b in range(BLK_DEV):
+            query = position * BLK_DEV + b
+            count = jnp.zeros((1, SPAN * tokens), F32)
+            for wanted in (query - 1, query, query + 1, 0, total - 1):
+                count = count + jnp.where(blocks == wanted, 1.0, 0.0)
+            for r in range(picks.shape[2]):
+                raw = picks[b, hh, r]
+                chosen = lax.rem(raw, BLK_DEV)
+                for units_held in range(2, SPAN + 1):
+                    chosen = jnp.where(
+                        span == units_held, lax.rem(raw, BLK_DEV * units_held), chosen
+                    )
+                count = count + jnp.where(blocks == chosen, 1.0, 0.0)
+            edge = (query == 0) | (query == total - 1)
+            count = jnp.where(edge, 1.0, count)
+            cnt[hh, b : b + 1, :] = jnp.where(usable, count, 0.0)
+
+    for k in range(2 * SPAN - 1):
+        near(k, lambda other, k=k: kv_arrival(k, other).wait_recv())
+    for j in range(SPAN):
+        part = kv_all[root + j]
+        kwin[pl.ds(j * tokens, tokens), :] = part[:, :head_w]
+        vwin[pl.ds(j * tokens, tokens), :] = part[:, head_w:]
+    gather_forward(1)
+
+    lanes = lax.div(lax.broadcasted_iota(jnp.int32, (1, head_w), 1), HEAD_DIM)
+
+    att[...] = jnp.zeros(att.shape, F32)
+
+    def attend(hh, carry):
+        mine = lanes == hh
+        query = jnp.where(mine, qs[...], jnp.zeros((), BF16))
+        for j in range(SPAN):
+            c = pl.ds(j * tokens, tokens)
+            lg[:, c] = dot(query, kwin[c, :], ((1,), (1,)))
+        for b in range(BLK_DEV):
+            r = pl.ds(b * BLK, BLK)
+            count = cnt[hh, b : b + 1, :]
+            logits = jnp.where(count > 0, lg[r, :], NEGATIVE)
+            grown = jnp.exp(logits - jnp.max(logits, axis=-1, keepdims=True)) * count
+            chance = grown / jnp.sum(grown, axis=-1, keepdims=True)
+            prob[hh, r, :] = chance
+            prob_low[hh, r, :] = chance.astype(BF16)
+        part = dot(prob_low[hh], vwin[...], ((1,), (0,)))
+        att[...] += jnp.where(mine, part, 0.0)
+        return carry
+
+    lax.fori_loop(0, HEAD, attend, 0)
+    att_low[...] = att[...].astype(BF16)
+    gather_finish(1)
+
+    def rows_of(k):
+        return pl.ds(al(k * quarter, quarter), quarter)
+
+    def rs_copy(op, d):
+        to = lax.rem(h + d, HEAD)
+        return copy(
+            part_send.at[op, rows_of(to), :], part_recv.at[op, h], rs_ss.at[op, d],
+            rs_rs.at[op, h], head=to,
+        )
+
+    def reduce_start(op):
+        part_send[op] = sum_f[...].astype(BF16)
+        for d in range(1, HEAD):
+            rs_copy(op, d).start()
+
+    def reduce_finish(op):
+        result = sum_f[rows_of(h), :]
+        for d in range(1, HEAD):
+            o = lax.rem(h + d, HEAD)
+            copy(
+                part_send.at[op, rows_of(o), :], part_recv.at[op, o], rs_ss.at[op, d],
+                rs_rs.at[op, o], head=o,
+            ).wait_recv()
+            result = result + part_recv[op, o].astype(F32)
+        return result
+
+    def ag_copy(op, whole, d):
+        to = lax.rem(h + d, HEAD)
+        return copy(
+            whole.at[rows_of(h), :], whole.at[rows_of(h), :], ag_ss.at[op, d], ag_rs.at[op, h],
+            head=to,
+        )
+
+    def spread_start(op, whole, value):
+        whole[rows_of(h), :] = value
+        for d in range(1, HEAD):
+            ag_copy(op, whole, d).start()
+
+    def spread_finish(op, whole):
+        for d in range(1, HEAD):
+            o = lax.rem(h + d, HEAD)
+            copy(
+                whole.at[rows_of(o), :], whole.at[rows_of(o), :], ag_ss.at[op, d],
+                ag_rs.at[op, o], head=o,
+            ).wait_recv()
+
+    def tiled(n, body):
+        def step(j, carry):
+            body(al(j * 256, 256))
+            return carry
+
+        lax.fori_loop(0, n // 256, step, 0)
+
+    def out_tile(c):
+        sum_f[:, pl.ds(c, 256)] = dot(att_low[...], wo_all[:, pl.ds(c, 256)], ((1,), (0,)))
+
+    tiled(width, out_tile)
+    reduce_start(0)
+    gather_forward(2)
+    gather_forward(3)
+    middle = tok[rows_of(h), :].astype(F32) + reduce_finish(0)
+    mid_own[...] = middle
+    xhat, _ = norm_parts(middle)
+    spread_start(0, n2, (xhat * gains[2:3, :] + gains[3:4, :]).astype(BF16))
+    gather_finish(2)
+    gather_finish(3)
+    spread_finish(0, n2)
+
+    root_c = (2.0 / 3.141592653589793) ** 0.5
+
+    def ffn_tile(c):
+        f = pl.ds(c, 256)
+        v = dot(n2[...], wu_all[:, f], ((1,), (0,))) + upb[:, f].astype(F32)
+        t = jnp.tanh(root_c * (v + 0.044715 * (v * v * v)))
+        hid[:, f] = (0.5 * v * (1.0 + t)).astype(BF16)
+        slope = 0.5 * (1.0 + t) + 0.5 * v * (1.0 - t * t) * (root_c * (1.0 + 0.134145 * v * v))
+        low = (dot(cot[...], wd_all[f, :], ((1,), (1,))) * slope).astype(BF16)
+        gp[:, f] = low
+        up_send[:, f] = jnp.broadcast_to(
+            jnp.sum(low.astype(F32), axis=0, keepdims=True), (8, 256)
+        )
+
+    tiled(wu_all.shape[1], ffn_tile)
+
+    def gn2_tile(c):
+        sum_f[:, pl.ds(c, 256)] = dot(gp[...], wu_all[pl.ds(c, 256), :], ((1,), (1,)))
+
+    tiled(width, gn2_tile)
+    reduce_start(1)
+
+    def up_copy(d):
+        to = lax.rem(s + d, SEQ)
+        return copy(up_send, up_recv.at[s], up_ss.at[d], up_rs.at[s], seq=to)
+
+    for d in range(1, SEQ):
+        up_copy(d).start()
+
+    send = [sq, so, su, sd]
+    arrive = [aq, ao, au, ad]
+    again = [bq, bo, bu, bd]
+    final = [rq, ro, ru, rd]
+    grads = [gq_o, go_o, gu_o, gd_o]
+
+    def cross_copy(w, zz):
+        return copy(
+            send[w].at[zz * 2 + 1 - y], arrive[w].at[zz], ra_ss.at[w, zz], ra_rs.at[w, zz],
+            seq=mate,
+        )
+
+    def along_copy(w, d):
+        zz = lax.rem(z + d, LINE)
+        return copy(
+            again[w].at[zz], final[w].at[z], rb_ss.at[w, zz], rb_rs.at[w, z], seq=zz * 2 + y
+        )
+
+    def grad_along(w):
+        for d in range(1, LINE):
+            zz = lax.rem(z + d, LINE)
+            cross_copy(w, zz).wait_recv()
+            mine = send[w][zz * 2 + y].astype(F32) + arrive[w][zz].astype(F32)
+            again[w][zz] = mine.astype(BF16)
+            along_copy(w, d).start()
+
+    def grad_finish(w):
+        cross_copy(w, z).wait_recv()
+        result = send[w][z * 2 + y].astype(F32) + arrive[w][z].astype(F32)
+        for d in range(1, LINE):
+            o = lax.rem(z + d, LINE)
+            copy(
+                again[w].at[o], final[w].at[o], rb_ss.at[w, o], rb_rs.at[w, o], seq=mate
+            ).wait_recv()
+            result = result + final[w][o].astype(F32)
+        grads[w][...] = result
+
+    def grad_drain(w):
+        for zz in range(LINE):
+            cross_copy(w, zz).wait_send()
+        for d in range(1, LINE):
+            along_copy(w, d).wait_send()
+
+    def down_step(zz, carry):
+        c = al(zz * 256, 256)
+        part = dot(hid[...], cot[:, pl.ds(c, 256)], ((0,), (0,))).astype(BF16)
+        sd[zz * 2] = part[:, :d_rows]
+        sd[zz * 2 + 1] = part[:, d_rows:]
+        cross_copy(3, zz).start()
+        return carry
+
+    def up_step(zz, carry):
+        c = al(zz * 256, 256)
+        part = dot(n2[:, pl.ds(c, 256)], gp[...], ((0,), (0,))).astype(BF16)
+        su[zz * 2] = part[:d_rows]
+        su[zz * 2 + 1] = part[d_rows:]
+        cross_copy(2, zz).start()
+        return carry
+
+    lax.fori_loop(0, LINE, down_step, 0)
+    lax.fori_loop(0, LINE, up_step, 0)
+
+    grad_two = reduce_finish(1)
+    xhat, inverse = norm_parts(mid_own[...])
+    dy = cot[rows_of(h), :].astype(F32)
+    sm_send[2:3, :] = jnp.sum(grad_two * xhat, axis=0, keepdims=True)
+    sm_send[3:4, :] = jnp.sum(grad_two, axis=0, keepdims=True)
+    sm_send[4:5, :] = jnp.sum(dy, axis=0, keepdims=True)
+    sm_send[5:8, :] = jnp.zeros((3, width), F32)
+    grad_mid = dy + norm_backward(xhat, inverse, grad_two * gains[2:3, :])
+    gm_own[...] = grad_mid
+    spread_start(1, gb, grad_mid.astype(BF16))
+
+    def down_tile(c):
+        sum_f[:, pl.ds(c, 256)] = dot(hid[...], wd_all[:, pl.ds(c, 256)], ((1,), (0,)))
+
+    tiled(width, down_tile)
+    reduce_start(2)
+    grad_along(3)
+    spread_finish(1, gb)
+
+    def wo_step(zz, carry):
+        c = al(zz * 256, 256)
+        part = dot(att_low[...], gb[:, pl.ds(c, 256)], ((0,), (0,))).astype(BF16)
+        so[zz * 2] = part[:, :d_rows]
+        so[zz * 2 + 1] = part[:, d_rows:]
+        cross_copy(1, zz).start()
+        return carry
+
+    gatt[...] = dot(gb[...], wo_all[...], ((1,), (1,))).astype(BF16)
+    lax.fori_loop(0, LINE, wo_step, 0)
+    ffn = reduce_finish(2)
+    spread_start(2, out_o, (mid_own[...] + ffn + gains[4:5, :]).astype(BF16))
+
+    dq[...] = jnp.zeros(dq.shape, F32)
+    dk[...] = jnp.zeros(dk.shape, F32)
+    dv[...] = jnp.zeros(dv.shape, F32)
+
+    def attend_back(hh, carry):
+        mine = lanes == hh
+        none = jnp.zeros((), BF16)
+        query = jnp.where(mine, qs[...], none)
+        grad = jnp.where(mine, gatt[...], none)
+        for j in range(SPAN):
+            c = pl.ds(j * tokens, tokens)
+            lg[:, c] = dot(grad, vwin[c, :], ((1,), (1,)))
+        for b in range(BLK_DEV):
+            r = pl.ds(b * BLK, BLK)
+            chance, grown = prob[hh, r, :], lg[r, :]
+            inner = jnp.sum(chance * grown, axis=-1, keepdims=True)
+            ds[r, :] = (chance * (grown - inner)).astype(BF16)
+        dq[...] += jnp.where(mine, dot(ds[...], kwin[...], ((1,), (0,))), 0.0)
+        for j in range(SPAN):
+            c = pl.ds(j * tokens, tokens)
+            dk[c, :] += dot(ds[:, c], query, ((0,), (0,)))
+            dv[c, :] += dot(prob_low[hh, :, c], grad, ((0,), (0,)))
+        return carry
+
+    lax.fori_loop(0, HEAD, attend_back, 0)
+    for k in range(2 * (SPAN - 1) + SPAN):
+        j = k - (SPAN - 1)
+        if 0 <= j < SPAN:
+            c = pl.ds(j * tokens, tokens)
+            dkv_pad[k, :, :head_w] = dk[c, :].astype(BF16)
+            dkv_pad[k, :, head_w:] = dv[c, :].astype(BF16)
+        else:
+            dkv_pad[k] = jnp.zeros(dkv_pad.shape[1:], BF16)
+
+    def dkv_copy(k, other):
+        back = 2 * (SPAN - 1) - k
+        return copy(
+            dkv_send.at[k], dkv_recv.at[back], dkv_ss.at[k], dkv_rs.at[back], seq=other
+        )
+
+    def dkv_arrival(k, other):
+        return copy(dkv_send.at[k], dkv_recv.at[k], dkv_ss.at[k], dkv_rs.at[k], seq=other)
+
+    for k in range(2 * SPAN - 1):
+        dkv_send[k] = dkv_pad[k + SPAN - 1 - root]
+        near(k, lambda other, k=k: dkv_copy(k, other).start())
+
+    gt[:, :head_w] = (dq[...] * scaling).astype(BF16)
+    grad_along(2)
+    grad_along(1)
+    for k in range(2 * SPAN - 1):
+        near(k, lambda other, k=k: dkv_arrival(k, other).wait_recv())
+    whole = dkv_send[SPAN - 1].astype(F32)
+    for k in range(2 * SPAN - 1):
+        if k != SPAN - 1:
+            whole = whole + dkv_recv[k].astype(F32)
+    gt[:, head_w:] = whole.astype(BF16)
+
+    def gn1_tile(c):
+        sum_f[:, pl.ds(c, 256)] = dot(gt[...], wq_all[pl.ds(c, 256), :], ((1,), (1,)))
+
+    tiled(width, gn1_tile)
+    reduce_start(3)
+
+    def wq_step(zz, carry):
+        c = al(zz * 256, 256)
+        part = dot(normed[:, pl.ds(c, 256)], gt[...], ((0,), (0,))).astype(BF16)
+        sq[zz * 2] = part[:d_rows]
+        sq[zz * 2 + 1] = part[d_rows:]
+        cross_copy(0, zz).start()
+        return carry
+
+    lax.fori_loop(0, LINE, wq_step, 0)
+    grad_one = reduce_finish(3)
+    xhat, inverse = norm_parts(tok[rows_of(h), :].astype(F32))
+    sm_send[0:1, :] = jnp.sum(grad_one * xhat, axis=0, keepdims=True)
+    sm_send[1:2, :] = jnp.sum(grad_one, axis=0, keepdims=True)
+
+    def small_copy(d):
+        to = lax.rem(s + d, SEQ)
+        return copy(
+            sm_send.at[:, pl.ds(al(to * d_rows, d_rows), d_rows)], sm_recv.at[s], sm_ss.at[d],
+            sm_rs.at[s], seq=to,
+        )
+
+    for d in range(1, SEQ):
+        small_copy(d).start()
+    grad_x = gm_own[...] + norm_backward(xhat, inverse, grad_one * gains[0:1, :])
+    spread_start(3, xgb, grad_x.astype(BF16))
+    grad_along(0)
+
+    sm_recv[s] = sm_send[:, pl.ds(al(s * d_rows, d_rows), d_rows)]
+    up_recv[s] = up_send[...]
+    for d in range(1, SEQ):
+        o = lax.rem(s + d, SEQ)
+        copy(
+            sm_send.at[:, pl.ds(0, d_rows)], sm_recv.at[o], sm_ss.at[d], sm_rs.at[o], seq=o
+        ).wait_recv()
+        copy(up_send, up_recv.at[o], up_ss.at[d], up_rs.at[o], seq=o).wait_recv()
+    part, ups = sm_recv[0], up_recv[0]
+    for o in range(1, SEQ):
+        part, ups = part + sm_recv[o], ups + up_recv[o]
+    upbg_o[...] = ups
+    sm_own[...] = part
+
+    def two_copy(d):
+        to = lax.rem(h + d, HEAD)
+        return copy(sm_own, sm_two.at[h], sm2_ss.at[d], sm2_rs.at[h], head=to)
+
+    for d in range(1, HEAD):
+        two_copy(d).start()
+    sm_two[h] = part
+    for w in (3, 2, 1):
+        grad_finish(w)
+    spread_finish(2, out_o)
+    spread_finish(3, xgb)
+    xg_o[...] = xgb[...].astype(F32)
+    for d in range(1, HEAD):
+        o = lax.rem(h + d, HEAD)
+        copy(sm_own, sm_two.at[o], sm2_ss.at[d], sm2_rs.at[o], head=o).wait_recv()
+    small_o[...] = (sm_two[0] + sm_two[1]) + (sm_two[2] + sm_two[3])
+    grad_finish(0)
+
+    for w in range(4):
+        gather_drain(w)
+        grad_drain(w)
+    for d in range(1, SEQ):
+        vec_copy(d).wait_send()
+        up_copy(d).wait_send()
+        small_copy(d).wait_send()
+    for k in range(2 * SPAN - 1):
+        near(k, lambda other, k=k: kv_copy(k, other).wait_send())
+        near(k, lambda other, k=k: dkv_copy(k, other).wait_send())
+    for d in range(1, HEAD):
+        two_copy(d).wait_send()
+        for op, ref in enumerate((n2, gb, out_o, xgb)):
+            rs_copy(op, d).wait_send()
+            ag_copy(op, ref, d).wait_send()
+
+
+def local_fused(
+    tokens, w_qkv, w_out, ln1_gain, ln1_bias, ln2_gain, ln2_bias, w_up, up_bias, w_down, down_bias,
+    seq_units, seq_pad, rand_picks, cotangent,
+):
+    tok, width = tokens.shape
+    rows, _, head_w = w_qkv.shape
+    hidden = w_up.shape[1]
+    vectors = jnp.stack([ln1_gain, ln1_bias, ln2_gain, ln2_bias, down_bias], axis=0)
+    vectors = jnp.pad(vectors.astype(F32), ((0, 3), (0, 0)))
+    near = 2 * SPAN - 1
+    quarter = tok // HEAD
+    v = pltpu.VMEM
+    dma = pltpu.SemaphoreType.DMA
+    shards = [(rows, 3 * head_w), (head_w, rows), (rows, hidden), (hidden, rows)]
+    scratch = [
+        v((width, 3 * head_w), BF16), v((head_w, width), BF16), v((width, hidden), BF16),
+        v((hidden, width), BF16), v((8, width), F32), v((tok, width), BF16),
+        v((tok, head_w), BF16), v((near, tok, 2 * head_w), BF16), v((SPAN * tok, head_w), BF16),
+        v((SPAN * tok, head_w), BF16), v((tok, SPAN * tok), F32), v((HEAD, tok, SPAN * tok), F32),
+        v((HEAD, tok, SPAN * tok), BF16), v((tok, SPAN * tok), BF16),
+        v((tok, head_w), F32), v((tok, head_w), BF16), v((tok, width), BF16),
+        v((tok, hidden), BF16), v((8, 128), F32), v((tok, hidden), BF16), v((tok, width), BF16),
+        v((tok, width), BF16), v((quarter, width), F32), v((quarter, width), F32),
+        v((tok, head_w), BF16), v((tok, head_w), F32), v((SPAN * tok, head_w), F32),
+        v((SPAN * tok, head_w), F32), v((near + SPAN - 1, tok, 2 * head_w), BF16),
+        v((near, tok, 2 * head_w), BF16), v((near, tok, 2 * head_w), BF16),
+        v((tok, 3 * head_w), BF16), v((4, tok, width), BF16), v((4, HEAD, quarter, width), BF16),
+        v((tok, width), F32), v((HEAD, 8, SPAN * tok), F32),
+    ]
+    for lead in (SEQ, LINE, LINE, LINE):
+        scratch += [v((lead,) + shape, BF16) for shape in shards]
+    scratch += [
+        v((8, width), F32), v((SEQ, 8, rows), F32), v((8, rows), F32), v((HEAD, 8, rows), F32),
+        v((8, hidden), F32), v((SEQ, 8, hidden), F32),
+    ]
+    scratch += [
+        dma(shape)
+        for shape in (
+            (4, 7), (4, SEQ), (7,), (SEQ,), (near,), (near,), (near,), (near,),
+            (4, HEAD), (4, HEAD), (4, HEAD), (4, HEAD), (4, LINE), (4, LINE), (4, LINE), (4, LINE),
+            (SEQ,), (SEQ,), (HEAD,), (HEAD,), (SEQ,), (SEQ,),
+        )
+    ]
+    outs = [
+        ((tok, width), BF16), ((tok, width), F32), (shards[0], F32), (shards[1], F32),
+        (shards[2], F32), (shards[3], F32), ((8, rows), F32), ((8, hidden), F32),
+    ]
+    smem, vmem = pl.BlockSpec(memory_space=pltpu.SMEM), pl.BlockSpec(memory_space=pltpu.VMEM)
+    out, xg, gq, go, gu, gd, small, upg = pl.pallas_call(
+        fused_kernel,
+        out_shape=[jax.ShapeDtypeStruct(*o) for o in outs],
+        in_specs=[smem] * 3 + [vmem] * 8,
+        out_specs=[vmem] * 8,
+        scratch_shapes=scratch,
+        compiler_params=pltpu.CompilerParams(
+            collective_id=0, has_side_effects=True, vmem_limit_bytes=VMEM_BYTES
+        ),
+        name="fused_layer",
+    )(
+        seq_units, seq_pad, rand_picks, tokens, cotangent, w_qkv.reshape(rows, 3 * head_w), w_out,
+        w_up, w_down, vectors, up_bias.reshape(1, hidden),
+    )
+    return (
+        out, xg, gq.reshape(rows, 3, head_w), go, small[0], small[1], small[2], small[3], gu,
+        upg[0], gd, small[4],
+    )
+
+
 IN_SPECS = (
     P("seq", None), P("seq", None, "head"), P("head", "seq"), P("seq"), P("seq"), P("seq"),
     P("seq"), P("seq", "head"), P("head"), P("head", "seq"), P("seq"), P(), P(),
@@ -169,6 +795,8 @@
 
 
 def solution(mesh):
+    fits = mesh.shape["seq"] == SEQ and mesh.shape["head"] == HEAD
     return jax.shard_map(
-        local_general, mesh=mesh, in_specs=IN_SPECS, out_specs=OUT_SPECS, check_vma=False
+        local_fused if fits else local_general, mesh=mesh, in_specs=IN_SPECS,
+        out_specs=OUT_SPECS, check_vma=False,
     )

time: 853 us -> 268 us (0.31)
  waiting for transfers between devices: 636 us -> 0 us
  Pallas kernels: 0 us -> 253 us
  blocking collectives: 77.8 us -> 0 us
  matrix products: 35.6 us -> 0 us
  starting transfers between devices: 29.3 us -> 0 us
  between operations: 24.6 us -> 0.74 us
  other arithmetic: 18.9 us -> 0.6 us
  local copies, waits for them, and re-layouts: 29.2 us -> 13.1 us
    reduce_scatter x5 -> x0, waiting for transfers between devices: 348 us -> none  [local_general(): lax.psum_scatter(v, 'seq', scatter_dimension=d, tiled=True)]
    pallas_call x0 -> x1, Pallas kernels: none -> 253 us  [local_fused(): pl.pallas_call(fused_kernel, out_shape=[jax.ShapeDtypeStruct(*o) for o in...]
    psum x4 -> x0, waiting for transfers between devices: 146 us -> none  [the longest x1 41.7 us: local_general(): lax.psum(jnp.einsum('tcf,dcf->td', grad_triple, qkv, preferred_element_ty...]
    all_gather x3 -> x0, waiting for transfers between devices: 98.5 us -> none  [the longest x1 52.1 us: local_general(): cols = lambda v: lax.all_gather(v, 'seq', axis=1, tiled=True)]
    all_gather x2 -> x0, blocking collectives: 55.7 us -> none  [local_general(): cols = lambda v: lax.all_gather(v, 'seq', axis=1, tiled=True)]
    ppermute x12 -> x0, waiting for transfers between devices: 42.2 us -> none  [shifted(): lax.ppermute(value, axis, [(i, i + steps) for i in range(first, last)])]
    dot_general x18 -> x0, matrix products: 35.6 us -> none  [the longest x9 20.3 us: dot(): return lax.dot_general(a, b, (dims, ((), ())), preferred_element_type=F32)]
    ppermute x12 -> x0, starting transfers between devices: 28.6 us -> none  [shifted(): lax.ppermute(value, axis, [(i, i + steps) for i in range(first, last)])]
  transfers between devices with their start and end apart: 24 -> 0, of which waited for: 17 -> 0; matrix products, arithmetic and copies ran while one was open for 4% -> 0% of each run, Pallas kernels for 0% -> 0%
where the time goes in v2:
time: 268 us
  Pallas kernels  253 us (94%)
  local copies, waits for them, and re-layouts  13.1 us (5%)
    pallas_call x1, Pallas kernels, local_fused(): pl.pallas_call(fused_kernel, out_shape=[jax.ShapeDtypeStruct(*o) for o in...  253 us
    unnamed x34, local copies, waits for them, and re-layouts  8.58 us

profile of v2, /device:TPU:0, one launch (start us, length us, event | category | flops | bytes accessed | tf_op | source)
XLA Modules:
  0.0 267.8 jit_solution(5906177026113195653)
XLA Ops:
  0.6 0.0 copy-start.11
  0.7 0.0 copy-start.12
  0.7 0.0 copy-start.8
  0.7 0.0 copy-start.9
  0.7 0.0 copy-start.10
  0.7 0.6 copy-done.11
  1.3 0.0 copy-done.12
  1.3 0.0 copy-done.8
  1.3 0.0 copy-done.9
  1.3 0.0 copy-done.10
  1.4 0.0 copy-start.6
  1.4 0.0 copy-start.5
  1.4 0.6 pad_convert_fusion.vec
  2.0 0.0 copy-done.6
  2.0 0.6 reshape.34.upb
  2.6 0.0 copy-done.5
  2.6 0.7 copy.31.picks
  3.3 1.1 copy.30
  4.4 0.8 copy.32.wq
  5.3 253.3 %fused_layer.1 = (bf16[256,1024]{1,0:T(8,128)(2,1)}, f32[256,1024]{1,0:T(8,128)}, f32[128,768]{1,0:T(8,128)}, f32[256,128]{1,0:T(8,128)}, f32[128,1024]{1,0:T(8,...) custom-call(s32[4]{0:T(128)} %units.1, s32[4]{0:T(128)} %pads.1, s32[4,4,3]{2,1,0:T(4,128)} %copy.31.picks, ...), custom_call_target="tpu_custom_call" | custom-call | tf_op jit(solution)/shard_map/fused_layer/pallas_call | solution.py:766
  258.6 0.0 copy-start.7
  258.6 0.7 copy-done.7
  259.3 0.5 slice_bitcast_fusion
  259.8 1.4 slice.22
  261.1 0.0 copy-start.3
  261.1 1.2 copy.33
  262.4 0.0 copy-start
  262.4 0.9 copy.34
  263.3 0.0 copy-done.3
  263.3 0.8 copy.40
  264.1 0.0 copy-done
  264.1 0.0 copy-start.4
  264.1 0.0 copy-start.2
  264.1 1.0 copy.41
  265.1 0.0 copy-done.4
  265.1 0.7 copy.42
  265.7 0.0 copy-done.2
  265.7 0.0 copy-start.1
  265.7 0.8 copy.43
  266.5 0.4 copy-done.1
  267.0 0.8 copy.44
  (1 shorter events, 0.0 us)
Async XLA Ops:
  0.6 0.7 copy-start.11
  0.7 0.7 copy-start.12
  0.7 0.7 copy-start.8
  0.7 0.7 copy-start.9
  0.7 0.7 copy-start.10
  1.4 0.7 copy-start.6
  1.4 1.2 copy-start.5
  258.6 0.7 copy-start.7
  261.1 2.1 copy-start.3
  262.4 1.7 copy-start
  264.1 1.0 copy-start.4
  264.1 1.7 copy-start.2
  265.7 1.2 copy-start.1

commit v3 on v1

--- a/solution.py
+++ b/solution.py
@@ -1,6 +1,11 @@
+import functools
+import types
+
 import jax
 import jax.numpy as jnp
 from jax import lax
+from jax.experimental import pallas as pl
+from jax.experimental.pallas import tpu as pltpu
 from jax.sharding import PartitionSpec as P
 
 HEAD_DIM = 64
@@ -157,6 +162,721 @@
     )
 
 
+MESH = pl.DeviceIdType.MESH
+SEQ = 8
+HEAD = 4
+LINE = 4
+NEAR = 2 * SPAN - 1
+QKV_KV, QKV_Q, OUT, UP, DOWN = range(5)
+VMEM_BYTES = 60 * 1024 * 1024
+
+
+def al(value, multiple):
+    return pl.multiple_of(value, multiple)
+
+
+def fused_kernel(names, *refs):
+    r = types.SimpleNamespace(**dict(zip(names, refs)))
+    s, h = lax.axis_index("seq"), lax.axis_index("head")
+    z, y, x, c = lax.div(s, 2), lax.rem(s, 2), lax.div(h, 2), lax.rem(h, 2)
+    e = lax.rem(z, 2)
+    pair_z = z + 1 - 2 * e
+    mate = z * 2 + 1 - y
+    pair = pair_z * 2 + y
+    twin = x * 2 + 1 - c
+    across = (1 - x) * 2 + c
+    tokens, width = r.tok.shape
+    quarter = tokens // HEAD
+    head_w = r.qs.shape[1]
+    rows = r.wq.shape[1]
+    half = r.wu_all.shape[1]
+    sent = []
+
+    def copy(src, dst, ss, rs, **where):
+        return pltpu.make_async_remote_copy(
+            src_ref=src, dst_ref=dst, send_sem=ss, recv_sem=rs, device_id=where,
+            device_id_type=MESH,
+        )
+
+    def when(cond, then):
+        if cond is None:
+            then()
+        else:
+            pl.when(cond)(lambda: then())
+
+    def send(cond, *args, **where):
+        one = copy(*args, **where)
+        when(cond, one.start)
+        sent.append((cond, one))
+
+    def arrived(cond, dst, rs, like=None):
+        when(cond, copy(dst if like is None else like, dst, r.v_ss.at[0], rs, seq=mate).wait_recv)
+
+    barrier = pltpu.get_barrier_semaphore()
+    greeted = [{"seq": lax.rem(s + d, SEQ)} for d in range(1, SEQ)]
+    greeted += [{"head": lax.rem(h + d, HEAD)} for d in range(1, HEAD)]
+    greeted += [{"seq": pair, "head": across}]
+    for where in greeted:
+        pl.semaphore_signal(barrier, inc=1, device_id=where, device_id_type=MESH)
+    for k, ref in enumerate((r.g1, r.b1, r.g2, r.b2, r.b3)):
+        r.vec[k : k + 1, :] = ref[...].reshape(1, rows).astype(F32)
+    r.vec[5:8, :] = jnp.zeros((3, rows), F32)
+    for k in range(NEAR):
+        other = s + k - (SPAN - 1)
+
+        @pl.when((other < 0) | (other >= SEQ))
+        def _():
+            r.kv_all[k] = jnp.zeros(r.kv_all.shape[1:], BF16)
+            r.dkv_recv[k] = jnp.zeros(r.dkv_recv.shape[1:], BF16)
+
+    pl.semaphore_wait(barrier, len(greeted))
+
+    def cols(o, size):
+        return pl.ds(al(o * size, size), size)
+
+    relay_slot = [lambda o: r.wq_all.at[:, cols(o, rows), :], lambda o: r.wo_all.at[:, cols(o, rows)]]
+    relay_src = [r.wq, r.wo]
+
+    def relay_send(w, src, o, up_k, mate_k):
+        def args(k):
+            return src, relay_slot[w](o), r.g_ss.at[w, k], r.g_rs.at[w, o]
+
+        return args
+
+    def relay_start(w):
+        src, dst, rs = relay_src[w], relay_slot[w](s), r.g_rs.at[w, s]
+        send(z < LINE - 1, src, dst, r.g_ss.at[w, 0], rs, seq=s + 2)
+        send(z > 0, src, dst, r.g_ss.at[w, 4], rs, seq=s - 2)
+        send(None, src, dst, r.g_ss.at[w, 8], rs, seq=mate)
+
+    def relay_round(w, k):
+        for sign, first, third in ((-1, 0, 8 + k), (1, 4, 11 + k)):
+            from_z = z + sign * k
+            there = (from_z >= 0) & (from_z < LINE)
+            o = jnp.clip(from_z, 0, LINE - 1) * 2 + y
+            ref, rs = relay_slot[w](o), r.g_rs.at[w, o]
+            arrived(there, ref, rs)
+            onward = (z < LINE - 1) if sign < 0 else (z > 0)
+            send(there & onward, ref, ref, r.g_ss.at[w, first + k], rs, seq=s - 2 * sign)
+            send(there, ref, ref, r.g_ss.at[w, third], rs, seq=mate)
+
+    def relay_finish(w):
+        for d in range(LINE):
+            o = lax.rem(z + d, LINE) * 2 + 1 - y
+            arrived(None, relay_slot[w](o), r.g_rs.at[w, o])
+
+    for d in range(1, SEQ):
+        send(
+            None, r.vec, r.gains.at[:, cols(s, rows)], r.v_ss.at[d - 1], r.v_rs.at[s],
+            seq=lax.rem(s + d, SEQ),
+        )
+    relay_start(0)
+    r.gains[:, cols(s, rows)] = r.vec[...]
+    r.wq_all[:, cols(s, rows), :] = r.wq[...]
+    r.wo_all[:, cols(s, rows)] = r.wo[...]
+
+    start, leader, span, pad = 0, 0, 0, 0
+    for k in range(r.units.shape[0]):
+        here = r.units[k]
+        inside = (s >= start) & (s < start + here)
+        leader = jnp.where(inside, start, leader)
+        span = jnp.where(inside, here, span)
+        pad = jnp.where(inside, r.pads[k], pad)
+        start = start + here
+    position = s - leader
+    root = jnp.clip(SPAN - 1 - position, 0, SPAN - 1)
+    total = span * BLK_DEV
+    live = span * tokens - pad
+
+    for k in range(HEAD):
+        q = pl.ds(k * quarter, quarter)
+        r.xh[q, :] = norm_parts(r.tok[q, :].astype(F32))[0]
+    relay_round(0, 1)
+    relay_start(1)
+
+    columns = lax.broadcasted_iota(jnp.int32, (1, SPAN * tokens), 1)
+    usable = columns < live
+    blocks = lax.div(columns, BLK)
+    for hh in range(HEAD):
+        if hh == 2:
+            relay_round(0, 2)
+        for b in range(BLK_DEV):
+            query = position * BLK_DEV + b
+            count = jnp.zeros((1, SPAN * tokens), F32)
+            for wanted in (query - 1, query, query + 1, 0, total - 1):
+                count = count + jnp.where(blocks == wanted, 1.0, 0.0)
+            for k in range(r.picks.shape[0]):
+                raw = r.picks[k, b, hh]
+                chosen = lax.rem(raw, BLK_DEV)
+                for held in range(2, SPAN + 1):
+                    chosen = jnp.where(span == held, lax.rem(raw, BLK_DEV * held), chosen)
+                count = count + jnp.where(blocks == chosen, 1.0, 0.0)
+            count = jnp.where((query == 0) | (query == total - 1), 1.0, count)
+            r.cnt[hh, b : b + 1, :] = jnp.where(usable, count, 0.0)
+    relay_round(0, 3)
+
+    ffn_src = {
+        UP: lambda k: r.wu.at[:, cols(k, half)],
+        DOWN: lambda k: r.wd.at[cols(k, half), :],
+    }
+    ffn_slot = {
+        UP: lambda o: r.wu_all.at[cols(o, rows), :],
+        DOWN: lambda o: r.wd_all.at[:, cols(o, rows)],
+    }
+
+    def ffn_start(w):
+        i = w - UP
+        for d in range(1, LINE):
+            to = lax.rem(z + d, LINE)
+            send(
+                None, ffn_src[w](lax.rem(to, 2)), ffn_slot[w](s), r.f_ss.at[i, d - 1],
+                r.f_rs.at[i, s], seq=to * 2 + y,
+            )
+        send(
+            None, ffn_src[w](e), ffn_slot[w](s), r.f_ss.at[i, 3], r.f_rs.at[i, s], seq=mate
+        )
+
+    def ffn_forward(w):
+        i = w - UP
+        for d in range(1, LINE):
+            o = lax.rem(z + LINE - d, LINE) * 2 + y
+            ref = ffn_slot[w](o)
+            arrived(None, ref, r.f_rs.at[i, o])
+            send(None, ref, ref, r.f_ss.at[i, 3 + d], r.f_rs.at[i, o], seq=mate)
+
+    def ffn_finish(w):
+        for d in range(LINE):
+            o = lax.rem(z + d, LINE) * 2 + 1 - y
+            arrived(None, ffn_slot[w](o), r.f_rs.at[w - UP, o])
+
+    ffn_start(UP)
+    for ref, src in ((ffn_slot[UP](s), ffn_src[UP](e)), (ffn_slot[DOWN](s), ffn_src[DOWN](e))):
+        ref[...] = src[...]
+
+    for d in range(1, SEQ):
+        o = lax.rem(s + d, SEQ)
+        arrived(None, r.gains.at[:, cols(o, rows)], r.v_rs.at[o], r.vec)
+    for k in range(HEAD):
+        q = pl.ds(k * quarter, quarter)
+        r.normed[q, :] = (r.xh[q, :] * r.gains[0:1, :] + r.gains[1:2, :]).astype(BF16)
+    relay_finish(0)
+    scaling = HEAD_DIM ** (-0.5)
+    for k in (1, 2):
+        part = dot(r.normed[...], r.wq_all[k], ((1,), (0,)))
+        r.kv_all[SPAN - 1, :, pl.ds((k - 1) * head_w, head_w)] = part.astype(BF16)
+
+    def kv_send(cond, slot, back, k, to):
+        send(cond, r.kv_all.at[slot], r.kv_all.at[back], r.kv_ss.at[k], r.kv_rs.at[back], seq=to)
+
+    def kv_wait(cond, slot):
+        arrived(cond, r.kv_all.at[slot], r.kv_rs.at[slot])
+
+    low, high = z > 0, z < LINE - 1
+    from_mate = 4 - 2 * y
+    kv_send(None, 3, 2 + 2 * y, 0, mate)
+    kv_send(high, 3, 1, 1, s + 2)
+    kv_send(low, 3, 5, 2, s - 2)
+    part = dot(r.normed[...], r.wq_all[0], ((1,), (0,)))
+    r.qs[...] = (part.astype(BF16).astype(F32) * scaling).astype(BF16)
+    kv_wait(None, from_mate)
+    kv_send(high, from_mate, 2 - 2 * y, 3, s + 2)
+    kv_send(low, from_mate, 6 - 2 * y, 4, s - 2)
+    for k in range(1, LINE):
+        relay_round(1, k)
+    kv_wait(low, 2 - 2 * y)
+    kv_wait(high, 6 - 2 * y)
+    kv_send((y == 0) & low & high, 2, 0, 5, s + 2)
+    kv_send((y == 1) & low & high, 4, 6, 6, s - 2)
+    ffn_start(DOWN)
+
+    half_t = tokens // 2
+    r.cotx[cols(e, tokens), :] = r.cot[...]
+
+    def cot_rows(unit, core):
+        return r.cotx.at[pl.ds(al(unit * tokens + core * half_t, half_t), half_t), :]
+
+    send(None, r.cot.at[cols(c, half_t), :], cot_rows(e, c), r.c_ss.at[0], r.c_rs.at[0], seq=pair)
+    ffn_forward(UP)
+    kv_wait(low, 1)
+    kv_wait(high, 5)
+    kv_wait((y == 0) & (z >= 2), 0)
+    kv_wait((y == 1) & (z <= 1), 6)
+    for j in range(SPAN):
+        part = r.kv_all[root + j]
+        r.kwin[pl.ds(j * tokens, tokens), :] = part[:, :head_w]
+        r.vwin[pl.ds(j * tokens, tokens), :] = part[:, head_w:]
+
+    lanes = lax.div(lax.broadcasted_iota(jnp.int32, (1, head_w), 1), HEAD_DIM)
+    none = jnp.zeros((), BF16)
+    r.att[...] = jnp.zeros(r.att.shape, F32)
+
+    def attend(hh, carry):
+        mine = lanes == hh
+        query = jnp.where(mine, r.qs[...], none)
+        for j in range(SPAN):
+            k = pl.ds(j * tokens, tokens)
+            r.lg[:, k] = dot(query, r.kwin[k, :], ((1,), (1,)))
+        for b in range(BLK_DEV):
+            q = pl.ds(b * BLK, BLK)
+            count = r.cnt[hh, b : b + 1, :]
+            logits = jnp.where(count > 0, r.lg[q, :], NEGATIVE)
+            grown = jnp.exp(logits - jnp.max(logits, axis=-1, keepdims=True)) * count
+            chance = grown / jnp.sum(grown, axis=-1, keepdims=True)
+            r.prob[hh, q, :] = chance
+            r.prob_low[hh, q, :] = chance.astype(BF16)
+        part = dot(r.prob_low[hh], r.vwin[...], ((1,), (0,)))
+        r.att[...] += jnp.where(mine, part, 0.0)
+        return carry
+
+    lax.fori_loop(0, HEAD, attend, 0)
+    r.att_low[...] = r.att[...].astype(BF16)
+    relay_finish(1)
+
+    def rows_of(k):
+        return cols(k, quarter)
+
+    def reduce_start(op):
+        r.part_send[op] = r.sum_f[:tokens, :].astype(BF16)
+        for d in range(1, HEAD):
+            to = lax.rem(h + d, HEAD)
+            send(
+                None, r.part_send.at[op, rows_of(to), :], r.part_recv.at[op, h],
+                r.rs_ss.at[op, d], r.rs_rs.at[op, h], head=to,
+            )
+
+    def reduce_finish(op):
+        result = r.sum_f[rows_of(h), :]
+        for d in range(1, HEAD):
+            o = lax.rem(h + d, HEAD)
+            arrived(None, r.part_recv.at[op, o], r.rs_rs.at[op, o])
+            result = result + r.part_recv[op, o].astype(F32)
+        return result
+
+    def spread_start(op, whole, value):
+        whole[rows_of(h), :] = value
+        for d in range(1, HEAD):
+            ref = whole.at[rows_of(h), :]
+            send(
+                None, ref, ref, r.ag_ss.at[op, d], r.ag_rs.at[op, h], head=lax.rem(h + d, HEAD)
+            )
+
+    def spread_finish(op, whole):
+        for d in range(1, HEAD):
+            o = lax.rem(h + d, HEAD)
+            arrived(None, whole.at[rows_of(o), :], r.ag_rs.at[op, o])
+
+    def block_rows(unit, head):
+        return pl.ds(al(unit * tokens + head * quarter, quarter), quarter)
+
+    def pair_start(op):
+        for u in range(2):
+            for v in range(2):
+                block = r.sum_f[block_rows(u, v * 2 + 1 - c), :]
+                r.p1_send[op, u * 2 + v] = block.astype(BF16)
+        send(None, r.p1_send.at[op], r.p1_recv.at[op], r.p1_ss.at[op], r.p1_rs.at[op], head=twin)
+
+    def pair_middle(op):
+        arrived(None, r.p1_recv.at[op], r.p1_rs.at[op])
+        for du, dv in ((1, 1), (1, 0), (0, 1), (0, 0)):
+            u, v = lax.rem(e + du, 2), lax.rem(x + dv, 2)
+            block = r.sum_f[block_rows(u, v * 2 + c), :] + r.p1_recv[op, u * 2 + v].astype(F32)
+            if du or dv:
+                k = u * 2 + v
+                r.p2_send[op, k] = block.astype(BF16)
+                send(
+                    None, r.p2_send.at[op, k], r.p2_recv.at[op, e * 2 + x], r.p2_ss.at[op, k],
+                    r.p2_rs.at[op, e * 2 + x], seq=pair if du else s, head=across if dv else h,
+                )
+            else:
+                r.p_own[op] = block
+
+    def pair_finish(op):
+        result = r.p_own[op]
+        for du, dv in ((0, 1), (1, 0), (1, 1)):
+            k = lax.rem(e + du, 2) * 2 + lax.rem(x + dv, 2)
+            arrived(None, r.p2_recv.at[op, k], r.p2_rs.at[op, k])
+            result = result + r.p2_recv[op, k].astype(F32)
+        return result
+
+    def tiled(n, body):
+        def step(j, carry):
+            body(al(j * 256, 256))
+            return carry
+
+        lax.fori_loop(0, n // 256, step, 0)
+
+    def out_tile(k):
+        k = pl.ds(k, 256)
+        r.sum_f[:tokens, k] = dot(r.att_low[...], r.wo_all[:, k], ((1,), (0,)))
+
+    tiled(width, out_tile)
+    reduce_start(0)
+    arrived(None, cot_rows(1 - e, c), r.c_rs.at[0])
+    send(
+        None, cot_rows(1 - e, c), cot_rows(1 - e, c), r.c_ss.at[1], r.c_rs.at[1], head=twin
+    )
+    ffn_forward(DOWN)
+    middle = r.tok[rows_of(h), :].astype(F32) + reduce_finish(0)
+    r.mid_own[...] = middle
+    xhat, _ = norm_parts(middle)
+
+    def n2_rows(unit, head):
+        return r.n2x.at[block_rows(unit, head), :]
+
+    r.n2x[block_rows(e, h), :] = (xhat * r.gains[2:3, :] + r.gains[3:4, :]).astype(BF16)
+    mine, tag = n2_rows(e, h), e * 4 + h
+    send(None, mine, mine, r.n2_ss.at[0], r.n2_rs.at[tag], head=across)
+    send(None, mine, mine, r.n2_ss.at[1], r.n2_rs.at[tag], seq=pair, head=across)
+    send(None, mine, mine, r.n2_ss.at[2], r.n2_rs.at[tag], seq=pair)
+    send(None, mine, mine, r.n2_ss.at[3], r.n2_rs.at[tag], head=twin)
+    ffn_finish(UP)
+    ffn_finish(DOWN)
+    for k, (unit, head) in enumerate(((e, across), (1 - e, h), (1 - e, across))):
+        ref, tag = n2_rows(unit, head), unit * 4 + head
+        arrived(None, ref, r.n2_rs.at[tag])
+        send(None, ref, ref, r.n2_ss.at[4 + k], r.n2_rs.at[tag], head=twin)
+    for unit in (e, 1 - e):
+        for head in (x * 2 + 1 - c, (1 - x) * 2 + 1 - c):
+            arrived(None, n2_rows(unit, head), r.n2_rs.at[unit * 4 + head])
+    arrived(None, cot_rows(1 - e, 1 - c), r.c_rs.at[1])
+
+    root_c = (2.0 / 3.141592653589793) ** 0.5
+    r.up_send[half // 128 :, :] = jnp.zeros((8 - half // 128, 128), F32)
+    for j in range(half // 256):
+        f = pl.ds(j * 256, 256)
+        bias = r.upb[:, pl.ds(al(e * half + j * 256, 256), 256)].astype(F32)
+        v = dot(r.n2x[...], r.wu_all[:, f], ((1,), (0,))) + bias
+        t = jnp.tanh(root_c * (v + 0.044715 * (v * v * v)))
+        r.hid[:, f] = (0.5 * v * (1.0 + t)).astype(BF16)
+        slope = 0.5 * (1.0 + t) + 0.5 * v * (1.0 - t * t) * (root_c * (1.0 + 0.134145 * v * v))
+        low_p = (dot(r.cotx[...], r.wd_all[f, :], ((1,), (1,))) * slope).astype(BF16)
+        r.gp[:, f] = low_p
+        sums = jnp.sum(low_p.astype(F32), axis=0, keepdims=True)
+        r.up_send[2 * j : 2 * j + 1, :] = sums[:, :128]
+        r.up_send[2 * j + 1 : 2 * j + 2, :] = sums[:, 128:]
+
+    def gn2_tile(k):
+        k = pl.ds(k, 256)
+        r.sum_f[:, k] = dot(r.gp[...], r.wu_all[k, :], ((1,), (1,)))
+
+    tiled(width, gn2_tile)
+    pair_start(0)
+
+    grad_send = {QKV_KV: r.skv, QKV_Q: r.sq, OUT: r.so, UP: r.su, DOWN: r.sd}
+    grad_arrive = {QKV_KV: r.akv, QKV_Q: r.aq, OUT: r.ao, UP: r.au, DOWN: r.ad}
+    grad_again = {QKV_KV: r.bkv, QKV_Q: r.bq, OUT: r.bo, UP: r.bu, DOWN: r.bd}
+    grad_final = {QKV_KV: r.rkv, QKV_Q: r.rq, OUT: r.ro, UP: r.ru, DOWN: r.rd}
+
+    def tile_of(i):
+        return lax.rem(z + 1 + i, LINE)
+
+    def grad_cross(w, zz):
+        send(
+            None, grad_send[w].at[zz * 2 + 1 - y], grad_arrive[w].at[zz], r.ra_ss.at[w, zz],
+            r.ra_rs.at[w, zz], seq=mate,
+        )
+
+    def grad_along(w, ks=(1, 2, 3)):
+        for d in ks:
+            zz = lax.rem(z + d, LINE)
+            arrived(None, grad_arrive[w].at[zz], r.ra_rs.at[w, zz])
+            both = grad_send[w][zz * 2 + y].astype(F32) + grad_arrive[w][zz].astype(F32)
+            grad_again[w][zz] = both.astype(BF16)
+            send(
+                None, grad_again[w].at[zz], grad_final[w].at[z], r.rb_ss.at[w, zz],
+                r.rb_rs.at[w, z], seq=zz * 2 + y,
+            )
+
+    def grad_own(w):
+        arrived(None, grad_arrive[w].at[z], r.ra_rs.at[w, z])
+        return grad_send[w][z * 2 + y].astype(F32) + grad_arrive[w][z].astype(F32)
+
+    def grad_from(w, o):
+        arrived(None, grad_final[w].at[o], r.rb_rs.at[w, o])
+        return grad_final[w][o].astype(F32)
+
+    def grad_sum(w):
+        result = grad_own(w)
+        for d in range(1, LINE):
+            result = result + grad_from(w, lax.rem(z + d, LINE))
+        return result
+
+    def grad_halves(w):
+        same = grad_own(w) + grad_from(w, lax.rem(z + 2, LINE))
+        other = grad_from(w, lax.rem(z + 1, LINE)) + grad_from(w, lax.rem(z + 3, LINE))
+        return same, other
+
+    def down_step(i):
+        zz = tile_of(i)
+        part = dot(r.hid[...], r.cotx[:, cols(zz, 256)], ((0,), (0,))).astype(BF16)
+        r.sd[zz * 2] = part[:, :rows]
+        r.sd[zz * 2 + 1] = part[:, rows:]
+        grad_cross(DOWN, zz)
+
+    def up_step(i):
+        zz = tile_of(i)
+        part = dot(r.n2x[:, cols(zz, 256)], r.gp[...], ((0,), (0,))).astype(BF16)
+        r.su[zz * 2] = part[:rows]
+        r.su[zz * 2 + 1] = part[rows:]
+        grad_cross(UP, zz)
+
+    down_step(0)
+    down_step(1)
+    pair_middle(0)
+    down_step(2)
+    down_step(3)
+    for i in range(LINE):
+        up_step(i)
+    for d in range(1, SEQ):
+        send(
+            None, r.up_send, r.up_recv.at[s], r.up_ss.at[d], r.up_rs.at[s],
+            seq=lax.rem(s + d, SEQ),
+        )
+
+    grad_two = pair_finish(0)
+    xhat, inverse = norm_parts(r.mid_own[...])
+    dy = r.cot[rows_of(h), :].astype(F32)
+    grad_mid = dy + norm_backward(xhat, inverse, grad_two * r.gains[2:3, :])
+    r.gm_own[...] = grad_mid
+    spread_start(0, r.gb, grad_mid.astype(BF16))
+    r.sm_send[2:3, :] = jnp.sum(grad_two * xhat, axis=0, keepdims=True)
+    r.sm_send[3:4, :] = jnp.sum(grad_two, axis=0, keepdims=True)
+    r.sm_send[4:5, :] = jnp.sum(dy, axis=0, keepdims=True)
+    r.sm_send[5:8, :] = jnp.zeros((3, width), F32)
+
+    def down_tile(k):
+        k = pl.ds(k, 256)
+        r.sum_f[:, k] = dot(r.hid[...], r.wd_all[:, k], ((1,), (0,)))
+
+    tiled(width, down_tile)
+    pair_start(1)
+    grad_along(DOWN)
+    pair_middle(1)
+    spread_finish(0, r.gb)
+    r.gatt[...] = dot(r.gb[...], r.wo_all[...], ((1,), (1,))).astype(BF16)
+    for i in range(LINE):
+        zz = tile_of(i)
+        part = dot(r.att_low[...], r.gb[:, cols(zz, 256)], ((0,), (0,))).astype(BF16)
+        r.so[zz * 2] = part[:, :rows]
+        r.so[zz * 2 + 1] = part[:, rows:]
+        grad_cross(OUT, zz)
+    grad_along(UP)
+
+    r.dq[...] = jnp.zeros(r.dq.shape, F32)
+    r.dk[...] = jnp.zeros(r.dk.shape, F32)
+    r.dv[...] = jnp.zeros(r.dv.shape, F32)
+
+    def attend_back(hh, carry):
+        mine = lanes == hh
+        query = jnp.where(mine, r.qs[...], none)
+        grad = jnp.where(mine, r.gatt[...], none)
+        for j in range(SPAN):
+            k = pl.ds(j * tokens, tokens)
+            r.lg[:, k] = dot(grad, r.vwin[k, :], ((1,), (1,)))
+        for b in range(BLK_DEV):
+            q = pl.ds(b * BLK, BLK)
+            chance, grown = r.prob[hh, q, :], r.lg[q, :]
+            inner = jnp.sum(chance * grown, axis=-1, keepdims=True)
+            r.ds[q, :] = (chance * (grown - inner)).astype(BF16)
+        r.dq[...] += jnp.where(mine, dot(r.ds[...], r.kwin[...], ((1,), (0,))), 0.0)
+        for j in range(SPAN):
+            k = pl.ds(j * tokens, tokens)
+            r.dk[k, :] += dot(r.ds[:, k], query, ((0,), (0,)))
+            r.dv[k, :] += dot(r.prob_low[hh, :, k], grad, ((0,), (0,)))
+        return carry
+
+    lax.fori_loop(0, HEAD, attend_back, 0)
+    for k in range(2 * (SPAN - 1) + SPAN):
+        j = k - (SPAN - 1)
+        if 0 <= j < SPAN:
+            q = pl.ds(j * tokens, tokens)
+            r.dkv_pad[k, :, :head_w] = r.dk[q, :].astype(BF16)
+            r.dkv_pad[k, :, head_w:] = r.dv[q, :].astype(BF16)
+        else:
+            r.dkv_pad[k] = jnp.zeros(r.dkv_pad.shape[1:], BF16)
+    for k in range(NEAR):
+        r.dkv_send[k] = r.dkv_pad[k + SPAN - 1 - root]
+        other, back = s + k - (SPAN - 1), 2 * (SPAN - 1) - k
+        if k != SPAN - 1:
+            send(
+                (other >= 0) & (other < SEQ), r.dkv_send.at[k], r.dkv_recv.at[back],
+                r.dkv_ss.at[k], r.dkv_rs.at[back], seq=other,
+            )
+
+    r.gtq[...] = (r.dq[...] * scaling).astype(BF16)
+    for i in range(LINE):
+        zz = tile_of(i)
+        part = dot(r.normed[:, cols(zz, 256)], r.gtq[...], ((0,), (0,))).astype(BF16)
+        r.sq[zz * 2] = part[:rows]
+        r.sq[zz * 2 + 1] = part[rows:]
+        grad_cross(QKV_Q, zz)
+    grad_along(OUT)
+    ffn = pair_finish(1)
+    spread_start(1, r.out_o, (r.mid_own[...] + ffn + r.gains[4:5, :]).astype(BF16))
+
+    whole = r.dkv_send[SPAN - 1].astype(F32)
+    for k in range(NEAR):
+        if k != SPAN - 1:
+            other = s + k - (SPAN - 1)
+            arrived((other >= 0) & (other < SEQ), r.dkv_recv.at[k], r.dkv_rs.at[k])
+            whole = whole + r.dkv_recv[k].astype(F32)
+    r.gtkv[...] = whole.astype(BF16)
+    for i in range(LINE):
+        zz = tile_of(i)
+        part = dot(r.normed[:, cols(zz, 256)], r.gtkv[...], ((0,), (0,))).astype(BF16)
+        for v in range(2):
+            for k in range(2):
+                r.skv[zz * 2 + v, k] = part[v * rows : (v + 1) * rows, k * head_w : (k + 1) * head_w]
+        grad_cross(QKV_KV, zz)
+
+    def gn1_tile(k):
+        k = pl.ds(k, 256)
+        r.sum_f[:tokens, k] = (
+            dot(r.gtq[...], r.wq_all[0, k, :], ((1,), (1,)))
+            + dot(r.gtkv[:, :head_w], r.wq_all[1, k, :], ((1,), (1,)))
+            + dot(r.gtkv[:, head_w:], r.wq_all[2, k, :], ((1,), (1,)))
+        )
+
+    tiled(width, gn1_tile)
+    reduce_start(1)
+    grad_along(QKV_Q)
+    grad_along(QKV_KV)
+    grad_one = reduce_finish(1)
+    xhat, inverse = norm_parts(r.tok[rows_of(h), :].astype(F32))
+    r.sm_send[0:1, :] = jnp.sum(grad_one * xhat, axis=0, keepdims=True)
+    r.sm_send[1:2, :] = jnp.sum(grad_one, axis=0, keepdims=True)
+    for d in range(1, SEQ):
+        to = lax.rem(s + d, SEQ)
+        send(
+            None, r.sm_send.at[:, cols(to, rows)], r.sm_recv.at[s], r.sm_ss.at[d], r.sm_rs.at[s],
+            seq=to,
+        )
+    grad_x = r.gm_own[...] + norm_backward(xhat, inverse, grad_one * r.gains[0:1, :])
+    spread_start(2, r.xgb, grad_x.astype(BF16))
+
+    same, other = grad_halves(DOWN)
+    r.gd_o[cols(e, half), :] = same
+    r.gd_o[cols(1 - e, half), :] = other
+    same, other = grad_halves(UP)
+    r.gu_o[:, cols(e, half)] = same
+    r.gu_o[:, cols(1 - e, half)] = other
+    r.go_o[...] = grad_sum(OUT)
+
+    r.sm_recv[s] = r.sm_send[:, cols(s, rows)]
+    r.up_recv[s] = r.up_send[...]
+    for d in range(1, SEQ):
+        o = lax.rem(s + d, SEQ)
+        arrived(None, r.sm_recv.at[o], r.sm_rs.at[o], r.vec)
+        arrived(None, r.up_recv.at[o], r.up_rs.at[o])
+    part = r.sm_recv[0]
+    for o in range(1, SEQ):
+        part = part + r.sm_recv[o]
+    r.sm_own[...] = part
+    for d in range(1, HEAD):
+        send(
+            None, r.sm_own, r.sm_two.at[h], r.sm2_ss.at[d], r.sm2_rs.at[h],
+            head=lax.rem(h + d, HEAD),
+        )
+    r.sm_two[h] = part
+    tall = half // 128
+    for u in range(2):
+        ups = jnp.zeros((tall, 128), F32)
+        for o in range(SEQ):
+            if (o // 2) % 2 == u:
+                ups = ups + r.up_recv[o, :tall, :]
+        r.small_o[8 + u * tall : 8 + (u + 1) * tall, :] = ups
+    spread_finish(1, r.out_o)
+    spread_finish(2, r.xgb)
+    r.xg_o[...] = r.xgb[...].astype(F32)
+    for d in range(1, HEAD):
+        o = lax.rem(h + d, HEAD)
+        arrived(None, r.sm_two.at[o], r.sm2_rs.at[o])
+    r.small_o[0:8, :] = (r.sm_two[0] + r.sm_two[1]) + (r.sm_two[2] + r.sm_two[3])
+    r.gq_o[0] = grad_sum(QKV_Q)
+    r.gq_o[1:3] = grad_sum(QKV_KV)
+
+    for cond, one in sent:
+        when(cond, one.wait_send)
+
+
+def local_fused(
+    tokens, w_qkv, w_out, ln1_gain, ln1_bias, ln2_gain, ln2_bias, w_up, up_bias, w_down, down_bias,
+    seq_units, seq_pad, rand_picks, cotangent,
+):
+    tok, width = tokens.shape
+    rows, _, head_w = w_qkv.shape
+    hidden = w_up.shape[1]
+    half = hidden // 2
+    quarter = tok // HEAD
+    keys = SPAN * tok
+    smem, vmem = pl.BlockSpec(memory_space=pltpu.SMEM), pl.BlockSpec(memory_space=pltpu.VMEM)
+    ins = dict(
+        units=seq_units, pads=seq_pad, picks=jnp.transpose(rand_picks, (2, 0, 1)), tok=tokens,
+        cot=cotangent, wq=jnp.transpose(w_qkv, (1, 0, 2)), wo=w_out, wu=w_up, wd=w_down,
+        g1=ln1_gain, b1=ln1_bias, g2=ln2_gain, b2=ln2_bias, b3=down_bias,
+        upb=up_bias.reshape(1, hidden),
+    )
+    outs = dict(
+        out_o=((tok, width), BF16), xg_o=((tok, width), F32), gq_o=((3, rows, head_w), F32),
+        go_o=((head_w, rows), F32), gu_o=((rows, hidden), F32), gd_o=((hidden, rows), F32),
+        small_o=((16, rows), F32),
+    )
+    scratch = dict(
+        wq_all=((3, width, head_w), BF16), wo_all=((head_w, width), BF16),
+        wu_all=((width, half), BF16), wd_all=((half, width), BF16), vec=((8, rows), F32),
+        gains=((8, width), F32), xh=((tok, width), F32), normed=((tok, width), BF16),
+        qs=((tok, head_w), BF16), kv_all=((NEAR, tok, 2 * head_w), BF16),
+        kwin=((keys, head_w), BF16), vwin=((keys, head_w), BF16), lg=((tok, keys), F32),
+        prob=((HEAD, tok, keys), F32), prob_low=((HEAD, tok, keys), BF16), ds=((tok, keys), BF16),
+        att=((tok, head_w), F32), att_low=((tok, head_w), BF16), n2x=((2 * tok, width), BF16),
+        cotx=((2 * tok, width), BF16), hid=((2 * tok, half), BF16), gp=((2 * tok, half), BF16),
+        gb=((tok, width), BF16), xgb=((tok, width), BF16), mid_own=((quarter, width), F32),
+        gm_own=((quarter, width), F32), gatt=((tok, head_w), BF16), dq=((tok, head_w), F32),
+        dk=((keys, head_w), F32), dv=((keys, head_w), F32),
+        dkv_pad=((NEAR + SPAN - 1, tok, 2 * head_w), BF16),
+        dkv_send=((NEAR, tok, 2 * head_w), BF16), dkv_recv=((NEAR, tok, 2 * head_w), BF16),
+        gtq=((tok, head_w), BF16), gtkv=((tok, 2 * head_w), BF16),
+        part_send=((2, tok, width), BF16), part_recv=((2, HEAD, quarter, width), BF16),
+        sum_f=((2 * tok, width), F32), cnt=((HEAD, 8, keys), F32),
+        p1_send=((2, 4, quarter, width), BF16), p1_recv=((2, 4, quarter, width), BF16),
+        p2_send=((2, 4, quarter, width), BF16), p2_recv=((2, 4, quarter, width), BF16),
+        p_own=((2, quarter, width), F32), sm_send=((8, width), F32),
+        sm_recv=((SEQ, 8, rows), F32), sm_own=((8, rows), F32), sm_two=((HEAD, 8, rows), F32),
+        up_send=((8, 128), F32), up_recv=((SEQ, 8, 128), F32),
+    )
+    shards = dict(
+        kv=(2, rows, head_w), q=(rows, head_w), o=(head_w, rows), u=(rows, half), d=(half, rows)
+    )
+    for lead, count in (("s", SEQ), ("a", LINE), ("b", LINE), ("r", LINE)):
+        for name, shape in shards.items():
+            scratch[lead + name] = ((count,) + shape, BF16)
+    semaphores = dict(
+        g_ss=(2, 16), g_rs=(2, SEQ), f_ss=(2, 7), f_rs=(2, SEQ), v_ss=(7,), v_rs=(SEQ,),
+        kv_ss=(NEAR,), kv_rs=(NEAR,), dkv_ss=(NEAR,), dkv_rs=(NEAR,), c_ss=(2,), c_rs=(2,),
+        rs_ss=(2, HEAD), rs_rs=(2, HEAD), ag_ss=(3, HEAD), ag_rs=(3, HEAD), n2_ss=(7,),
+        n2_rs=(8,), p1_ss=(2,), p1_rs=(2,), p2_ss=(2, 4), p2_rs=(2, 4), ra_ss=(5, LINE),
+        ra_rs=(5, LINE), rb_ss=(5, LINE), rb_rs=(5, LINE), sm_ss=(SEQ,), sm_rs=(SEQ,),
+        sm2_ss=(HEAD,), sm2_rs=(HEAD,), up_ss=(SEQ,), up_rs=(SEQ,),
+    )
+    names = [*ins, *outs, *scratch, *semaphores]
+    out, xg, gq, go, gu, gd, small = pl.pallas_call(
+        functools.partial(fused_kernel, names),
+        out_shape=[jax.ShapeDtypeStruct(*o) for o in outs.values()],
+        in_specs=[smem] * 3 + [vmem] * (len(ins) - 3),
+        out_specs=[vmem] * len(outs),
+        scratch_shapes=[pltpu.VMEM(*v) for v in scratch.values()]
+        + [pltpu.SemaphoreType.DMA(v) for v in semaphores.values()],
+        compiler_params=pltpu.CompilerParams(
+            collective_id=0, has_side_effects=True, vmem_limit_bytes=VMEM_BYTES
+        ),
+        name="fused_layer",
+    )(*ins.values())
+    return (
+        out, xg, jnp.transpose(gq, (1, 0, 2)), go, small[0], small[1], small[2], small[3], gu,
+        small[8:16].reshape(hidden), gd, small[4],
+    )
+
+
 IN_SPECS = (
     P("seq", None), P("seq", None, "head"), P("head", "seq"), P("seq"), P("seq"), P("seq"),
     P("seq"), P("seq", "head"), P("head"), P("head", "seq"), P("seq"), P(), P(),
@@ -169,6 +889,8 @@
 
 
 def solution(mesh):
+    fits = mesh.shape["seq"] == SEQ and mesh.shape["head"] == HEAD
     return jax.shard_map(
-        local_general, mesh=mesh, in_specs=IN_SPECS, out_specs=OUT_SPECS, check_vma=False
-    )
+        local_fused if fits else local_general, mesh=mesh, in_specs=IN_SPECS,
+        out_specs=OUT_SPECS, check_vma=False,
+    )

time: 853 us -> 186 us (0.22)
  waiting for transfers between devices: 636 us -> 0 us
  Pallas kernels: 0 us -> 174 us
  blocking collectives: 77.8 us -> 0 us
  matrix products: 35.6 us -> 0 us
  starting transfers between devices: 29.3 us -> 0 us
  between operations: 24.6 us -> 0.68 us
  other arithmetic: 18.9 us -> 0 us
  local copies, waits for them, and re-layouts: 29.2 us -> 10.7 us
    reduce_scatter x5 -> x0, waiting for transfers between devices: 348 us -> none  [local_general(): lax.psum_scatter(v, 'seq', scatter_dimension=d, tiled=True)]
    pallas_call x0 -> x1, Pallas kernels: none -> 174 us  [local_fused(): pl.pallas_call(functools.partial(fused_kernel, names), out_shape=[jax.Sha...]
    psum x4 -> x0, waiting for transfers between devices: 146 us -> none  [the longest x1 41.7 us: local_general(): lax.psum(jnp.einsum('tcf,dcf->td', grad_triple, qkv, preferred_element_ty...]
    all_gather x3 -> x0, waiting for transfers between devices: 98.5 us -> none  [the longest x1 52.1 us: local_general(): cols = lambda v: lax.all_gather(v, 'seq', axis=1, tiled=True)]
    all_gather x2 -> x0, blocking collectives: 55.7 us -> none  [local_general(): cols = lambda v: lax.all_gather(v, 'seq', axis=1, tiled=True)]
    ppermute x12 -> x0, waiting for transfers between devices: 42.2 us -> none  [shifted(): lax.ppermute(value, axis, [(i, i + steps) for i in range(first, last)])]
    dot_general x18 -> x0, matrix products: 35.6 us -> none  [the longest x9 20.3 us: dot(): return lax.dot_general(a, b, (dims, ((), ())), preferred_element_type=F32)]
    ppermute x12 -> x0, starting transfers between devices: 28.6 us -> none  [shifted(): lax.ppermute(value, axis, [(i, i + steps) for i in range(first, last)])]
  transfers between devices with their start and end apart: 24 -> 0, of which waited for: 17 -> 0; matrix products, arithmetic and copies ran while one was open for 4% -> 0% of each run, Pallas kernels for 0% -> 0%
where the time goes in v3:
time: 186 us
  Pallas kernels  174 us (94%)
  local copies, waits for them, and re-layouts  10.7 us (6%)
    pallas_call x1, Pallas kernels, local_fused(): pl.pallas_call(functools.partial(fused_kernel, names), out_shape=[jax.Sha...  174 us
    unnamed x18, local copies, waits for them, and re-layouts  7.46 us

profile of v3, /device:TPU:0, one launch (start us, length us, event | category | flops | bytes accessed | tf_op | source)
XLA Modules:
  0.0 185.7 jit_solution(9756264660522114352)
XLA Ops:
  0.6 0.0 copy-start.5
  0.7 0.7 copy-done.5
  1.3 0.6 reshape.30.refs_14_
  1.9 174.4 %fused_layer.1 = (bf16[256,1024]{1,0:T(8,128)(2,1)}, f32[256,1024]{1,0:T(8,128)}, f32[3,128,256]{2,1,0:T(8,128)}, f32[256,128]{1,0:T(8,128)}, f32[128,1024]{1,0:...) custom-call(s32[4]{0:T(128)} %refs_0_.1, s32[4]{0:T(128)} %refs_1_.1, s32[3,4,4]{2,1,0:T(4,128)} %bitcast.17, ...), custom_call_target="tpu_custom_call" | custom-call | tf_op jit(solution)/shard_map/fused_layer/pallas_call | solution.py:862
  176.3 0.0 copy-start
  176.3 1.4 slice_bitcast_fusion.1
  177.7 1.3 slice_bitcast_fusion
  179.0 1.9 %copy.33 = bf16[256,1024]{1,0:T(8,128)(2,1)} copy(bf16[256,1024]{1,0:T(8,128)(2,1)} %get-tuple-element.43) | data formatting | bytes 1048576
  180.8 0.0 copy-done
  180.8 0.0 copy-start.3
  180.8 1.0 copy.34
  181.8 0.3 copy-done.3
  182.1 0.0 copy-start.4
  182.1 0.0 copy-start.2
  182.1 0.7 copy.35
  182.8 0.2 copy-done.4
  183.1 0.7 copy.36
  183.7 0.0 copy-done.2
  183.7 0.0 copy-start.1
  183.7 0.8 copy.37
  184.5 0.4 copy-done.1
  184.9 0.8 copy.38
Async XLA Ops:
  0.6 0.7 copy-start.5
  176.3 4.5 %copy-start = (f32[256,1024]{1,0:T(8,128)S(1)}, f32[256,1024]{1,0:T(8,128)}, u32[]{:S(2)}) copy-start(f32[256,1024]{1,0:T(8,128)} %get-tuple-element.44) | copy-start | bytes 3145732
  180.8 1.2 copy-start.3
  182.1 1.0 copy-start.4
  182.1 1.7 copy-start.2
  183.7 1.2 copy-start.1

commit v4 on v3

--- a/solution.py
+++ b/solution.py
@@ -221,27 +221,17 @@
     for k, ref in enumerate((r.g1, r.b1, r.g2, r.b2, r.b3)):
         r.vec[k : k + 1, :] = ref[...].reshape(1, rows).astype(F32)
     r.vec[5:8, :] = jnp.zeros((3, rows), F32)
-    for k in range(NEAR):
-        other = s + k - (SPAN - 1)
-
-        @pl.when((other < 0) | (other >= SEQ))
-        def _():
-            r.kv_all[k] = jnp.zeros(r.kv_all.shape[1:], BF16)
-            r.dkv_recv[k] = jnp.zeros(r.dkv_recv.shape[1:], BF16)
-
     pl.semaphore_wait(barrier, len(greeted))
 
     def cols(o, size):
         return pl.ds(al(o * size, size), size)
 
-    relay_slot = [lambda o: r.wq_all.at[:, cols(o, rows), :], lambda o: r.wo_all.at[:, cols(o, rows)]]
-    relay_src = [r.wq, r.wo]
-
-    def relay_send(w, src, o, up_k, mate_k):
-        def args(k):
-            return src, relay_slot[w](o), r.g_ss.at[w, k], r.g_rs.at[w, o]
-
-        return args
+    relay_slot = [
+        lambda o: r.wq_all.at[1:3, cols(o, rows), :],
+        lambda o: r.wq_all.at[0, cols(o, rows), :],
+        lambda o: r.wo_all.at[:, cols(o, rows)],
+    ]
+    relay_src = [r.wq.at[1:3], r.wq.at[0], r.wo]
 
     def relay_start(w):
         src, dst, rs = relay_src[w], relay_slot[w](s), r.g_rs.at[w, s]
@@ -265,6 +255,37 @@
             o = lax.rem(z + d, LINE) * 2 + 1 - y
             arrived(None, relay_slot[w](o), r.g_rs.at[w, o])
 
+    low, high = z > 0, z < LINE - 1
+    from_mate = 4 - 2 * y
+
+    def token_rows(slot, head):
+        return r.nall.at[slot, cols(head, quarter), :]
+
+    def token_send(cond, slot, back, k, to):
+        send(cond, token_rows(slot, h), token_rows(back, h), r.t_ns.at[k], r.t_rs.at[back, h], seq=to)
+
+    def token_share(cond, slot):
+        ref = token_rows(slot, h)
+        arrived(cond, ref, r.t_rs.at[slot, h])
+        send(cond, ref, ref, r.t_ss.at[slot, 0], r.t_rs.at[slot, h], head=across)
+        send(cond, ref, ref, r.t_ss.at[slot, 1], r.t_rs.at[slot, h], head=twin)
+
+    def token_pass(cond, slot):
+        ref = token_rows(slot, across)
+        arrived(cond, ref, r.t_rs.at[slot, across])
+        send(cond, ref, ref, r.t_ss.at[slot, 2], r.t_rs.at[slot, across], head=twin)
+
+    def token_ready(cond, slot):
+        arrived(cond, token_rows(slot, twin), r.t_rs.at[slot, twin])
+        other = (1 - x) * 2 + 1 - c
+        arrived(cond, token_rows(slot, other), r.t_rs.at[slot, other])
+
+    far_in = jnp.where(y == 0, z >= 2, z <= 1)
+    far_slot = 6 * y
+    slots = (
+        (None, from_mate), (low, 1), (high, 5), (low, 2 - 2 * y), (high, 6 - 2 * y),
+        (far_in, far_slot),
+    )
     for d in range(1, SEQ):
         send(
             None, r.vec, r.gains.at[:, cols(s, rows)], r.v_ss.at[d - 1], r.v_rs.at[s],
@@ -272,8 +293,53 @@
         )
     relay_start(0)
     r.gains[:, cols(s, rows)] = r.vec[...]
+    for k in range(NEAR):
+        other = s + k - (SPAN - 1)
+
+        @pl.when((other < 0) | (other >= SEQ))
+        def _():
+            r.nall[k] = jnp.zeros(r.nall.shape[1:], BF16)
+
+    for k, cond in enumerate((low & high, high, low, high, low)):
+
+        @pl.when(jnp.logical_not(cond))
+        def _():
+            r.dkv_recv[k] = jnp.zeros(r.dkv_recv.shape[1:], BF16)
+
+    for d in range(1, SEQ):
+        o = lax.rem(s + d, SEQ)
+        arrived(None, r.gains.at[:, cols(o, rows)], r.v_rs.at[o], r.vec)
+
+    def normalise(q):
+        xhat, _ = norm_parts(r.tok[q, :].astype(F32))
+        r.nall[SPAN - 1, q, :] = (xhat * r.gains[0:1, :] + r.gains[1:2, :]).astype(BF16)
+
+    normalise(cols(h, quarter))
+    token_send(None, SPAN - 1, 2 + 2 * y, 0, mate)
+    token_send(high, SPAN - 1, 1, 1, s + 2)
+    token_send(low, SPAN - 1, 5, 2, s - 2)
+    for d in range(1, HEAD):
+        normalise(cols(lax.rem(h + d, HEAD), quarter))
+    token_share(*slots[0])
+    token_send(high, from_mate, 2 - 2 * y, 3, s + 2)
+    token_send(low, from_mate, 6 - 2 * y, 4, s - 2)
+    relay_round(0, 1)
+    token_share(*slots[1])
+    token_share(*slots[2])
     r.wq_all[:, cols(s, rows), :] = r.wq[...]
     r.wo_all[:, cols(s, rows)] = r.wo[...]
+    token_share(*slots[3])
+    token_share(*slots[4])
+    token_send((y == 0) & low & high, 2, 0, 5, s + 2)
+    token_send((y == 1) & low & high, 4, 6, 5, s - 2)
+    relay_round(0, 2)
+    relay_start(1)
+    relay_round(0, 3)
+    token_share(*slots[5])
+    for cond, slot in slots[:3]:
+        token_pass(cond, slot)
+    relay_round(1, 1)
+    relay_start(2)
 
     start, leader, span, pad = 0, 0, 0, 0
     for k in range(r.units.shape[0]):
@@ -288,18 +354,10 @@
     total = span * BLK_DEV
     live = span * tokens - pad
 
-    for k in range(HEAD):
-        q = pl.ds(k * quarter, quarter)
-        r.xh[q, :] = norm_parts(r.tok[q, :].astype(F32))[0]
-    relay_round(0, 1)
-    relay_start(1)
-
     columns = lax.broadcasted_iota(jnp.int32, (1, SPAN * tokens), 1)
     usable = columns < live
     blocks = lax.div(columns, BLK)
     for hh in range(HEAD):
-        if hh == 2:
-            relay_round(0, 2)
         for b in range(BLK_DEV):
             query = position * BLK_DEV + b
             count = jnp.zeros((1, SPAN * tokens), F32)
@@ -308,12 +366,13 @@
             for k in range(r.picks.shape[0]):
                 raw = r.picks[k, b, hh]
                 chosen = lax.rem(raw, BLK_DEV)
-                for held in range(2, SPAN + 1):
-                    chosen = jnp.where(span == held, lax.rem(raw, BLK_DEV * held), chosen)
+                for k_units in range(2, SPAN + 1):
+                    chosen = jnp.where(span == k_units, lax.rem(raw, BLK_DEV * k_units), chosen)
                 count = count + jnp.where(blocks == chosen, 1.0, 0.0)
             count = jnp.where((query == 0) | (query == total - 1), 1.0, count)
-            r.cnt[hh, b : b + 1, :] = jnp.where(usable, count, 0.0)
-    relay_round(0, 3)
+            held = usable & (count > 0)
+            bias = jnp.log(jnp.maximum(count, 1.0))
+            r.bias[hh, b : b + 1, :] = jnp.where(held, bias, NEGATIVE)
 
     ffn_src = {
         UP: lambda k: r.wu.at[:, cols(k, half)],
@@ -350,44 +409,28 @@
             arrived(None, ffn_slot[w](o), r.f_rs.at[w - UP, o])
 
     ffn_start(UP)
+    relay_round(1, 2)
+    relay_round(1, 3)
+    for cond, slot in slots[3:]:
+        token_pass(cond, slot)
     for ref, src in ((ffn_slot[UP](s), ffn_src[UP](e)), (ffn_slot[DOWN](s), ffn_src[DOWN](e))):
         ref[...] = src[...]
 
-    for d in range(1, SEQ):
-        o = lax.rem(s + d, SEQ)
-        arrived(None, r.gains.at[:, cols(o, rows)], r.v_rs.at[o], r.vec)
-    for k in range(HEAD):
-        q = pl.ds(k * quarter, quarter)
-        r.normed[q, :] = (r.xh[q, :] * r.gains[0:1, :] + r.gains[1:2, :]).astype(BF16)
+    ffn_start(DOWN)
+    for cond, slot in slots:
+        token_ready(cond, slot)
     relay_finish(0)
     scaling = HEAD_DIM ** (-0.5)
-    for k in (1, 2):
-        part = dot(r.normed[...], r.wq_all[k], ((1,), (0,)))
-        r.kv_all[SPAN - 1, :, pl.ds((k - 1) * head_w, head_w)] = part.astype(BF16)
-
-    def kv_send(cond, slot, back, k, to):
-        send(cond, r.kv_all.at[slot], r.kv_all.at[back], r.kv_ss.at[k], r.kv_rs.at[back], seq=to)
-
-    def kv_wait(cond, slot):
-        arrived(cond, r.kv_all.at[slot], r.kv_rs.at[slot])
-
-    low, high = z > 0, z < LINE - 1
-    from_mate = 4 - 2 * y
-    kv_send(None, 3, 2 + 2 * y, 0, mate)
-    kv_send(high, 3, 1, 1, s + 2)
-    kv_send(low, 3, 5, 2, s - 2)
-    part = dot(r.normed[...], r.wq_all[0], ((1,), (0,)))
+    for j in range(SPAN):
+        q = pl.ds(j * tokens, tokens)
+        rows_in = r.nall[root + j]
+        r.kwin[q, :] = dot(rows_in, r.wq_all[1], ((1,), (0,))).astype(BF16)
+        r.vwin[q, :] = dot(rows_in, r.wq_all[2], ((1,), (0,))).astype(BF16)
+    relay_finish(1)
+    part = dot(r.nall[SPAN - 1], r.wq_all[0], ((1,), (0,)))
     r.qs[...] = (part.astype(BF16).astype(F32) * scaling).astype(BF16)
-    kv_wait(None, from_mate)
-    kv_send(high, from_mate, 2 - 2 * y, 3, s + 2)
-    kv_send(low, from_mate, 6 - 2 * y, 4, s - 2)
     for k in range(1, LINE):
-        relay_round(1, k)
-    kv_wait(low, 2 - 2 * y)
-    kv_wait(high, 6 - 2 * y)
-    kv_send((y == 0) & low & high, 2, 0, 5, s + 2)
-    kv_send((y == 1) & low & high, 4, 6, 6, s - 2)
-    ffn_start(DOWN)
+        relay_round(2, k)
 
     half_t = tokens // 2
     r.cotx[cols(e, tokens), :] = r.cot[...]
@@ -397,14 +440,6 @@
 
     send(None, r.cot.at[cols(c, half_t), :], cot_rows(e, c), r.c_ss.at[0], r.c_rs.at[0], seq=pair)
     ffn_forward(UP)
-    kv_wait(low, 1)
-    kv_wait(high, 5)
-    kv_wait((y == 0) & (z >= 2), 0)
-    kv_wait((y == 1) & (z <= 1), 6)
-    for j in range(SPAN):
-        part = r.kv_all[root + j]
-        r.kwin[pl.ds(j * tokens, tokens), :] = part[:, :head_w]
-        r.vwin[pl.ds(j * tokens, tokens), :] = part[:, head_w:]
 
     lanes = lax.div(lax.broadcasted_iota(jnp.int32, (1, head_w), 1), HEAD_DIM)
     none = jnp.zeros((), BF16)
@@ -418,51 +453,52 @@
             r.lg[:, k] = dot(query, r.kwin[k, :], ((1,), (1,)))
         for b in range(BLK_DEV):
             q = pl.ds(b * BLK, BLK)
-            count = r.cnt[hh, b : b + 1, :]
-            logits = jnp.where(count > 0, r.lg[q, :], NEGATIVE)
-            grown = jnp.exp(logits - jnp.max(logits, axis=-1, keepdims=True)) * count
-            chance = grown / jnp.sum(grown, axis=-1, keepdims=True)
-            r.prob[hh, q, :] = chance
-            r.prob_low[hh, q, :] = chance.astype(BF16)
-        part = dot(r.prob_low[hh], r.vwin[...], ((1,), (0,)))
+            logits = r.lg[q, :] + r.bias[hh, b : b + 1, :]
+            grown = jnp.exp(logits - jnp.max(logits, axis=-1, keepdims=True))
+            scale = 1.0 / jnp.sum(grown, axis=-1, keepdims=True)
+            r.prob[hh, q, :] = (grown * scale).astype(BF16)
+        part = dot(r.prob[hh], r.vwin[...], ((1,), (0,)))
         r.att[...] += jnp.where(mine, part, 0.0)
         return carry
 
     lax.fori_loop(0, HEAD, attend, 0)
     r.att_low[...] = r.att[...].astype(BF16)
-    relay_finish(1)
+    relay_finish(2)
+
+    beyond = (1 - x) * 2 + 1 - c
 
     def rows_of(k):
         return cols(k, quarter)
 
     def reduce_start(op):
-        r.part_send[op] = r.sum_f[:tokens, :].astype(BF16)
-        for d in range(1, HEAD):
-            to = lax.rem(h + d, HEAD)
-            send(
-                None, r.part_send.at[op, rows_of(to), :], r.part_recv.at[op, h],
-                r.rs_ss.at[op, d], r.rs_rs.at[op, h], head=to,
-            )
+        for v in range(2):
+            r.q1_send[op, v] = r.sum_f[rows_of(v * 2 + 1 - c), :].astype(BF16)
+        send(None, r.q1_send.at[op], r.q1_recv.at[op], r.q1_ss.at[op], r.q1_rs.at[op], head=twin)
+
+    def reduce_middle(op):
+        arrived(None, r.q1_recv.at[op], r.q1_rs.at[op])
+        block = r.sum_f[rows_of(across), :] + r.q1_recv[op, 1 - x].astype(F32)
+        r.q2_send[op] = block.astype(BF16)
+        send(None, r.q2_send.at[op], r.q2_recv.at[op], r.q2_ss.at[op], r.q2_rs.at[op], head=across)
+        r.q_own[op] = r.sum_f[rows_of(h), :] + r.q1_recv[op, x].astype(F32)
 
     def reduce_finish(op):
-        result = r.sum_f[rows_of(h), :]
-        for d in range(1, HEAD):
-            o = lax.rem(h + d, HEAD)
-            arrived(None, r.part_recv.at[op, o], r.rs_rs.at[op, o])
-            result = result + r.part_recv[op, o].astype(F32)
-        return result
+        arrived(None, r.q2_recv.at[op], r.q2_rs.at[op])
+        return r.q_own[op] + r.q2_recv[op].astype(F32)
 
     def spread_start(op, whole, value):
         whole[rows_of(h), :] = value
-        for d in range(1, HEAD):
-            ref = whole.at[rows_of(h), :]
-            send(
-                None, ref, ref, r.ag_ss.at[op, d], r.ag_rs.at[op, h], head=lax.rem(h + d, HEAD)
-            )
+        ref = whole.at[rows_of(h), :]
+        send(None, ref, ref, r.ag_ss.at[op, 0], r.ag_rs.at[op, h], head=across)
+        send(None, ref, ref, r.ag_ss.at[op, 1], r.ag_rs.at[op, h], head=twin)
+
+    def spread_pass(op, whole):
+        ref = whole.at[rows_of(across), :]
+        arrived(None, ref, r.ag_rs.at[op, across])
+        send(None, ref, ref, r.ag_ss.at[op, 2], r.ag_rs.at[op, across], head=twin)
 
     def spread_finish(op, whole):
-        for d in range(1, HEAD):
-            o = lax.rem(h + d, HEAD)
+        for o in (twin, beyond):
             arrived(None, whole.at[rows_of(o), :], r.ag_rs.at[op, o])
 
     def block_rows(unit, head):
@@ -511,6 +547,7 @@
 
     tiled(width, out_tile)
     reduce_start(0)
+    reduce_middle(0)
     arrived(None, cot_rows(1 - e, c), r.c_rs.at[0])
     send(
         None, cot_rows(1 - e, c), cot_rows(1 - e, c), r.c_ss.at[1], r.c_rs.at[1], head=twin
@@ -652,6 +689,7 @@
     pair_start(1)
     grad_along(DOWN)
     pair_middle(1)
+    spread_pass(0, r.gb)
     spread_finish(0, r.gb)
     r.gatt[...] = dot(r.gb[...], r.wo_all[...], ((1,), (1,))).astype(BF16)
     for i in range(LINE):
@@ -660,7 +698,7 @@
         r.so[zz * 2] = part[:, :rows]
         r.so[zz * 2 + 1] = part[:, rows:]
         grad_cross(OUT, zz)
-    grad_along(UP)
+    grad_along(UP, (1, 2))
 
     r.dq[...] = jnp.zeros(r.dq.shape, F32)
     r.dk[...] = jnp.zeros(r.dk.shape, F32)
@@ -675,14 +713,14 @@
             r.lg[:, k] = dot(grad, r.vwin[k, :], ((1,), (1,)))
         for b in range(BLK_DEV):
             q = pl.ds(b * BLK, BLK)
-            chance, grown = r.prob[hh, q, :], r.lg[q, :]
+            chance, grown = r.prob[hh, q, :].astype(F32), r.lg[q, :]
             inner = jnp.sum(chance * grown, axis=-1, keepdims=True)
             r.ds[q, :] = (chance * (grown - inner)).astype(BF16)
         r.dq[...] += jnp.where(mine, dot(r.ds[...], r.kwin[...], ((1,), (0,))), 0.0)
         for j in range(SPAN):
             k = pl.ds(j * tokens, tokens)
             r.dk[k, :] += dot(r.ds[:, k], query, ((0,), (0,)))
-            r.dv[k, :] += dot(r.prob_low[hh, :, k], grad, ((0,), (0,)))
+            r.dv[k, :] += dot(r.prob[hh, :, k], grad, ((0,), (0,)))
         return carry
 
     lax.fori_loop(0, HEAD, attend_back, 0)
@@ -696,38 +734,68 @@
             r.dkv_pad[k] = jnp.zeros(r.dkv_pad.shape[1:], BF16)
     for k in range(NEAR):
         r.dkv_send[k] = r.dkv_pad[k + SPAN - 1 - root]
-        other, back = s + k - (SPAN - 1), 2 * (SPAN - 1) - k
-        if k != SPAN - 1:
-            send(
-                (other >= 0) & (other < SEQ), r.dkv_send.at[k], r.dkv_recv.at[back],
-                r.dkv_ss.at[k], r.dkv_rs.at[back], seq=other,
-            )
-
     r.gtq[...] = (r.dq[...] * scaling).astype(BF16)
+
+    def grad_hop(cond, slot, into, k, to):
+        send(cond, r.dkv_send.at[slot], r.dkv_recv.at[into], r.dkv_ss.at[k], r.dkv_rs.at[into], seq=to)
+
+    def add_to(slot, *froms):
+        both = r.dkv_send[slot].astype(F32)
+        for k in froms:
+            both = both + r.dkv_recv[k].astype(F32)
+        r.dkv_send[slot] = both.astype(BF16)
+
+    def grad_wait(cond, into):
+        arrived(cond, r.dkv_recv.at[into], r.dkv_rs.at[into])
+
+    FAR, ABOVE, BELOW, LINE_ABOVE, LINE_BELOW, MATE = range(6)
+    grad_hop((y == 0) & (z >= 2), 0, FAR, 0, s - 2)
+    grad_hop((y == 1) & (z <= 1), 6, FAR, 0, s + 2)
+    grad_hop((y == 0) & high, 6, BELOW, 1, s + 2)
+    grad_hop((y == 1) & low, 0, ABOVE, 1, s - 2)
+
+    grad_along(UP, (3,))
+
     for i in range(LINE):
         zz = tile_of(i)
-        part = dot(r.normed[:, cols(zz, 256)], r.gtq[...], ((0,), (0,))).astype(BF16)
+        part = jnp.zeros((256, 2 * head_w), F32)
+        for j in range(SPAN):
+            part = part + dot(
+                r.nall[root + j, :, cols(zz, 256)], r.dkv_pad[j + SPAN - 1], ((0,), (0,))
+            )
+        part = part.astype(BF16)
+        for v in range(2):
+            for k in range(2):
+                r.skv[zz * 2 + v, k] = part[v * rows : (v + 1) * rows, k * head_w : (k + 1) * head_w]
+        grad_cross(QKV_KV, zz)
+        if i == 1:
+            grad_wait(low & high, FAR)
+            add_to(2 + 2 * y, FAR)
+            grad_hop((y == 0) & low, 2, ABOVE, 2, s - 2)
+            grad_hop((y == 1) & high, 4, BELOW, 2, s + 2)
+            grad_hop(low, 1, LINE_ABOVE, 3, s - 2)
+            grad_hop(high, 5, LINE_BELOW, 4, s + 2)
+    grad_wait(high, ABOVE)
+    grad_wait(low, BELOW)
+    add_to(from_mate, ABOVE, BELOW)
+    grad_hop(None, from_mate, MATE, 5, mate)
+    for i in range(LINE):
+        zz = tile_of(i)
+        part = dot(r.nall[SPAN - 1, :, cols(zz, 256)], r.gtq[...], ((0,), (0,))).astype(BF16)
         r.sq[zz * 2] = part[:rows]
         r.sq[zz * 2 + 1] = part[rows:]
         grad_cross(QKV_Q, zz)
     grad_along(OUT)
+    grad_along(QKV_KV)
     ffn = pair_finish(1)
     spread_start(1, r.out_o, (r.mid_own[...] + ffn + r.gains[4:5, :]).astype(BF16))
-
+    grad_wait(high, LINE_ABOVE)
+    grad_wait(low, LINE_BELOW)
+    grad_wait(None, MATE)
     whole = r.dkv_send[SPAN - 1].astype(F32)
-    for k in range(NEAR):
-        if k != SPAN - 1:
-            other = s + k - (SPAN - 1)
-            arrived((other >= 0) & (other < SEQ), r.dkv_recv.at[k], r.dkv_rs.at[k])
-            whole = whole + r.dkv_recv[k].astype(F32)
+    for k in (LINE_ABOVE, LINE_BELOW, MATE):
+        whole = whole + r.dkv_recv[k].astype(F32)
     r.gtkv[...] = whole.astype(BF16)
-    for i in range(LINE):
-        zz = tile_of(i)
-        part = dot(r.normed[:, cols(zz, 256)], r.gtkv[...], ((0,), (0,))).astype(BF16)
-        for v in range(2):
-            for k in range(2):
-                r.skv[zz * 2 + v, k] = part[v * rows : (v + 1) * rows, k * head_w : (k + 1) * head_w]
-        grad_cross(QKV_KV, zz)
 
     def gn1_tile(k):
         k = pl.ds(k, 256)
@@ -739,8 +807,8 @@
 
     tiled(width, gn1_tile)
     reduce_start(1)
+    reduce_middle(1)
     grad_along(QKV_Q)
-    grad_along(QKV_KV)
     grad_one = reduce_finish(1)
     xhat, inverse = norm_parts(r.tok[rows_of(h), :].astype(F32))
     r.sm_send[0:1, :] = jnp.sum(grad_one * xhat, axis=0, keepdims=True)
@@ -751,6 +819,7 @@
             None, r.sm_send.at[:, cols(to, rows)], r.sm_recv.at[s], r.sm_ss.at[d], r.sm_rs.at[s],
             seq=to,
         )
+    spread_pass(1, r.out_o)
     grad_x = r.gm_own[...] + norm_backward(xhat, inverse, grad_one * r.gains[0:1, :])
     spread_start(2, r.xgb, grad_x.astype(BF16))
 
@@ -760,6 +829,7 @@
     same, other = grad_halves(UP)
     r.gu_o[:, cols(e, half)] = same
     r.gu_o[:, cols(1 - e, half)] = other
+    spread_pass(2, r.xgb)
     r.go_o[...] = grad_sum(OUT)
 
     r.sm_recv[s] = r.sm_send[:, cols(s, rows)]
@@ -824,20 +894,22 @@
     scratch = dict(
         wq_all=((3, width, head_w), BF16), wo_all=((head_w, width), BF16),
         wu_all=((width, half), BF16), wd_all=((half, width), BF16), vec=((8, rows), F32),
-        gains=((8, width), F32), xh=((tok, width), F32), normed=((tok, width), BF16),
-        qs=((tok, head_w), BF16), kv_all=((NEAR, tok, 2 * head_w), BF16),
+        gains=((8, width), F32), nall=((NEAR, tok, width), BF16),
+        qs=((tok, head_w), BF16),
         kwin=((keys, head_w), BF16), vwin=((keys, head_w), BF16), lg=((tok, keys), F32),
-        prob=((HEAD, tok, keys), F32), prob_low=((HEAD, tok, keys), BF16), ds=((tok, keys), BF16),
+        prob=((HEAD, tok, keys), BF16), ds=((tok, keys), BF16),
         att=((tok, head_w), F32), att_low=((tok, head_w), BF16), n2x=((2 * tok, width), BF16),
         cotx=((2 * tok, width), BF16), hid=((2 * tok, half), BF16), gp=((2 * tok, half), BF16),
         gb=((tok, width), BF16), xgb=((tok, width), BF16), mid_own=((quarter, width), F32),
         gm_own=((quarter, width), F32), gatt=((tok, head_w), BF16), dq=((tok, head_w), F32),
         dk=((keys, head_w), F32), dv=((keys, head_w), F32),
         dkv_pad=((NEAR + SPAN - 1, tok, 2 * head_w), BF16),
-        dkv_send=((NEAR, tok, 2 * head_w), BF16), dkv_recv=((NEAR, tok, 2 * head_w), BF16),
+        dkv_send=((NEAR, tok, 2 * head_w), BF16), dkv_recv=((6, tok, 2 * head_w), BF16),
         gtq=((tok, head_w), BF16), gtkv=((tok, 2 * head_w), BF16),
-        part_send=((2, tok, width), BF16), part_recv=((2, HEAD, quarter, width), BF16),
-        sum_f=((2 * tok, width), F32), cnt=((HEAD, 8, keys), F32),
+        q1_send=((2, 2, quarter, width), BF16), q1_recv=((2, 2, quarter, width), BF16),
+        q2_send=((2, quarter, width), BF16), q2_recv=((2, quarter, width), BF16),
+        q_own=((2, quarter, width), F32),
+        sum_f=((2 * tok, width), F32), bias=((HEAD, 8, keys), F32),
         p1_send=((2, 4, quarter, width), BF16), p1_recv=((2, 4, quarter, width), BF16),
         p2_send=((2, 4, quarter, width), BF16), p2_recv=((2, 4, quarter, width), BF16),
         p_own=((2, quarter, width), F32), sm_send=((8, width), F32),
@@ -851,15 +923,15 @@
         for name, shape in shards.items():
             scratch[lead + name] = ((count,) + shape, BF16)
     semaphores = dict(
-        g_ss=(2, 16), g_rs=(2, SEQ), f_ss=(2, 7), f_rs=(2, SEQ), v_ss=(7,), v_rs=(SEQ,),
-        kv_ss=(NEAR,), kv_rs=(NEAR,), dkv_ss=(NEAR,), dkv_rs=(NEAR,), c_ss=(2,), c_rs=(2,),
-        rs_ss=(2, HEAD), rs_rs=(2, HEAD), ag_ss=(3, HEAD), ag_rs=(3, HEAD), n2_ss=(7,),
+        g_ss=(3, 16), g_rs=(3, SEQ), f_ss=(2, 7), f_rs=(2, SEQ), v_ss=(7,), v_rs=(SEQ,),
+        t_ns=(6,), t_ss=(NEAR, 3), t_rs=(NEAR, HEAD), dkv_ss=(6,), dkv_rs=(6,), c_ss=(2,), c_rs=(2,),
+        q1_ss=(2,), q1_rs=(2,), q2_ss=(2,), q2_rs=(2,), ag_ss=(3, 3), ag_rs=(3, HEAD), n2_ss=(7,),
         n2_rs=(8,), p1_ss=(2,), p1_rs=(2,), p2_ss=(2, 4), p2_rs=(2, 4), ra_ss=(5, LINE),
         ra_rs=(5, LINE), rb_ss=(5, LINE), rb_rs=(5, LINE), sm_ss=(SEQ,), sm_rs=(SEQ,),
         sm2_ss=(HEAD,), sm2_rs=(HEAD,), up_ss=(SEQ,), up_rs=(SEQ,),
     )
     names = [*ins, *outs, *scratch, *semaphores]
-    out, xg, gq, go, gu, gd, small = pl.pallas_call(
+    results = pl.pallas_call(
         functools.partial(fused_kernel, names),
         out_shape=[jax.ShapeDtypeStruct(*o) for o in outs.values()],
         in_specs=[smem] * 3 + [vmem] * (len(ins) - 3),
@@ -871,10 +943,29 @@
         ),
         name="fused_layer",
     )(*ins.values())
-    return (
-        out, xg, jnp.transpose(gq, (1, 0, 2)), go, small[0], small[1], small[2], small[3], gu,
-        small[8:16].reshape(hidden), gd, small[4],
-    )
+    large = list(outs.values())[:-1]
+    handed = pl.pallas_call(
+        hand_over_kernel,
+        out_shape=[jax.ShapeDtypeStruct(*o) for o in large]
+        + [jax.ShapeDtypeStruct((rows,), F32)] * 5
+        + [jax.ShapeDtypeStruct((hidden,), F32)],
+        in_specs=[vmem] * len(outs),
+        out_specs=[vmem] * (len(large) + 6),
+        name="hand_over",
+    )(*results)
+    out, xg, gq, go, gu, gd, g1, b1, g2, b2, b3, upg = handed
+    return out, xg, jnp.transpose(gq, (1, 0, 2)), go, g1, b1, g2, b2, gu, upg, gd, b3
+
+
+def hand_over_kernel(*refs):
+    large = (len(refs) - 7) // 2
+    small, vectors = refs[large], refs[2 * large + 1 :]
+    for k in range(large):
+        refs[large + 1 + k][...] = refs[k][...]
+    for k in range(5):
+        vectors[k][...] = small[k, :]
+    for k in range(8):
+        vectors[5][pl.ds(k * 128, 128)] = small[8 + k, :]
 
 
 IN_SPECS = (

time: 186 us -> 169 us (0.909)
  local copies, waits for them, and re-layouts: 10.7 us -> 1.27 us
  Pallas kernels: 174 us -> 167 us
    pallas_call x1, Pallas kernels: 174 us -> 163 us  [local_fused(): pl.pallas_call(functools.partial(fused_kernel, names), out_shape=[jax.Sha...]
    unnamed x18 -> x2, local copies, waits for them, and re-layouts: 7.46 us -> 0.67 us
    pallas_call x0 -> x1, Pallas kernels: none -> 3.61 us  [local_fused(): pl.pallas_call(hand_over_kernel, out_shape=[jax.ShapeDtypeStruct(*o) for...]
where the time goes in v4:
time: 169 us
  Pallas kernels  167 us (99%)
    pallas_call x1, Pallas kernels, local_fused(): pl.pallas_call(functools.partial(fused_kernel, names), out_shape=[jax.Sha...  163 us
    pallas_call x1, Pallas kernels, local_fused(): pl.pallas_call(hand_over_kernel, out_shape=[jax.ShapeDtypeStruct(*o) for...  3.61 us

profile of v4, /device:TPU:0, one launch (start us, length us, event | category | flops | bytes accessed | tf_op | source)
XLA Modules:
  0.0 169.2 jit_solution(11820554156306437723)
XLA Ops:
  0.6 0.0 copy-start
  0.7 0.7 copy-done
  1.3 0.6 reshape.27.refs_14_
  1.9 163.5 %fused_layer.1 = (bf16[256,1024]{1,0:T(8,128)(2,1)}, f32[256,1024]{1,0:T(8,128)}, f32[3,128,256]{2,1,0:T(8,128)}, f32[256,128]{1,0:T(8,128)}, f32[128,1024]{1,0:...) custom-call(s32[4]{0:T(128)} %refs_0_.1, s32[4]{0:T(128)} %refs_1_.1, s32[3,4,4]{2,1,0:T(4,128)} %bitcast.4, ...), custom_call_target="tpu_custom_call" | custom-call | tf_op jit(solution)/shard_map/fused_layer/pallas_call | solution.py:934
  165.4 3.6 %hand_over.1 = (bf16[256,1024]{1,0:T(8,128)(2,1)}, f32[256,1024]{1,0:T(8,128)}, f32[3,128,256]{2,1,0:T(8,128)}, f32[256,128]{1,0:T(8,128)}, f32[128,1024]{1,0:T(...) custom-call(bf16[256,1024]{1,0:T(8,128)(2,1)} %get-tuple-element.31., ...), custom_call_target="tpu_custom_call" | custom-call | tf_op jit(solution)/shard_map/hand_over/pallas_call | solution.py:947
Async XLA Ops:
  0.6 0.7 copy-start

commit v5 on v4

--- a/solution.py
+++ b/solution.py
@@ -395,22 +395,30 @@
             None, ffn_src[w](e), ffn_slot[w](s), r.f_ss.at[i, 3], r.f_rs.at[i, s], seq=mate
         )
 
-    def ffn_forward(w):
+    def by_distance(k):
+        up = k + jnp.where(z <= k, 1, 0)
+        down = k + jnp.where(LINE - 1 - z <= k, 1, 0)
+        return jnp.where(z < LINE // 2, up, LINE - 1 - down)
+
+    def ffn_forward(w, ks=(0, 1, 2)):
         i = w - UP
-        for d in range(1, LINE):
-            o = lax.rem(z + LINE - d, LINE) * 2 + y
+        for k in ks:
+            o = by_distance(k) * 2 + y
             ref = ffn_slot[w](o)
             arrived(None, ref, r.f_rs.at[i, o])
-            send(None, ref, ref, r.f_ss.at[i, 3 + d], r.f_rs.at[i, o], seq=mate)
+            send(None, ref, ref, r.f_ss.at[i, 4 + k], r.f_rs.at[i, o], seq=mate)
 
     def ffn_finish(w):
         for d in range(LINE):
             o = lax.rem(z + d, LINE) * 2 + 1 - y
             arrived(None, ffn_slot[w](o), r.f_rs.at[w - UP, o])
 
+    relay_round(1, 2)
+    relay_round(2, 1)
+    relay_round(1, 3)
+    relay_round(2, 2)
     ffn_start(UP)
-    relay_round(1, 2)
-    relay_round(1, 3)
+    relay_round(2, 3)
     for cond, slot in slots[3:]:
         token_pass(cond, slot)
     for ref, src in ((ffn_slot[UP](s), ffn_src[UP](e)), (ffn_slot[DOWN](s), ffn_src[DOWN](e))):
@@ -429,17 +437,29 @@
     relay_finish(1)
     part = dot(r.nall[SPAN - 1], r.wq_all[0], ((1,), (0,)))
     r.qs[...] = (part.astype(BF16).astype(F32) * scaling).astype(BF16)
-    for k in range(1, LINE):
-        relay_round(2, k)
-
-    half_t = tokens // 2
     r.cotx[cols(e, tokens), :] = r.cot[...]
-
-    def cot_rows(unit, core):
-        return r.cotx.at[pl.ds(al(unit * tokens + core * half_t, half_t), half_t), :]
-
-    send(None, r.cot.at[cols(c, half_t), :], cot_rows(e, c), r.c_ss.at[0], r.c_rs.at[0], seq=pair)
-    ffn_forward(UP)
+    beyond = (1 - x) * 2 + 1 - c
+
+    def block_rows(unit, head):
+        return pl.ds(al(unit * tokens + head * quarter, quarter), quarter)
+
+    def cot_rows(unit, head):
+        return r.cotx.at[block_rows(unit, head), :]
+
+    send(
+        None, r.cot.at[cols(h, quarter), :], cot_rows(e, h), r.c_ss.at[0], r.c_rs.at[h], seq=pair
+    )
+
+    def cot_share():
+        ref = cot_rows(1 - e, h)
+        arrived(None, ref, r.c_rs.at[h])
+        send(None, ref, ref, r.c_ss.at[1], r.c_rs.at[h], head=across)
+        send(None, ref, ref, r.c_ss.at[2], r.c_rs.at[h], head=twin)
+
+    def cot_pass():
+        ref = cot_rows(1 - e, across)
+        arrived(None, ref, r.c_rs.at[across])
+        send(None, ref, ref, r.c_ss.at[3], r.c_rs.at[across], head=twin)
 
     lanes = lax.div(lax.broadcasted_iota(jnp.int32, (1, head_w), 1), HEAD_DIM)
     none = jnp.zeros((), BF16)
@@ -461,11 +481,12 @@
         r.att[...] += jnp.where(mine, part, 0.0)
         return carry
 
-    lax.fori_loop(0, HEAD, attend, 0)
+    lax.fori_loop(0, HEAD // 2, attend, 0)
+    ffn_forward(UP, (0,))
+    lax.fori_loop(HEAD // 2, HEAD, attend, 0)
+    ffn_forward(UP, (1,))
     r.att_low[...] = r.att[...].astype(BF16)
     relay_finish(2)
-
-    beyond = (1 - x) * 2 + 1 - c
 
     def rows_of(k):
         return cols(k, quarter)
@@ -501,13 +522,12 @@
         for o in (twin, beyond):
             arrived(None, whole.at[rows_of(o), :], r.ag_rs.at[op, o])
 
-    def block_rows(unit, head):
-        return pl.ds(al(unit * tokens + head * quarter, quarter), quarter)
+    pair_sum = [r.sum_f, r.sum_g]
 
     def pair_start(op):
         for u in range(2):
             for v in range(2):
-                block = r.sum_f[block_rows(u, v * 2 + 1 - c), :]
+                block = pair_sum[op][block_rows(u, v * 2 + 1 - c), :]
                 r.p1_send[op, u * 2 + v] = block.astype(BF16)
         send(None, r.p1_send.at[op], r.p1_recv.at[op], r.p1_ss.at[op], r.p1_rs.at[op], head=twin)
 
@@ -515,7 +535,7 @@
         arrived(None, r.p1_recv.at[op], r.p1_rs.at[op])
         for du, dv in ((1, 1), (1, 0), (0, 1), (0, 0)):
             u, v = lax.rem(e + du, 2), lax.rem(x + dv, 2)
-            block = r.sum_f[block_rows(u, v * 2 + c), :] + r.p1_recv[op, u * 2 + v].astype(F32)
+            block = pair_sum[op][block_rows(u, v * 2 + c), :] + r.p1_recv[op, u * 2 + v].astype(F32)
             if du or dv:
                 k = u * 2 + v
                 r.p2_send[op, k] = block.astype(BF16)
@@ -526,6 +546,38 @@
             else:
                 r.p_own[op] = block
 
+    def pair_x(op):
+        arrived(None, r.p1_recv.at[op], r.p1_rs.at[op])
+        for du in (1, 0):
+            u = lax.rem(e + du, 2)
+            k = u * 2 + 1 - x
+            block = pair_sum[op][block_rows(u, across), :] + r.p1_recv[op, k].astype(F32)
+            r.p2_send[op, k] = block.astype(BF16)
+            send(
+                None, r.p2_send.at[op, k], r.p2_recv.at[op, u], r.p2_ss.at[op, k],
+                r.p2_rs.at[op, u], head=across,
+            )
+
+    def pair_z(op):
+        for du in (1, 0):
+            u = lax.rem(e + du, 2)
+            arrived(None, r.p2_recv.at[op, u], r.p2_rs.at[op, u])
+            block = pair_sum[op][block_rows(u, h), :] + r.p1_recv[op, u * 2 + x].astype(F32)
+            block = block + r.p2_recv[op, u].astype(F32)
+            if du:
+                k = u * 2 + x
+                r.p2_send[op, k] = block.astype(BF16)
+                send(
+                    None, r.p2_send.at[op, k], r.p2_recv.at[op, 2], r.p2_ss.at[op, k],
+                    r.p2_rs.at[op, 2], seq=pair,
+                )
+            else:
+                r.p_own[op] = block
+
+    def pair_end(op):
+        arrived(None, r.p2_recv.at[op, 2], r.p2_rs.at[op, 2])
+        return r.p_own[op] + r.p2_recv[op, 2].astype(F32)
+
     def pair_finish(op):
         result = r.p_own[op]
         for du, dv in ((0, 1), (1, 0), (1, 1)):
@@ -534,25 +586,11 @@
             result = result + r.p2_recv[op, k].astype(F32)
         return result
 
-    def tiled(n, body):
-        def step(j, carry):
-            body(al(j * 256, 256))
-            return carry
-
-        lax.fori_loop(0, n // 256, step, 0)
-
-    def out_tile(k):
-        k = pl.ds(k, 256)
-        r.sum_f[:tokens, k] = dot(r.att_low[...], r.wo_all[:, k], ((1,), (0,)))
-
-    tiled(width, out_tile)
+    r.sum_f[:tokens, :] = dot(r.att_low[...], r.wo_all[...], ((1,), (0,)))
     reduce_start(0)
     reduce_middle(0)
-    arrived(None, cot_rows(1 - e, c), r.c_rs.at[0])
-    send(
-        None, cot_rows(1 - e, c), cot_rows(1 - e, c), r.c_ss.at[1], r.c_rs.at[1], head=twin
-    )
-    ffn_forward(DOWN)
+    ffn_forward(UP, (2,))
+    ffn_forward(DOWN, (0,))
     middle = r.tok[rows_of(h), :].astype(F32) + reduce_finish(0)
     r.mid_own[...] = middle
     xhat, _ = norm_parts(middle)
@@ -562,20 +600,26 @@
 
     r.n2x[block_rows(e, h), :] = (xhat * r.gains[2:3, :] + r.gains[3:4, :]).astype(BF16)
     mine, tag = n2_rows(e, h), e * 4 + h
-    send(None, mine, mine, r.n2_ss.at[0], r.n2_rs.at[tag], head=across)
-    send(None, mine, mine, r.n2_ss.at[1], r.n2_rs.at[tag], seq=pair, head=across)
-    send(None, mine, mine, r.n2_ss.at[2], r.n2_rs.at[tag], seq=pair)
-    send(None, mine, mine, r.n2_ss.at[3], r.n2_rs.at[tag], head=twin)
-    ffn_finish(UP)
-    ffn_finish(DOWN)
+    send(None, mine, mine, r.n2_ss.at[0], r.n2_rs.at[tag], seq=pair)
+    send(None, mine, mine, r.n2_ss.at[1], r.n2_rs.at[tag], head=across)
+    send(None, mine, mine, r.n2_ss.at[2], r.n2_rs.at[tag], head=twin)
+    cot_share()
+    ffn_forward(DOWN, (1,))
     for k, (unit, head) in enumerate(((e, across), (1 - e, h), (1 - e, across))):
         ref, tag = n2_rows(unit, head), unit * 4 + head
         arrived(None, ref, r.n2_rs.at[tag])
-        send(None, ref, ref, r.n2_ss.at[4 + k], r.n2_rs.at[tag], head=twin)
+        if k == 1:
+            send(None, ref, ref, r.n2_ss.at[6], r.n2_rs.at[tag], head=across)
+        send(None, ref, ref, r.n2_ss.at[3 + k], r.n2_rs.at[tag], head=twin)
+    cot_pass()
+    ffn_forward(DOWN, (2,))
+    ffn_finish(UP)
+    ffn_finish(DOWN)
     for unit in (e, 1 - e):
         for head in (x * 2 + 1 - c, (1 - x) * 2 + 1 - c):
             arrived(None, n2_rows(unit, head), r.n2_rs.at[unit * 4 + head])
-    arrived(None, cot_rows(1 - e, 1 - c), r.c_rs.at[1])
+    for head in (twin, beyond):
+        arrived(None, cot_rows(1 - e, head), r.c_rs.at[head])
 
     root_c = (2.0 / 3.141592653589793) ** 0.5
     r.up_send[half // 128 :, :] = jnp.zeros((8 - half // 128, 128), F32)
@@ -592,13 +636,6 @@
         r.up_send[2 * j : 2 * j + 1, :] = sums[:, :128]
         r.up_send[2 * j + 1 : 2 * j + 2, :] = sums[:, 128:]
 
-    def gn2_tile(k):
-        k = pl.ds(k, 256)
-        r.sum_f[:, k] = dot(r.gp[...], r.wu_all[k, :], ((1,), (1,)))
-
-    tiled(width, gn2_tile)
-    pair_start(0)
-
     grad_send = {QKV_KV: r.skv, QKV_Q: r.sq, OUT: r.so, UP: r.su, DOWN: r.sd}
     grad_arrive = {QKV_KV: r.akv, QKV_Q: r.aq, OUT: r.ao, UP: r.au, DOWN: r.ad}
     grad_again = {QKV_KV: r.bkv, QKV_Q: r.bq, OUT: r.bo, UP: r.bu, DOWN: r.bd}
@@ -658,10 +695,15 @@
         grad_cross(UP, zz)
 
     down_step(0)
+    r.sum_f[...] = dot(r.gp[...], r.wu_all[...], ((1,), (1,)))
+    pair_start(0)
     down_step(1)
     pair_middle(0)
+    r.sum_g[...] = dot(r.hid[...], r.wd_all[...], ((1,), (0,)))
+    pair_start(1)
     down_step(2)
     down_step(3)
+    pair_x(1)
     for i in range(LINE):
         up_step(i)
     for d in range(1, SEQ):
@@ -681,14 +723,8 @@
     r.sm_send[4:5, :] = jnp.sum(dy, axis=0, keepdims=True)
     r.sm_send[5:8, :] = jnp.zeros((3, width), F32)
 
-    def down_tile(k):
-        k = pl.ds(k, 256)
-        r.sum_f[:, k] = dot(r.hid[...], r.wd_all[:, k], ((1,), (0,)))
-
-    tiled(width, down_tile)
-    pair_start(1)
     grad_along(DOWN)
-    pair_middle(1)
+    pair_z(1)
     spread_pass(0, r.gb)
     spread_finish(0, r.gb)
     r.gatt[...] = dot(r.gb[...], r.wo_all[...], ((1,), (1,))).astype(BF16)
@@ -787,7 +823,7 @@
         grad_cross(QKV_Q, zz)
     grad_along(OUT)
     grad_along(QKV_KV)
-    ffn = pair_finish(1)
+    ffn = pair_end(1)
     spread_start(1, r.out_o, (r.mid_own[...] + ffn + r.gains[4:5, :]).astype(BF16))
     grad_wait(high, LINE_ABOVE)
     grad_wait(low, LINE_BELOW)
@@ -797,18 +833,13 @@
         whole = whole + r.dkv_recv[k].astype(F32)
     r.gtkv[...] = whole.astype(BF16)
 
-    def gn1_tile(k):
-        k = pl.ds(k, 256)
-        r.sum_f[:tokens, k] = (
-            dot(r.gtq[...], r.wq_all[0, k, :], ((1,), (1,)))
-            + dot(r.gtkv[:, :head_w], r.wq_all[1, k, :], ((1,), (1,)))
-            + dot(r.gtkv[:, head_w:], r.wq_all[2, k, :], ((1,), (1,)))
-        )
-
-    tiled(width, gn1_tile)
+    r.sum_f[:tokens, :] = (
+        dot(r.gtq[...], r.wq_all[0], ((1,), (1,)))
+        + dot(r.gtkv[:, :head_w], r.wq_all[1], ((1,), (1,)))
+        + dot(r.gtkv[:, head_w:], r.wq_all[2], ((1,), (1,)))
+    )
     reduce_start(1)
     reduce_middle(1)
-    grad_along(QKV_Q)
     grad_one = reduce_finish(1)
     xhat, inverse = norm_parts(r.tok[rows_of(h), :].astype(F32))
     r.sm_send[0:1, :] = jnp.sum(grad_one * xhat, axis=0, keepdims=True)
@@ -820,6 +851,7 @@
             seq=to,
         )
     spread_pass(1, r.out_o)
+    grad_along(QKV_Q)
     grad_x = r.gm_own[...] + norm_backward(xhat, inverse, grad_one * r.gains[0:1, :])
     spread_start(2, r.xgb, grad_x.astype(BF16))
 
@@ -909,7 +941,7 @@
         q1_send=((2, 2, quarter, width), BF16), q1_recv=((2, 2, quarter, width), BF16),
         q2_send=((2, quarter, width), BF16), q2_recv=((2, quarter, width), BF16),
         q_own=((2, quarter, width), F32),
-        sum_f=((2 * tok, width), F32), bias=((HEAD, 8, keys), F32),
+        sum_f=((2 * tok, width), F32), sum_g=((2 * tok, width), F32), bias=((HEAD, 8, keys), F32),
         p1_send=((2, 4, quarter, width), BF16), p1_recv=((2, 4, quarter, width), BF16),
         p2_send=((2, 4, quarter, width), BF16), p2_recv=((2, 4, quarter, width), BF16),
         p_own=((2, quarter, width), F32), sm_send=((8, width), F32),
@@ -924,7 +956,7 @@
             scratch[lead + name] = ((count,) + shape, BF16)
     semaphores = dict(
         g_ss=(3, 16), g_rs=(3, SEQ), f_ss=(2, 7), f_rs=(2, SEQ), v_ss=(7,), v_rs=(SEQ,),
-        t_ns=(6,), t_ss=(NEAR, 3), t_rs=(NEAR, HEAD), dkv_ss=(6,), dkv_rs=(6,), c_ss=(2,), c_rs=(2,),
+        t_ns=(6,), t_ss=(NEAR, 3), t_rs=(NEAR, HEAD), dkv_ss=(6,), dkv_rs=(6,), c_ss=(4,), c_rs=(HEAD,),
         q1_ss=(2,), q1_rs=(2,), q2_ss=(2,), q2_rs=(2,), ag_ss=(3, 3), ag_rs=(3, HEAD), n2_ss=(7,),
         n2_rs=(8,), p1_ss=(2,), p1_rs=(2,), p2_ss=(2, 4), p2_rs=(2, 4), ra_ss=(5, LINE),
         ra_rs=(5, LINE), rb_ss=(5, LINE), rb_rs=(5, LINE), sm_ss=(SEQ,), sm_rs=(SEQ,),

time: 169 us -> 162 us (0.959)
  Pallas kernels: 167 us -> 160 us
    pallas_call x1, Pallas kernels: 163 us -> 156 us  [local_fused(): pl.pallas_call(functools.partial(fused_kernel, names), out_shape=[jax.Sha...]
where the time goes in v5:
time: 162 us
  Pallas kernels  160 us (99%)
    pallas_call x1, Pallas kernels, local_fused(): pl.pallas_call(functools.partial(fused_kernel, names), out_shape=[jax.Sha...  156 us
    pallas_call x1, Pallas kernels, local_fused(): pl.pallas_call(hand_over_kernel, out_shape=[jax.ShapeDtypeStruct(*o) for...  3.61 us

profile of v5, /device:TPU:0, one launch (start us, length us, event | category | flops | bytes accessed | tf_op | source)
XLA Modules:
  0.0 161.6 jit_solution(273326293854916806)
XLA Ops:
  0.6 0.0 copy-start
  0.7 0.7 copy-done
  1.3 0.6 reshape.27.refs_14_
  1.9 155.9 %fused_layer.1 = (bf16[256,1024]{1,0:T(8,128)(2,1)}, f32[256,1024]{1,0:T(8,128)}, f32[3,128,256]{2,1,0:T(8,128)}, f32[256,128]{1,0:T(8,128)}, f32[128,1024]{1,0:...) custom-call(s32[4]{0:T(128)} %refs_0_.1, s32[4]{0:T(128)} %refs_1_.1, s32[3,4,4]{2,1,0:T(4,128)} %bitcast.4, ...), custom_call_target="tpu_custom_call" | custom-call | tf_op jit(solution)/shard_map/fused_layer/pallas_call | solution.py:966
  157.9 3.6 %hand_over.1 = (bf16[256,1024]{1,0:T(8,128)(2,1)}, f32[256,1024]{1,0:T(8,128)}, f32[3,128,256]{2,1,0:T(8,128)}, f32[256,128]{1,0:T(8,128)}, f32[128,1024]{1,0:T(...) custom-call(bf16[256,1024]{1,0:T(8,128)(2,1)} %get-tuple-element.31., ...), custom_call_target="tpu_custom_call" | custom-call | tf_op jit(solution)/shard_map/hand_over/pallas_call | solution.py:979
Async XLA Ops:
  0.6 0.7 copy-start

commit v6 on v5

--- a/solution.py
+++ b/solution.py
@@ -558,7 +558,7 @@
                 r.p2_rs.at[op, u], head=across,
             )
 
-    def pair_z(op):
+    def pair_over(op):
         for du in (1, 0):
             u = lax.rem(e + du, 2)
             arrived(None, r.p2_recv.at[op, u], r.p2_rs.at[op, u])
@@ -661,6 +661,46 @@
                 r.rb_rs.at[w, z], seq=zz * 2 + y,
             )
 
+    outer, inner = (z == 0) | (z == LINE - 1), (z == 1) | (z == LINE - 2)
+    far_half = 2 - 2 * lax.div(z, 2)
+    far_inner = 2 - lax.div(z, 2)
+    grad_hold = {QKV_KV: r.hkv, QKV_Q: r.hq, OUT: r.ho}
+
+    def tile_far(i):
+        return (far_half, far_half + 1, pair_z, z)[i]
+
+    def grad_first(w):
+        for k in range(3):
+            zz = tile_far(k)
+            arrived(None, grad_arrive[w].at[zz], r.ra_rs.at[w, zz])
+            both = grad_send[w][zz * 2 + y].astype(F32) + grad_arrive[w][zz].astype(F32)
+            grad_again[w][zz] = both.astype(BF16)
+            if k < 2:
+                send(
+                    outer, grad_again[w].at[zz], grad_hold[w].at[k], r.rh_ss.at[w, k],
+                    r.rh_rs.at[w, k], seq=pair,
+                )
+            else:
+                send(
+                    None, grad_again[w].at[zz], grad_final[w].at[z], r.rb_ss.at[w, zz],
+                    r.rb_rs.at[w, z], seq=pair,
+                )
+
+    def grad_second(w):
+        for k in range(2):
+            zz = tile_far(k)
+            arrived(inner, grad_hold[w].at[k], r.rh_rs.at[w, k])
+
+            @pl.when(inner)
+            def _():
+                both = grad_again[w][zz].astype(F32) + grad_hold[w][k].astype(F32)
+                grad_again[w][zz] = both.astype(BF16)
+
+            send(
+                inner, grad_again[w].at[zz], grad_final[w].at[z], r.rb_ss.at[w, zz],
+                r.rb_rs.at[w, z], seq=zz * 2 + y,
+            )
+
     def grad_own(w):
         arrived(None, grad_arrive[w].at[z], r.ra_rs.at[w, z])
         return grad_send[w][z * 2 + y].astype(F32) + grad_arrive[w][z].astype(F32)
@@ -670,10 +710,7 @@
         return grad_final[w][o].astype(F32)
 
     def grad_sum(w):
-        result = grad_own(w)
-        for d in range(1, LINE):
-            result = result + grad_from(w, lax.rem(z + d, LINE))
-        return result
+        return grad_own(w) + grad_from(w, pair_z) + grad_from(w, far_inner)
 
     def grad_halves(w):
         same = grad_own(w) + grad_from(w, lax.rem(z + 2, LINE))
@@ -724,12 +761,12 @@
     r.sm_send[5:8, :] = jnp.zeros((3, width), F32)
 
     grad_along(DOWN)
-    pair_z(1)
+    pair_over(1)
     spread_pass(0, r.gb)
     spread_finish(0, r.gb)
     r.gatt[...] = dot(r.gb[...], r.wo_all[...], ((1,), (1,))).astype(BF16)
     for i in range(LINE):
-        zz = tile_of(i)
+        zz = tile_far(i)
         part = dot(r.att_low[...], r.gb[:, cols(zz, 256)], ((0,), (0,))).astype(BF16)
         r.so[zz * 2] = part[:, :rows]
         r.so[zz * 2 + 1] = part[:, rows:]
@@ -793,7 +830,7 @@
     grad_along(UP, (3,))
 
     for i in range(LINE):
-        zz = tile_of(i)
+        zz = tile_far(i)
         part = jnp.zeros((256, 2 * head_w), F32)
         for j in range(SPAN):
             part = part + dot(
@@ -811,18 +848,19 @@
             grad_hop((y == 1) & high, 4, BELOW, 2, s + 2)
             grad_hop(low, 1, LINE_ABOVE, 3, s - 2)
             grad_hop(high, 5, LINE_BELOW, 4, s + 2)
+    grad_first(OUT)
     grad_wait(high, ABOVE)
     grad_wait(low, BELOW)
     add_to(from_mate, ABOVE, BELOW)
     grad_hop(None, from_mate, MATE, 5, mate)
     for i in range(LINE):
-        zz = tile_of(i)
+        zz = tile_far(i)
         part = dot(r.nall[SPAN - 1, :, cols(zz, 256)], r.gtq[...], ((0,), (0,))).astype(BF16)
         r.sq[zz * 2] = part[:rows]
         r.sq[zz * 2 + 1] = part[rows:]
         grad_cross(QKV_Q, zz)
-    grad_along(OUT)
-    grad_along(QKV_KV)
+    grad_second(OUT)
+    grad_first(QKV_KV)
     ffn = pair_end(1)
     spread_start(1, r.out_o, (r.mid_own[...] + ffn + r.gains[4:5, :]).astype(BF16))
     grad_wait(high, LINE_ABOVE)
@@ -840,6 +878,7 @@
     )
     reduce_start(1)
     reduce_middle(1)
+    grad_second(QKV_KV)
     grad_one = reduce_finish(1)
     xhat, inverse = norm_parts(r.tok[rows_of(h), :].astype(F32))
     r.sm_send[0:1, :] = jnp.sum(grad_one * xhat, axis=0, keepdims=True)
@@ -851,7 +890,7 @@
             seq=to,
         )
     spread_pass(1, r.out_o)
-    grad_along(QKV_Q)
+    grad_first(QKV_Q)
     grad_x = r.gm_own[...] + norm_backward(xhat, inverse, grad_one * r.gains[0:1, :])
     spread_start(2, r.xgb, grad_x.astype(BF16))
 
@@ -862,6 +901,7 @@
     r.gu_o[:, cols(e, half)] = same
     r.gu_o[:, cols(1 - e, half)] = other
     spread_pass(2, r.xgb)
+    grad_second(QKV_Q)
     r.go_o[...] = grad_sum(OUT)
 
     r.sm_recv[s] = r.sm_send[:, cols(s, rows)]
@@ -951,7 +991,7 @@
     shards = dict(
         kv=(2, rows, head_w), q=(rows, head_w), o=(head_w, rows), u=(rows, half), d=(half, rows)
     )
-    for lead, count in (("s", SEQ), ("a", LINE), ("b", LINE), ("r", LINE)):
+    for lead, count in (("s", SEQ), ("a", LINE), ("b", LINE), ("r", LINE), ("h", 2)):
         for name, shape in shards.items():
             scratch[lead + name] = ((count,) + shape, BF16)
     semaphores = dict(
@@ -959,7 +999,7 @@
         t_ns=(6,), t_ss=(NEAR, 3), t_rs=(NEAR, HEAD), dkv_ss=(6,), dkv_rs=(6,), c_ss=(4,), c_rs=(HEAD,),
         q1_ss=(2,), q1_rs=(2,), q2_ss=(2,), q2_rs=(2,), ag_ss=(3, 3), ag_rs=(3, HEAD), n2_ss=(7,),
         n2_rs=(8,), p1_ss=(2,), p1_rs=(2,), p2_ss=(2, 4), p2_rs=(2, 4), ra_ss=(5, LINE),
-        ra_rs=(5, LINE), rb_ss=(5, LINE), rb_rs=(5, LINE), sm_ss=(SEQ,), sm_rs=(SEQ,),
+        ra_rs=(5, LINE), rh_ss=(5, 2), rh_rs=(5, 2), rb_ss=(5, LINE), rb_rs=(5, LINE), sm_ss=(SEQ,), sm_rs=(SEQ,),
         sm2_ss=(HEAD,), sm2_rs=(HEAD,), up_ss=(SEQ,), up_rs=(SEQ,),
     )
     names = [*ins, *outs, *scratch, *semaphores]

time: 162 us -> 157 us (0.969)
  Pallas kernels: 160 us -> 155 us
    pallas_call x1, Pallas kernels: 156 us -> 151 us  [local_fused(): pl.pallas_call(functools.partial(fused_kernel, names), out_shape=[jax.Sha...]
where the time goes in v6:
time: 157 us
  Pallas kernels  155 us (99%)
    pallas_call x1, Pallas kernels, local_fused(): pl.pallas_call(functools.partial(fused_kernel, names), out_shape=[jax.Sha...  151 us
    pallas_call x1, Pallas kernels, local_fused(): pl.pallas_call(hand_over_kernel, out_shape=[jax.ShapeDtypeStruct(*o) for...  3.61 us

profile of v6, /device:TPU:0, one launch (start us, length us, event | category | flops | bytes accessed | tf_op | source)
XLA Modules:
  0.0 156.7 jit_solution(8728252573745287264)
XLA Ops:
  0.6 0.0 copy-start
  0.7 0.7 copy-done
  1.3 0.6 reshape.27.refs_14_
  1.9 151.0 %fused_layer.1 = (bf16[256,1024]{1,0:T(8,128)(2,1)}, f32[256,1024]{1,0:T(8,128)}, f32[3,128,256]{2,1,0:T(8,128)}, f32[256,128]{1,0:T(8,128)}, f32[128,1024]{1,0:...) custom-call(s32[4]{0:T(128)} %refs_0_.1, s32[4]{0:T(128)} %refs_1_.1, s32[3,4,4]{2,1,0:T(4,128)} %bitcast.4, ...), custom_call_target="tpu_custom_call" | custom-call | tf_op jit(solution)/shard_map/fused_layer/pallas_call | solution.py:1006
  152.9 3.6 %hand_over.1 = (bf16[256,1024]{1,0:T(8,128)(2,1)}, f32[256,1024]{1,0:T(8,128)}, f32[3,128,256]{2,1,0:T(8,128)}, f32[256,128]{1,0:T(8,128)}, f32[128,1024]{1,0:T(...) custom-call(bf16[256,1024]{1,0:T(8,128)(2,1)} %get-tuple-element.31., ...), custom_call_target="tpu_custom_call" | custom-call | tf_op jit(solution)/shard_map/hand_over/pallas_call | solution.py:1019
Async XLA Ops:
  0.6 0.7 copy-start

commit v7 on v6

--- a/solution.py
+++ b/solution.py
@@ -221,6 +221,7 @@
     for k, ref in enumerate((r.g1, r.b1, r.g2, r.b2, r.b3)):
         r.vec[k : k + 1, :] = ref[...].reshape(1, rows).astype(F32)
     r.vec[5:8, :] = jnp.zeros((3, rows), F32)
+    r.upb_f[...] = r.upb[...].reshape(1, 2 * half).astype(F32)
     pl.semaphore_wait(barrier, len(greeted))
 
     def cols(o, size):
@@ -614,23 +615,26 @@
     cot_pass()
     ffn_forward(DOWN, (2,))
     ffn_finish(UP)
-    ffn_finish(DOWN)
     for unit in (e, 1 - e):
         for head in (x * 2 + 1 - c, (1 - x) * 2 + 1 - c):
             arrived(None, n2_rows(unit, head), r.n2_rs.at[unit * 4 + head])
-    for head in (twin, beyond):
-        arrived(None, cot_rows(1 - e, head), r.c_rs.at[head])
 
     root_c = (2.0 / 3.141592653589793) ** 0.5
     r.up_send[half // 128 :, :] = jnp.zeros((8 - half // 128, 128), F32)
     for j in range(half // 256):
         f = pl.ds(j * 256, 256)
-        bias = r.upb[:, pl.ds(al(e * half + j * 256, 256), 256)].astype(F32)
+        bias = r.upb_f[:, pl.ds(al(e * half + j * 256, 256), 256)]
         v = dot(r.n2x[...], r.wu_all[:, f], ((1,), (0,))) + bias
         t = jnp.tanh(root_c * (v + 0.044715 * (v * v * v)))
         r.hid[:, f] = (0.5 * v * (1.0 + t)).astype(BF16)
         slope = 0.5 * (1.0 + t) + 0.5 * v * (1.0 - t * t) * (root_c * (1.0 + 0.134145 * v * v))
-        low_p = (dot(r.cotx[...], r.wd_all[f, :], ((1,), (1,))) * slope).astype(BF16)
+        r.slope[:, f] = slope
+    ffn_finish(DOWN)
+    for head in (twin, beyond):
+        arrived(None, cot_rows(1 - e, head), r.c_rs.at[head])
+    for j in range(half // 256):
+        f = pl.ds(j * 256, 256)
+        low_p = (dot(r.cotx[...], r.wd_all[f, :], ((1,), (1,))) * r.slope[:, f]).astype(BF16)
         r.gp[:, f] = low_p
         sums = jnp.sum(low_p.astype(F32), axis=0, keepdims=True)
         r.up_send[2 * j : 2 * j + 1, :] = sums[:, :128]
@@ -788,11 +792,10 @@
             q = pl.ds(b * BLK, BLK)
             chance, grown = r.prob[hh, q, :].astype(F32), r.lg[q, :]
             inner = jnp.sum(chance * grown, axis=-1, keepdims=True)
-            r.ds[q, :] = (chance * (grown - inner)).astype(BF16)
-        r.dq[...] += jnp.where(mine, dot(r.ds[...], r.kwin[...], ((1,), (0,))), 0.0)
+            r.ds[hh, q, :] = (chance * (grown - inner)).astype(BF16)
         for j in range(SPAN):
             k = pl.ds(j * tokens, tokens)
-            r.dk[k, :] += dot(r.ds[:, k], query, ((0,), (0,)))
+            r.dk[k, :] += dot(r.ds[hh, :, k], query, ((0,), (0,)))
             r.dv[k, :] += dot(r.prob[hh, :, k], grad, ((0,), (0,)))
         return carry
 
@@ -801,58 +804,80 @@
         j = k - (SPAN - 1)
         if 0 <= j < SPAN:
             q = pl.ds(j * tokens, tokens)
-            r.dkv_pad[k, :, :head_w] = r.dk[q, :].astype(BF16)
-            r.dkv_pad[k, :, head_w:] = r.dv[q, :].astype(BF16)
+            r.dkv_pad[k, 0] = r.dk[q, :].astype(BF16)
+            r.dkv_pad[k, 1] = r.dv[q, :].astype(BF16)
         else:
             r.dkv_pad[k] = jnp.zeros(r.dkv_pad.shape[1:], BF16)
     for k in range(NEAR):
         r.dkv_send[k] = r.dkv_pad[k + SPAN - 1 - root]
-    r.gtq[...] = (r.dq[...] * scaling).astype(BF16)
-
-    def grad_hop(cond, slot, into, k, to):
-        send(cond, r.dkv_send.at[slot], r.dkv_recv.at[into], r.dkv_ss.at[k], r.dkv_rs.at[into], seq=to)
-
-    def add_to(slot, *froms):
-        both = r.dkv_send[slot].astype(F32)
+
+    def grad_hop(cond, slot, into, k, to, v):
+        send(
+            cond, r.dkv_send.at[slot, v], r.dkv_recv.at[into, v], r.dkv_ss.at[k, v],
+            r.dkv_rs.at[into, v], seq=to,
+        )
+
+    def add_to(v, slot, *froms):
+        both = r.dkv_send[slot, v].astype(F32)
         for k in froms:
-            both = both + r.dkv_recv[k].astype(F32)
-        r.dkv_send[slot] = both.astype(BF16)
-
-    def grad_wait(cond, into):
-        arrived(cond, r.dkv_recv.at[into], r.dkv_rs.at[into])
+            both = both + r.dkv_recv[k, v].astype(F32)
+        r.dkv_send[slot, v] = both.astype(BF16)
+
+    def grad_wait(cond, into, v):
+        arrived(cond, r.dkv_recv.at[into, v], r.dkv_rs.at[into, v])
 
     FAR, ABOVE, BELOW, LINE_ABOVE, LINE_BELOW, MATE = range(6)
-    grad_hop((y == 0) & (z >= 2), 0, FAR, 0, s - 2)
-    grad_hop((y == 1) & (z <= 1), 6, FAR, 0, s + 2)
-    grad_hop((y == 0) & high, 6, BELOW, 1, s + 2)
-    grad_hop((y == 1) & low, 0, ABOVE, 1, s - 2)
-
-    grad_along(UP, (3,))
+    for v in range(2):
+        grad_hop((y == 0) & (z >= 2), 0, FAR, 0, s - 2, v)
+        grad_hop((y == 1) & (z <= 1), 6, FAR, 0, s + 2, v)
+    for v in range(2):
+        grad_hop((y == 0) & high, 6, BELOW, 1, s + 2, v)
+        grad_hop((y == 1) & low, 0, ABOVE, 1, s - 2, v)
+
+    def hop_far(v):
+        grad_wait(low & high, FAR, v)
+        add_to(v, 2 + 2 * y, FAR)
+        grad_hop((y == 0) & low, 2, ABOVE, 2, s - 2, v)
+        grad_hop((y == 1) & high, 4, BELOW, 2, s + 2, v)
+
+    def hop_line(v):
+        grad_hop(low, 1, LINE_ABOVE, 3, s - 2, v)
+        grad_hop(high, 5, LINE_BELOW, 4, s + 2, v)
+
+    def hop_mate(v):
+        grad_wait(high, ABOVE, v)
+        grad_wait(low, BELOW, v)
+        add_to(v, from_mate, ABOVE, BELOW)
+        grad_hop(None, from_mate, MATE, 5, mate, v)
+
+    def queries_back(hh, carry):
+        r.dq[...] += jnp.where(lanes == hh, dot(r.ds[hh], r.kwin[...], ((1,), (0,))), 0.0)
+        return carry
 
     for i in range(LINE):
         zz = tile_far(i)
-        part = jnp.zeros((256, 2 * head_w), F32)
-        for j in range(SPAN):
-            part = part + dot(
-                r.nall[root + j, :, cols(zz, 256)], r.dkv_pad[j + SPAN - 1], ((0,), (0,))
-            )
-        part = part.astype(BF16)
-        for v in range(2):
-            for k in range(2):
-                r.skv[zz * 2 + v, k] = part[v * rows : (v + 1) * rows, k * head_w : (k + 1) * head_w]
+        for k in range(2):
+            part = jnp.zeros((256, head_w), F32)
+            for j in range(SPAN):
+                part = part + dot(
+                    r.nall[root + j, :, cols(zz, 256)], r.dkv_pad[j + SPAN - 1, k], ((0,), (0,))
+                )
+            part = part.astype(BF16)
+            for v in range(2):
+                r.skv[zz * 2 + v, k] = part[v * rows : (v + 1) * rows]
         grad_cross(QKV_KV, zz)
         if i == 1:
-            grad_wait(low & high, FAR)
-            add_to(2 + 2 * y, FAR)
-            grad_hop((y == 0) & low, 2, ABOVE, 2, s - 2)
-            grad_hop((y == 1) & high, 4, BELOW, 2, s + 2)
-            grad_hop(low, 1, LINE_ABOVE, 3, s - 2)
-            grad_hop(high, 5, LINE_BELOW, 4, s + 2)
+            hop_far(0)
+        if i == 2:
+            hop_far(1)
+            hop_line(0)
+            hop_line(1)
+    grad_along(UP, (3,))
+    hop_mate(0)
+    hop_mate(1)
     grad_first(OUT)
-    grad_wait(high, ABOVE)
-    grad_wait(low, BELOW)
-    add_to(from_mate, ABOVE, BELOW)
-    grad_hop(None, from_mate, MATE, 5, mate)
+    lax.fori_loop(0, HEAD, queries_back, 0)
+    r.gtq[...] = (r.dq[...] * scaling).astype(BF16)
     for i in range(LINE):
         zz = tile_far(i)
         part = dot(r.nall[SPAN - 1, :, cols(zz, 256)], r.gtq[...], ((0,), (0,))).astype(BF16)
@@ -863,18 +888,19 @@
     grad_first(QKV_KV)
     ffn = pair_end(1)
     spread_start(1, r.out_o, (r.mid_own[...] + ffn + r.gains[4:5, :]).astype(BF16))
-    grad_wait(high, LINE_ABOVE)
-    grad_wait(low, LINE_BELOW)
-    grad_wait(None, MATE)
-    whole = r.dkv_send[SPAN - 1].astype(F32)
-    for k in (LINE_ABOVE, LINE_BELOW, MATE):
-        whole = whole + r.dkv_recv[k].astype(F32)
-    r.gtkv[...] = whole.astype(BF16)
+    for v in range(2):
+        grad_wait(high, LINE_ABOVE, v)
+        grad_wait(low, LINE_BELOW, v)
+        grad_wait(None, MATE, v)
+        whole = r.dkv_send[SPAN - 1, v].astype(F32)
+        for k in (LINE_ABOVE, LINE_BELOW, MATE):
+            whole = whole + r.dkv_recv[k, v].astype(F32)
+        r.gtkv[v] = whole.astype(BF16)
 
     r.sum_f[:tokens, :] = (
         dot(r.gtq[...], r.wq_all[0], ((1,), (1,)))
-        + dot(r.gtkv[:, :head_w], r.wq_all[1], ((1,), (1,)))
-        + dot(r.gtkv[:, head_w:], r.wq_all[2], ((1,), (1,)))
+        + dot(r.gtkv[0], r.wq_all[1], ((1,), (1,)))
+        + dot(r.gtkv[1], r.wq_all[2], ((1,), (1,)))
     )
     reduce_start(1)
     reduce_middle(1)
@@ -892,7 +918,7 @@
     spread_pass(1, r.out_o)
     grad_first(QKV_Q)
     grad_x = r.gm_own[...] + norm_backward(xhat, inverse, grad_one * r.gains[0:1, :])
-    spread_start(2, r.xgb, grad_x.astype(BF16))
+    spread_start(2, r.xg_o, grad_x.astype(BF16))
 
     same, other = grad_halves(DOWN)
     r.gd_o[cols(e, half), :] = same
@@ -900,7 +926,7 @@
     same, other = grad_halves(UP)
     r.gu_o[:, cols(e, half)] = same
     r.gu_o[:, cols(1 - e, half)] = other
-    spread_pass(2, r.xgb)
+    spread_pass(2, r.xg_o)
     grad_second(QKV_Q)
     r.go_o[...] = grad_sum(OUT)
 
@@ -928,8 +954,7 @@
                 ups = ups + r.up_recv[o, :tall, :]
         r.small_o[8 + u * tall : 8 + (u + 1) * tall, :] = ups
     spread_finish(1, r.out_o)
-    spread_finish(2, r.xgb)
-    r.xg_o[...] = r.xgb[...].astype(F32)
+    spread_finish(2, r.xg_o)
     for d in range(1, HEAD):
         o = lax.rem(h + d, HEAD)
         arrived(None, r.sm_two.at[o], r.sm2_rs.at[o])
@@ -956,28 +981,28 @@
         units=seq_units, pads=seq_pad, picks=jnp.transpose(rand_picks, (2, 0, 1)), tok=tokens,
         cot=cotangent, wq=jnp.transpose(w_qkv, (1, 0, 2)), wo=w_out, wu=w_up, wd=w_down,
         g1=ln1_gain, b1=ln1_bias, g2=ln2_gain, b2=ln2_bias, b3=down_bias,
-        upb=up_bias.reshape(1, hidden),
+        upb=up_bias,
     )
     outs = dict(
-        out_o=((tok, width), BF16), xg_o=((tok, width), F32), gq_o=((3, rows, head_w), F32),
+        out_o=((tok, width), BF16), xg_o=((tok, width), BF16), gq_o=((3, rows, head_w), F32),
         go_o=((head_w, rows), F32), gu_o=((rows, hidden), F32), gd_o=((hidden, rows), F32),
         small_o=((16, rows), F32),
     )
     scratch = dict(
         wq_all=((3, width, head_w), BF16), wo_all=((head_w, width), BF16),
-        wu_all=((width, half), BF16), wd_all=((half, width), BF16), vec=((8, rows), F32),
+        wu_all=((width, half), BF16), wd_all=((half, width), BF16), vec=((8, rows), F32), upb_f=((1, hidden), F32),
         gains=((8, width), F32), nall=((NEAR, tok, width), BF16),
         qs=((tok, head_w), BF16),
         kwin=((keys, head_w), BF16), vwin=((keys, head_w), BF16), lg=((tok, keys), F32),
-        prob=((HEAD, tok, keys), BF16), ds=((tok, keys), BF16),
+        prob=((HEAD, tok, keys), BF16), ds=((HEAD, tok, keys), BF16),
         att=((tok, head_w), F32), att_low=((tok, head_w), BF16), n2x=((2 * tok, width), BF16),
-        cotx=((2 * tok, width), BF16), hid=((2 * tok, half), BF16), gp=((2 * tok, half), BF16),
-        gb=((tok, width), BF16), xgb=((tok, width), BF16), mid_own=((quarter, width), F32),
+        cotx=((2 * tok, width), BF16), hid=((2 * tok, half), BF16), slope=((2 * tok, half), F32), gp=((2 * tok, half), BF16),
+        gb=((tok, width), BF16), mid_own=((quarter, width), F32),
         gm_own=((quarter, width), F32), gatt=((tok, head_w), BF16), dq=((tok, head_w), F32),
         dk=((keys, head_w), F32), dv=((keys, head_w), F32),
-        dkv_pad=((NEAR + SPAN - 1, tok, 2 * head_w), BF16),
-        dkv_send=((NEAR, tok, 2 * head_w), BF16), dkv_recv=((6, tok, 2 * head_w), BF16),
-        gtq=((tok, head_w), BF16), gtkv=((tok, 2 * head_w), BF16),
+        dkv_pad=((NEAR + SPAN - 1, 2, tok, head_w), BF16),
+        dkv_send=((NEAR, 2, tok, head_w), BF16), dkv_recv=((6, 2, tok, head_w), BF16),
+        gtq=((tok, head_w), BF16), gtkv=((2, tok, head_w), BF16),
         q1_send=((2, 2, quarter, width), BF16), q1_recv=((2, 2, quarter, width), BF16),
         q2_send=((2, quarter, width), BF16), q2_recv=((2, quarter, width), BF16),
         q_own=((2, quarter, width), F32),
@@ -996,7 +1021,7 @@
             scratch[lead + name] = ((count,) + shape, BF16)
     semaphores = dict(
         g_ss=(3, 16), g_rs=(3, SEQ), f_ss=(2, 7), f_rs=(2, SEQ), v_ss=(7,), v_rs=(SEQ,),
-        t_ns=(6,), t_ss=(NEAR, 3), t_rs=(NEAR, HEAD), dkv_ss=(6,), dkv_rs=(6,), c_ss=(4,), c_rs=(HEAD,),
+        t_ns=(6,), t_ss=(NEAR, 3), t_rs=(NEAR, HEAD), dkv_ss=(6, 2), dkv_rs=(6, 2), c_ss=(4,), c_rs=(HEAD,),
         q1_ss=(2,), q1_rs=(2,), q2_ss=(2,), q2_rs=(2,), ag_ss=(3, 3), ag_rs=(3, HEAD), n2_ss=(7,),
         n2_rs=(8,), p1_ss=(2,), p1_rs=(2,), p2_ss=(2, 4), p2_rs=(2, 4), ra_ss=(5, LINE),
         ra_rs=(5, LINE), rh_ss=(5, 2), rh_rs=(5, 2), rb_ss=(5, LINE), rb_rs=(5, LINE), sm_ss=(SEQ,), sm_rs=(SEQ,),
@@ -1015,7 +1040,7 @@
         ),
         name="fused_layer",
     )(*ins.values())
-    large = list(outs.values())[:-1]
+    large = [(v[0], F32 if k == "xg_o" else v[1]) for k, v in outs.items()][:-1]
     handed = pl.pallas_call(
         hand_over_kernel,
         out_shape=[jax.ShapeDtypeStruct(*o) for o in large]
@@ -1033,7 +1058,8 @@
     large = (len(refs) - 7) // 2
     small, vectors = refs[large], refs[2 * large + 1 :]
     for k in range(large):
-        refs[large + 1 + k][...] = refs[k][...]
+        target = refs[large + 1 + k]
+        target[...] = refs[k][...].astype(target.dtype)
     for k in range(5):
         vectors[k][...] = small[k, :]
     for k in range(8):

time: 157 us -> 153 us (0.975)
  Pallas kernels: 155 us -> 152 us
    pallas_call x1, Pallas kernels: 151 us -> 149 us  [local_fused(): pl.pallas_call(functools.partial(fused_kernel, names), out_shape=[jax.Sha...]
where the time goes in v7:
time: 153 us
  Pallas kernels  152 us (99%)
    pallas_call x1, Pallas kernels, local_fused(): pl.pallas_call(functools.partial(fused_kernel, names), out_shape=[jax.Sha...  149 us
    pallas_call x1, Pallas kernels, local_fused(): pl.pallas_call(hand_over_kernel, out_shape=[jax.ShapeDtypeStruct(*o) for...  3.45 us

profile of v7, /device:TPU:0, one launch (start us, length us, event | category | flops | bytes accessed | tf_op | source)
XLA Modules:
  0.0 152.9 jit_solution(4188045315755239790)
XLA Ops:
  0.7 148.6 %fused_layer.1 = (bf16[256,1024]{1,0:T(8,128)(2,1)}, bf16[256,1024]{1,0:T(8,128)(2,1)}, f32[3,128,256]{2,1,0:T(8,128)}, f32[256,128]{1,0:T(8,128)}, f32[128,1024...) custom-call(s32[4]{0:T(128)} %refs_0_.1, s32[4]{0:T(128)} %refs_1_.1, s32[3,4,4]{2,1,0:T(4,128)} %bitcast.4, ...), custom_call_target="tpu_custom_call" | custom-call | tf_op jit(solution)/shard_map/fused_layer/pallas_call | solution.py:1031
  149.3 3.5 %hand_over.1 = (bf16[256,1024]{1,0:T(8,128)(2,1)}, f32[256,1024]{1,0:T(8,128)}, f32[3,128,256]{2,1,0:T(8,128)}, f32[256,128]{1,0:T(8,128)}, f32[128,1024]{1,0:T(...) custom-call(bf16[256,1024]{1,0:T(8,128)(2,1)} %get-tuple-element.31., ...), custom_call_target="tpu_custom_call" | custom-call | tf_op jit(solution)/shard_map/hand_over/pallas_call | solution.py:1044

commit v8 on v7

--- a/solution.py
+++ b/solution.py
@@ -169,6 +169,7 @@
 NEAR = 2 * SPAN - 1
 QKV_KV, QKV_Q, OUT, UP, DOWN = range(5)
 VMEM_BYTES = 60 * 1024 * 1024
+PIECES = 2
 
 
 def al(value, multiple):
@@ -1041,13 +1042,20 @@
         name="fused_layer",
     )(*ins.values())
     large = [(v[0], F32 if k == "xg_o" else v[1]) for k, v in outs.items()][:-1]
+
+    def piece(out):
+        shape, axis = list(out[0]), len(out[0]) - 2
+        shape[axis] //= PIECES
+        return pl.BlockSpec(tuple(shape), lambda i: (0,) * axis + (i, 0))
+
     handed = pl.pallas_call(
         hand_over_kernel,
         out_shape=[jax.ShapeDtypeStruct(*o) for o in large]
         + [jax.ShapeDtypeStruct((rows,), F32)] * 5
         + [jax.ShapeDtypeStruct((hidden,), F32)],
-        in_specs=[vmem] * len(outs),
-        out_specs=[vmem] * (len(large) + 6),
+        grid=(PIECES,),
+        in_specs=[piece(o) for o in large] + [vmem],
+        out_specs=[piece(o) for o in large] + [vmem] * 6,
         name="hand_over",
     )(*results)
     out, xg, gq, go, gu, gd, g1, b1, g2, b2, b3, upg = handed

time: 153 us -> 153 us (level)
  no operation moved by 1% of the time
where the time goes in v8:
time: 153 us
  Pallas kernels  152 us (99%)
    pallas_call x1, Pallas kernels, local_fused(): pl.pallas_call(functools.partial(fused_kernel, names), out_shape=[jax.Sha...  149 us
    pallas_call x1, Pallas kernels, local_fused(): pl.pallas_call(hand_over_kernel, out_shape=[jax.ShapeDtypeStruct(*o) for...  3.08 us

profile of v8, /device:TPU:0, one launch (start us, length us, event | category | flops | bytes accessed | tf_op | source)
XLA Modules:
  0.0 152.5 jit_solution(4847202942616859713)
XLA Ops:
  0.7 148.6 %fused_layer.1 = (bf16[256,1024]{1,0:T(8,128)(2,1)}, bf16[256,1024]{1,0:T(8,128)(2,1)}, f32[3,128,256]{2,1,0:T(8,128)}, f32[256,128]{1,0:T(8,128)}, f32[128,1024...) custom-call(s32[4]{0:T(128)} %refs_0_.1, s32[4]{0:T(128)} %refs_1_.1, s32[3,4,4]{2,1,0:T(4,128)} %bitcast.4, ...), custom_call_target="tpu_custom_call" | custom-call | tf_op jit(solution)/shard_map/fused_layer/pallas_call | solution.py:1032
  149.3 3.1 %hand_over.1 = (bf16[256,1024]{1,0:T(8,128)(2,1)}, f32[256,1024]{1,0:T(8,128)}, f32[3,128,256]{2,1,0:T(8,128)}, f32[256,128]{1,0:T(8,128)}, f32[128,1024]{1,0:T(...) custom-call(bf16[256,1024]{1,0:T(8,128)(2,1)} %get-tuple-element.31., ...), custom_call_target="tpu_custom_call" | custom-call | tf_op jit(solution)/shard_map/hand_over/pallas_call | solution.py:1051

commit v9 on v8

--- a/solution.py
+++ b/solution.py
@@ -420,9 +420,9 @@
     relay_round(1, 3)
     relay_round(2, 2)
     ffn_start(UP)
-    relay_round(2, 3)
     for cond, slot in slots[3:]:
         token_pass(cond, slot)
+    relay_round(2, 3)
     for ref, src in ((ffn_slot[UP](s), ffn_src[UP](e)), (ffn_slot[DOWN](s), ffn_src[DOWN](e))):
         ref[...] = src[...]
 
@@ -754,6 +754,7 @@
             seq=lax.rem(s + d, SEQ),
         )
 
+    grad_along(DOWN, (1,))
     grad_two = pair_finish(0)
     xhat, inverse = norm_parts(r.mid_own[...])
     dy = r.cot[rows_of(h), :].astype(F32)
@@ -765,7 +766,7 @@
     r.sm_send[4:5, :] = jnp.sum(dy, axis=0, keepdims=True)
     r.sm_send[5:8, :] = jnp.zeros((3, width), F32)
 
-    grad_along(DOWN)
+    grad_along(DOWN, (2, 3))
     pair_over(1)
     spread_pass(0, r.gb)
     spread_finish(0, r.gb)

time: 153 us -> 152 us (level)
  no operation moved by 1% of the time
where the time goes in v9:
time: 152 us; the launch traced here: 151 us
  Pallas kernels  151 us (99%)
    pallas_call x1, Pallas kernels, local_fused(): pl.pallas_call(functools.partial(fused_kernel, names), out_shape=[jax.Sha...  147 us
    pallas_call x1, Pallas kernels, local_fused(): pl.pallas_call(hand_over_kernel, out_shape=[jax.ShapeDtypeStruct(*o) for...  3.08 us

profile of v9, /device:TPU:0, one launch (start us, length us, event | category | flops | bytes accessed | tf_op | source)
XLA Modules:
  0.0 151.4 jit_solution(16758566439284655490)
XLA Ops:
  0.7 147.4 %fused_layer.1 = (bf16[256,1024]{1,0:T(8,128)(2,1)}, bf16[256,1024]{1,0:T(8,128)(2,1)}, f32[3,128,256]{2,1,0:T(8,128)}, f32[256,128]{1,0:T(8,128)}, f32[128,1024...) custom-call(s32[4]{0:T(128)} %refs_0_.1, s32[4]{0:T(128)} %refs_1_.1, s32[3,4,4]{2,1,0:T(4,128)} %bitcast.4, ...), custom_call_target="tpu_custom_call" | custom-call | tf_op jit(solution)/shard_map/fused_layer/pallas_call | solution.py:1033
  148.1 3.1 %hand_over.1 = (bf16[256,1024]{1,0:T(8,128)(2,1)}, f32[256,1024]{1,0:T(8,128)}, f32[3,128,256]{2,1,0:T(8,128)}, f32[256,128]{1,0:T(8,128)}, f32[128,1024]{1,0:T(...) custom-call(bf16[256,1024]{1,0:T(8,128)(2,1)} %get-tuple-element.31., ...), custom_call_target="tpu_custom_call" | custom-call | tf_op jit(solution)/shard_map/hand_over/pallas_call | solution.py:1052

commit v10 on v9

--- a/solution.py
+++ b/solution.py
@@ -423,8 +423,13 @@
     for cond, slot in slots[3:]:
         token_pass(cond, slot)
     relay_round(2, 3)
-    for ref, src in ((ffn_slot[UP](s), ffn_src[UP](e)), (ffn_slot[DOWN](s), ffn_src[DOWN](e))):
-        ref[...] = src[...]
+    own_copies = [
+        pltpu.make_async_copy(ffn_src[UP](e), ffn_slot[UP](s), r.l_s.at[0]),
+        pltpu.make_async_copy(ffn_src[DOWN](e), ffn_slot[DOWN](s), r.l_s.at[1]),
+        pltpu.make_async_copy(r.cot, r.cotx.at[cols(e, tokens), :], r.l_s.at[2]),
+    ]
+    for one in own_copies:
+        one.start()
 
     ffn_start(DOWN)
     for cond, slot in slots:
@@ -439,7 +444,6 @@
     relay_finish(1)
     part = dot(r.nall[SPAN - 1], r.wq_all[0], ((1,), (0,)))
     r.qs[...] = (part.astype(BF16).astype(F32) * scaling).astype(BF16)
-    r.cotx[cols(e, tokens), :] = r.cot[...]
     beyond = (1 - x) * 2 + 1 - c
 
     def block_rows(unit, head):
@@ -620,6 +624,8 @@
         for head in (x * 2 + 1 - c, (1 - x) * 2 + 1 - c):
             arrived(None, n2_rows(unit, head), r.n2_rs.at[unit * 4 + head])
 
+    for one in own_copies:
+        one.wait()
     root_c = (2.0 / 3.141592653589793) ** 0.5
     r.up_send[half // 128 :, :] = jnp.zeros((8 - half // 128, 128), F32)
     for j in range(half // 256):
@@ -757,7 +763,7 @@
     grad_along(DOWN, (1,))
     grad_two = pair_finish(0)
     xhat, inverse = norm_parts(r.mid_own[...])
-    dy = r.cot[rows_of(h), :].astype(F32)
+    dy = r.cotx[block_rows(e, h), :].astype(F32)
     grad_mid = dy + norm_backward(xhat, inverse, grad_two * r.gains[2:3, :])
     r.gm_own[...] = grad_mid
     spread_start(0, r.gb, grad_mid.astype(BF16))
@@ -979,6 +985,7 @@
     quarter = tok // HEAD
     keys = SPAN * tok
     smem, vmem = pl.BlockSpec(memory_space=pltpu.SMEM), pl.BlockSpec(memory_space=pltpu.VMEM)
+    anywhere = pl.BlockSpec(memory_space=pl.ANY)
     ins = dict(
         units=seq_units, pads=seq_pad, picks=jnp.transpose(rand_picks, (2, 0, 1)), tok=tokens,
         cot=cotangent, wq=jnp.transpose(w_qkv, (1, 0, 2)), wo=w_out, wu=w_up, wd=w_down,
@@ -1023,7 +1030,7 @@
             scratch[lead + name] = ((count,) + shape, BF16)
     semaphores = dict(
         g_ss=(3, 16), g_rs=(3, SEQ), f_ss=(2, 7), f_rs=(2, SEQ), v_ss=(7,), v_rs=(SEQ,),
-        t_ns=(6,), t_ss=(NEAR, 3), t_rs=(NEAR, HEAD), dkv_ss=(6, 2), dkv_rs=(6, 2), c_ss=(4,), c_rs=(HEAD,),
+        t_ns=(6,), t_ss=(NEAR, 3), t_rs=(NEAR, HEAD), dkv_ss=(6, 2), dkv_rs=(6, 2), l_s=(3,), c_ss=(4,), c_rs=(HEAD,),
         q1_ss=(2,), q1_rs=(2,), q2_ss=(2,), q2_rs=(2,), ag_ss=(3, 3), ag_rs=(3, HEAD), n2_ss=(7,),
         n2_rs=(8,), p1_ss=(2,), p1_rs=(2,), p2_ss=(2, 4), p2_rs=(2, 4), ra_ss=(5, LINE),
         ra_rs=(5, LINE), rh_ss=(5, 2), rh_rs=(5, 2), rb_ss=(5, LINE), rb_rs=(5, LINE), sm_ss=(SEQ,), sm_rs=(SEQ,),
@@ -1033,7 +1040,7 @@
     results = pl.pallas_call(
         functools.partial(fused_kernel, names),
         out_shape=[jax.ShapeDtypeStruct(*o) for o in outs.values()],
-        in_specs=[smem] * 3 + [vmem] * (len(ins) - 3),
+        in_specs=[smem] * 3 + [anywhere if k in ("cot", "wu", "wd") else vmem for k in list(ins)[3:]],
         out_specs=[vmem] * len(outs),
         scratch_shapes=[pltpu.VMEM(*v) for v in scratch.values()]
         + [pltpu.SemaphoreType.DMA(v) for v in semaphores.values()],

time: 152 us -> 152 us (level)
  no operation moved by 1% of the time
where the time goes in v10:
time: 152 us; the launch traced here: 151 us
  Pallas kernels  151 us (99%)
    pallas_call x1, Pallas kernels, local_fused(): pl.pallas_call(functools.partial(fused_kernel, names), out_shape=[jax.Sha...  148 us
    pallas_call x1, Pallas kernels, local_fused(): pl.pallas_call(hand_over_kernel, out_shape=[jax.ShapeDtypeStruct(*o) for...  3.08 us

profile of v10, /device:TPU:0, one launch (start us, length us, event | category | flops | bytes accessed | tf_op | source)
XLA Modules:
  0.0 151.4 jit_solution(4749210339027808776)
XLA Ops:
  0.7 147.5 %fused_layer.1 = (bf16[256,1024]{1,0:T(8,128)(2,1)}, bf16[256,1024]{1,0:T(8,128)(2,1)}, f32[3,128,256]{2,1,0:T(8,128)}, f32[256,128]{1,0:T(8,128)}, f32[128,1024...) custom-call(s32[4]{0:T(128)} %refs_0_.1, s32[4]{0:T(128)} %refs_1_.1, s32[3,4,4]{2,1,0:T(4,128)} %bitcast.4, ...), custom_call_target="tpu_custom_call" | custom-call | tf_op jit(solution)/shard_map/fused_layer/pallas_call | solution.py:1040
  148.2 3.1 %hand_over.1 = (bf16[256,1024]{1,0:T(8,128)(2,1)}, f32[256,1024]{1,0:T(8,128)}, f32[3,128,256]{2,1,0:T(8,128)}, f32[256,128]{1,0:T(8,128)}, f32[128,1024]{1,0:T(...) custom-call(bf16[256,1024]{1,0:T(8,128)(2,1)} %get-tuple-element.31., ...), custom_call_target="tpu_custom_call" | custom-call | tf_op jit(solution)/shard_map/hand_over/pallas_call | solution.py:1059
